TPU v7x, 256 devices: a whole 4x4x8 slice. The times are simulated.
256 devices in a mesh: gz: 32 (over z, y_hi, core), col: 8 (over x, y_lo).
Axes of the slice: x: 4, y: 4 (y_hi: 2, y_lo: 2; y = y_hi * 2 + y_lo), z: 8, core: 2. Of those that a mesh axis runs over, the one named last changes fastest.
Arguments:
- features: bfloat16 [32, 512, 512], P('gz', 'col'), may hold values from -6 to 6
- filters: bfloat16 [3, 3, 3, 512, 512], P(None, None, None, 'col'), may hold values from -0.0546875 to 0.0546875
- cotangent: bfloat16 [32, 512, 512], P('gz', 'col'), may hold values from -6 to 6
Outputs:
- output: bfloat16 [32, 512, 512], P('gz', 'col')
- input_grad: bfloat16 [32, 512, 512], P('gz', 'col')
- filter_grad: float32 [3, 3, 3, 512, 512], P(None, None, None, 'col')
All inputs are finite; a program needn't handle non-finite values.
Results may differ from a plain program's by a relative error of at most 0.0015.
Values may be sent and summed in bfloat16 or wider, within the bound.
No kernel may reach another device: no remote copies, remote signals or barrier semaphores. Data moves between devices by JAX's collectives and lax.ppermute only.
A program may use at most 128 MiB of HBM per device.

v0:
```python
import jax
import jax.numpy as jnp
from jax import lax
from jax.sharding import PartitionSpec as P

NY = 32
NZ = 16


def extended(cells, sides, width):
    for axis, dim in sides:
        count = lax.axis_size(axis)
        ends = count - 1
        head = lax.slice_in_dim(cells, 0, width, axis=dim)
        tail = lax.slice_in_dim(cells, cells.shape[dim] - width, cells.shape[dim], axis=dim)
        cells = jnp.concatenate(
            [
                lax.ppermute(tail, axis, [(i, (i + 1) % count) for i in range(ends)]),
                cells,
                lax.ppermute(head, axis, [((i + 1) % count, i) for i in range(ends)]),
            ],
            axis=dim,
        )
    return cells


def spread_cells(block):
    shaped = block.reshape(block.shape[0], block.shape[1], NY, NZ)
    return jnp.pad(shaped, ((0, 0), (0, 0), (1, 1), (1, 1)))


def body(features, filters, cotangent):
    slab, local_in, cells = features.shape
    local_out = cotangent.shape[1]
    whole = lax.all_gather(features, "col", axis=1, tiled=True)
    padded = extended(whole, (("gz", 0),), 1)
    padded = spread_cells(padded)
    channels = padded.shape[1]
    cot_padded = spread_cells(extended(cotangent, (("gz", 0),), 1))
    output = jnp.zeros((slab, local_out, cells), jnp.float32)
    grads = []
    moved_list = []
    for shift_x in range(3):
        for shift_y in range(3):
            for shift_z in range(3):
                window = padded[
                    shift_x : shift_x + slab, :, shift_y : shift_y + NY, shift_z : shift_z + NZ
                ].reshape(slab, channels, cells)
                output = output + jnp.einsum(
                    "on,xnc->xoc",
                    filters[shift_x, shift_y, shift_z],
                    window,
                    preferred_element_type=jnp.float32,
                )
                grads.append(
                    jnp.einsum("xoc,xnc->on", cotangent, window, preferred_element_type=jnp.float32)
                )
                moved_list.append(
                    cot_padded[
                        2 - shift_x : 2 - shift_x + slab,
                        :,
                        2 - shift_y : 2 - shift_y + NY,
                        2 - shift_z : 2 - shift_z + NZ,
                    ].reshape(slab, local_out, cells)
                )
    flat_taps = filters.reshape(27, local_out, channels)
    total = jnp.zeros((local_in * lax.axis_size("col"), slab, cells), jnp.float32)
    for index in range(27):
        piece = flat_taps[index]
        total = total + jnp.einsum(
            "on,xoc->nxc", piece, moved_list[index], preferred_element_type=jnp.float32
        )
    summed = lax.psum_scatter(total, "col", scatter_dimension=0, tiled=True)
    input_grad = jnp.transpose(summed, (1, 0, 2)).astype(jnp.bfloat16)
    total_cells = slab * cells * lax.axis_size("gz")
    scale = 1.0 / jnp.sqrt(jnp.float32(total_cells))
    local_grad = jnp.stack(grads).reshape(3, 3, 3, local_out, channels) * scale
    filter_grad = lax.psum(local_grad, "gz")
    return (output.astype(jnp.bfloat16), input_grad, filter_grad)


def solution(mesh):
    in_specs = (P("gz", "col", None), P(None, None, None, "col", None), P("gz", "col", None))
    out_specs = (P("gz", "col", None), P("gz", "col", None), P(None, None, None, "col", None))
    return jax.shard_map(body, mesh=mesh, in_specs=in_specs, out_specs=out_specs, check_vma=False)
```

profile of v0, /device:TPU:1, one launch (start us, length us, event | category | flops | bytes accessed | tf_op | source)
XLA Modules:
  0.0 705.1 jit_solution(11146966032333530910)
XLA Ops:
  7.2 1.0 copy.31
  8.2 5.1 collective-permute-start.3
  13.3 3.0 collective-permute-start.2
  16.3 23.9 %all_gather.3 = bf16[1,512,512]{2,1,0:T(8,128)(2,1)S(1)} all-gather(bf16[1,64,512]{2,1,0:T(8,128)(2,1)} %param.3), channel_id=1, replica_groups=mesh['gz'=32,'col'=8] {'col'}, dimensions={1}, use_global_device_ids=true | all-gather | bytes 589824 | tf_op jit(solution)/shard_map/all_gather | solution.py:35
  40.2 1.0 copy.28
  41.3 6.8 collective-permute-start.1
  48.0 3.0 collective-permute-start
  51.1 0.6 dynamic-slice
  52.5 0.5 copy-done.26
  53.1 0.5 pad_slice_fusion.24
  53.6 0.9 copy-done.1
  57.2 0.4 copy-done.27
  57.5 0.3 fusion.18
  59.5 0.3 convolution_add_fusion.2
  62.0 0.3 fusion.21
  62.4 1.2 fusion.1
  63.6 3.6 copy.37
  67.2 324.5 %all-reduce.7 = bf16[512,1,512]{2,1,0:T(2,128)(2,1)} all-reduce(f32[512,1,512]{2,1,0:T(1,128)} %copy.37), channel_id=2, replica_groups=mesh['gz'=32,'col'=8] {'col'}, use_global_device_ids=true, to_apply=%region_0.1.clone | all-reduce | flops 262144 | bytes 1572864
  391.7 1.0 constant_dynamic-slice_fusion
  392.8 0.6 copy.45
  393.4 1.6 pad_maximum_fusion
  395.0 0.6 pad_slice_fusion.23
  395.7 3.4 pad_slice_fusion.8
  399.2 1.3 convolution_bitcast_fusion.50
  400.5 1.0 convolution_bitcast_fusion.49
  401.5 0.9 convolution_bitcast_fusion.48
  402.5 0.9 convolution_bitcast_fusion.47
  404.1 0.9 convolution_add_fusion.19
  405.0 0.9 fusion.123
  408.6 0.3 convolution_bitcast_fusion.57
  409.5 0.9 convolution_bitcast_fusion.55
  410.9 0.9 convolution_bitcast_fusion.54
  412.0 0.9 convolution_bitcast_fusion.53
  413.2 1.0 convolution_bitcast_fusion.52
  415.4 2.2 broadcast_multiply_fusion
  417.7 1.4 convolution_bitcast_fusion.51
  419.1 1.4 convolution_add_fusion.18
  420.5 0.3 convolution_add_fusion.17
  420.8 0.3 fusion.50
  421.1 0.3 convolution_add_fusion.15
  421.5 0.3 convolution_add_fusion.14
  421.8 0.3 convolution_add_fusion.13
  422.0 0.3 convolution_add_fusion.12
  422.6 0.3 convolution_add_fusion.10
  423.8 0.3 fusion.62
  424.3 1.0 fusion.63
  425.2 268.6 %all-reduce.6.cloned.1.call-done = f32[3,3,3,64,512]{4,3,2,1,0:T(8,128)} async-done(((f32[3,3,3,64,512]{4,3,2,1,0:T(8,128)}), f32[3,3,3,64,512]{4,3,2,1,0:T(8,128)}) %all-reduce.6.cloned.1.call-update) | async-done | bytes 3538960 | tf_op jit(solution)/shard_map/psum | solution.py:78
  693.8 4.4 copy.75
  (136 shorter events, 13.8 us)
Async XLA Ops:
  7.2 43.9 %copy-start.37 = (u32[256]{0:T(256)S(1)}, u32[256]{0:T(256)}, u32[]{:S(2)}) copy-start(u32[256]{0:T(256)} %constant.13) | copy-start | bytes 3076
  7.2 686.7 %all-reduce.6.cloned.1.call-start = ((), (), s32[]{:S(2)}) async-start(), calls=%async_computation | async-start | bytes 7077888 | tf_op jit(solution)/shard_map/psum | solution.py:78
  8.2 44.1 %collective-permute-start.3 = (bf16[1,64,512]{1,2,0:T(8,128)(2,1)S(1)}, bf16[1,64,512]{1,2,0:T(8,128)(2,1)S(1)}, u32[]{:S(2)}, u32[]{:S(2)}) collective-permute-start(bf16[1,64,512]{1,2,0:T(8,128)(2,1)S(1)} %copy.31), channel_id=1, source_target_pairs={{8,0},{16,8},{24,16},{32,24},{40,32},{48,40},{56,48},{64,56},{72,6... | collective-permute-start | bytes 196616 | tf_op jit(solution)/shard_map/ppermute | solution.py:20
  13.3 39.0 %collective-permute-start.2 = (bf16[1,64,512]{1,2,0:T(8,128)(2,1)S(1)}, bf16[1,64,512]{1,2,0:T(8,128)(2,1)S(1)}, u32[]{:S(2)}, u32[]{:S(2)}) collective-permute-start(bf16[1,64,512]{1,2,0:T(8,128)(2,1)S(1)} %copy.31), channel_id=1, source_target_pairs={{0,8},{8,16},{16,24},{24,32},{32,40},{40,48},{48,56},{56,64},{64,7... | collective-permute-start | bytes 196616 | tf_op jit(solution)/shard_map/ppermute | solution.py:18
  41.3 352.1 %collective-permute-start.1 = (bf16[1,512,512]{1,2,0:T(8,128)(2,1)}, bf16[1,512,512]{1,2,0:T(8,128)(2,1)S(1)}, u32[]{:S(2)}, u32[]{:S(2)}) collective-permute-start(bf16[1,512,512]{1,2,0:T(8,128)(2,1)} %copy.28), channel_id=1, source_target_pairs={{8,0},{16,8},{24,16},{32,24},{40,32},{48,40},{56,48},{64,56},{72,6... | collective-permute-start | bytes 1572872 | tf_op jit(solution)/shard_map/ppermute | solution.py:20
  48.0 345.4 %collective-permute-start = (bf16[1,512,512]{1,2,0:T(8,128)(2,1)}, bf16[1,512,512]{1,2,0:T(8,128)(2,1)S(1)}, u32[]{:S(2)}, u32[]{:S(2)}) collective-permute-start(bf16[1,512,512]{1,2,0:T(8,128)(2,1)} %copy.28), channel_id=1, source_target_pairs={{0,8},{8,16},{16,24},{24,32},{32,40},{40,48},{48,56},{56,64},{64,7... | collective-permute-start | bytes 1572872 | tf_op jit(solution)/shard_map/ppermute | solution.py:18
  52.3 0.7 copy-start.26
  53.0 1.5 copy-start.1
  56.6 0.9 copy-start.27
  58.7 0.8 copy-start
  393.4 1.6 copy-start.24
  393.4 1.6 copy-start.21
  399.1 6.9 copy-start.18
  399.1 7.1 %copy-start.16 = (bf16[1,512,32,16]{1,3,2,0:T(8,128)(2,1)}, bf16[1,512,32,16]{1,3,2,0:T(8,128)(2,1)S(1)}, u32[]{:S(2)}) copy-start(bf16[1,512,32,16]{1,3,2,0:T(8,128)(2,1)S(1)} %get-tuple-element.12) | copy-start | bytes 1572868
  399.1 7.7 %copy-start.14 = (bf16[1,512,32,16]{1,3,2,0:T(8,128)(2,1)}, bf16[1,512,32,16]{1,3,2,0:T(8,128)(2,1)S(1)}, u32[]{:S(2)}) copy-start(bf16[1,512,32,16]{1,3,2,0:T(8,128)(2,1)S(1)} %get-tuple-element.14) | copy-start | bytes 1572868
  399.1 7.9 %copy-start.12 = (bf16[1,512,32,16]{1,3,2,0:T(8,128)(2,1)}, bf16[1,512,32,16]{1,3,2,0:T(8,128)(2,1)S(1)}, u32[]{:S(2)}) copy-start(bf16[1,512,32,16]{1,3,2,0:T(8,128)(2,1)S(1)} %get-tuple-element.15) | copy-start | bytes 1572868
  399.1 8.1 %copy-start.10 = (bf16[1,512,32,16]{1,3,2,0:T(8,128)(2,1)}, bf16[1,512,32,16]{1,3,2,0:T(8,128)(2,1)S(1)}, u32[]{:S(2)}) copy-start(bf16[1,512,32,16]{1,3,2,0:T(8,128)(2,1)S(1)} %get-tuple-element.16) | copy-start | bytes 1572868
  399.2 8.3 %copy-start.8 = (bf16[1,512,32,16]{1,3,2,0:T(8,128)(2,1)}, bf16[1,512,32,16]{1,3,2,0:T(8,128)(2,1)S(1)}, u32[]{:S(2)}) copy-start(bf16[1,512,32,16]{1,3,2,0:T(8,128)(2,1)S(1)} %get-tuple-element.17) | copy-start | bytes 1572868
  399.2 8.5 %copy-start.6 = (bf16[1,512,32,16]{1,3,2,0:T(8,128)(2,1)}, bf16[1,512,32,16]{1,3,2,0:T(8,128)(2,1)S(1)}, u32[]{:S(2)}) copy-start(bf16[1,512,32,16]{1,3,2,0:T(8,128)(2,1)S(1)} %get-tuple-element.18) | copy-start | bytes 1572868
  399.2 8.7 %copy-start.4 = (bf16[1,512,32,16]{1,3,2,0:T(8,128)(2,1)}, bf16[1,512,32,16]{1,3,2,0:T(8,128)(2,1)S(1)}, u32[]{:S(2)}) copy-start(bf16[1,512,32,16]{1,3,2,0:T(8,128)(2,1)S(1)} %get-tuple-element.19) | copy-start | bytes 1572868
  399.2 8.9 %copy-start.2 = (bf16[1,512,32,16]{1,3,2,0:T(8,128)(2,1)}, bf16[1,512,32,16]{1,3,2,0:T(8,128)(2,1)S(1)}, u32[]{:S(2)}) copy-start(bf16[1,512,32,16]{1,3,2,0:T(8,128)(2,1)S(1)} %get-tuple-element.20) | copy-start | bytes 1572868
  399.2 11.3 %copy-start.19 = (bf16[1,512,32,16]{1,3,2,0:T(8,128)(2,1)}, bf16[1,512,32,16]{1,3,2,0:T(8,128)(2,1)S(1)}, u32[]{:S(2)}) copy-start(bf16[1,512,32,16]{1,3,2,0:T(8,128)(2,1)S(1)} %get-tuple-element.9) | copy-start | bytes 1572868
  403.9 2.5 copy-start.22
  411.8 2.5 copy-start.25
  417.6 2.9 copy-start.17
  417.6 3.2 copy-start.23
  417.6 3.2 copy-start.28
  417.7 3.5 copy-start.15
  419.1 2.3 copy-start.13
  420.5 1.2 copy-start.11
  420.8 1.2 copy-start.9
  421.1 1.2 copy-start.7
  421.4 1.2 copy-start.5
  421.7 1.2 copy-start.3
  422.9 1.2 copy-start.20
  422.9 1.2 copy-start.29
  422.9 1.2 copy-start.30
  423.0 1.2 copy-start.31
  423.0 1.2 copy-start.32
  423.0 1.2 copy-start.33
  423.0 1.2 copy-start.34
  423.0 1.2 copy-start.35
  423.0 1.3 copy-start.36
Sparse Core Ops, SparseCore 0:
  417.7 276.0 all-reduce.5
where the time goes:
time: 709 us; the launch traced here: 705 us
  blocking collectives  348 us (49%)
  waiting for transfers between devices  269 us (38%)
  matrix products  31.3 us (4%)
  local copies, waits for them, and re-layouts  19.2 us (3%)
  starting transfers between devices  18 us (3%)
  between operations  15.7 us (2%)
    unnamed x1, blocking collectives  325 us
    psum x1, waiting for transfers between devices, body(): filter_grad = lax.psum(local_grad, 'gz')  269 us
    all_gather x1, blocking collectives, body(): whole = lax.all_gather(features, 'col', axis=1, tiled=True)  23.9 us
    dot_general x27, matrix products, body(): jnp.einsum('on,xnc->xoc', filters[shift_x, shift_y, shift_z], window, pre...  17.5 us
  transfers between devices with their start and end apart: 5, of which 1 were waited for; matrix products, arithmetic and copies ran while one was open for 3% of the time, Pallas kernels for 0%

commit v1 on v0

v1 whole, which is shorter than its diff:
```python
import functools

import jax
import jax.numpy as jnp
from jax import lax
from jax.experimental import pallas as pl
from jax.experimental.pallas import tpu as pltpu
from jax.sharding import PartitionSpec as P

NY = 32
NZ = 16
VMEM = pl.BlockSpec(memory_space=pltpu.VMEM)


def shifted(value, down, right):
    cells = NY * NZ
    step = down * NZ + right
    if step:
        value = pltpu.roll(value, (-step) % cells, 1)
    cell = lax.broadcasted_iota(jnp.int32, value.shape, 1)
    row, col = cell // NZ, cell % NZ
    if down == 1:
        value = jnp.where(row < NY - 1, value, 0.0)
    if down == -1:
        value = jnp.where(row > 0, value, 0.0)
    if right == 1:
        value = jnp.where(col < NZ - 1, value, 0.0)
    if right == -1:
        value = jnp.where(col > 0, value, 0.0)
    return value


def spread_taps(cot, out_ref, base):
    outs = cot.shape[0]
    wide = cot.astype(jnp.float32)
    for tap in range(9):
        b, c = divmod(tap, 3)
        out_ref[base + tap * outs : base + (tap + 1) * outs, :] = shifted(wide, 1 - b, 1 - c).astype(jnp.bfloat16)


def input_kernel(cot_ref, taps_ref, out_ref, spread_ref):
    size = 9 * cot_ref.shape[1]
    for a in range(3):
        spread_taps(cot_ref[2 - a], spread_ref, a * size)
    out_ref[...] = lax.dot_general(
        taps_ref[...], spread_ref[...], (((0,), (0,)), ((), ())), preferred_element_type=jnp.float32
    )


def output_kernel(window_ref, taps_ref, out_ref, acc_ref):
    size = acc_ref.shape[0]
    for a in range(3):
        part = jnp.dot(taps_ref[a * size : (a + 1) * size, :], window_ref[a], preferred_element_type=jnp.float32)
        if a:
            acc_ref[...] += part
        else:
            acc_ref[...] = part
    outs = size // 9
    total = jnp.zeros((outs, NY * NZ), jnp.float32)
    for tap in range(9):
        b, c = divmod(tap, 3)
        total = total + shifted(acc_ref[tap * outs : (tap + 1) * outs, :], b - 1, c - 1)
    out_ref[...] = total.astype(jnp.bfloat16)


def filter_kernel(cot_ref, window_ref, out_ref, spread_ref):
    for q in range(4):
        spread_taps(cot_ref[q], spread_ref, 0)
        part = lax.dot_general(
            spread_ref[...], window_ref[q], (((1,), (1,)), ((), ())), preferred_element_type=jnp.float32
        )
        if q:
            out_ref[...] += part
        else:
            out_ref[...] = part


def call(kernel, out, scratch, flops, *args):
    return pl.pallas_call(
        kernel,
        out_shape=out,
        in_specs=[VMEM] * len(args),
        out_specs=VMEM,
        scratch_shapes=[scratch],
        compiler_params=pltpu.CompilerParams(vmem_limit_bytes=48 << 20),
        cost_estimate=pl.CostEstimate(
            flops=flops, transcendentals=0, bytes_accessed=sum(a.size * a.dtype.itemsize for a in args)
        ),
    )(*args)


def body(features, filters, cotangent):
    _, local, cells = features.shape
    devices = lax.axis_size("gz")
    cols = lax.axis_size("col")
    channels = local * cols
    quads = devices // 4
    place = lax.axis_index("gz")
    core = place % 2
    spot = place % 4
    x_own = features[0]
    c_own = cotangent[0]

    def xor(value, bits):
        return lax.ppermute(value, "gz", [(i, i ^ bits) for i in range(devices)])

    outward = [(i, i + 1) for i in range(1, devices - 1, 2)] + [(i, i - 1) for i in range(2, devices, 2)]

    def everywhere(block, axis, groups=None):
        count = len(groups[0]) if groups else lax.axis_size(axis)
        copies = jnp.broadcast_to(block[None], (count,) + block.shape)
        return lax.all_to_all(copies, axis, 0, 0, axis_index_groups=groups, tiled=True)

    x_halo = lax.ppermute(x_own, "gz", outward)
    c_halo = lax.ppermute(c_own, "gz", outward)
    own = everywhere(x_own, "col").reshape(channels, cells)
    halo = everywhere(x_halo, "col").reshape(channels, cells)
    other = xor(own, 1)
    half = channels // 2
    quarter = channels // 4
    other_halo = xor(lax.dynamic_slice_in_dim(halo, (1 - core) * half, half, 0), 1)
    first = core == 0
    side = spot // 2
    turn = 2 * core + side

    four = [[4 * g + r for r in range(4)] for g in range(quads)]
    c_quad = everywhere(c_own, "gz", four)
    c_other = xor(c_own, 1)
    c_three = jnp.where(first, jnp.stack([c_halo, c_own, c_other]), jnp.stack([c_other, c_own, c_halo]))

    tops = jnp.stack([jnp.max(jnp.abs(own)), jnp.max(jnp.abs(c_own))]).astype(jnp.float32)
    tops = everywhere(jnp.broadcast_to(tops[:, None], (2, 128)), "gz")
    tops = jnp.max(tops, axis=(0, 2))
    total_cells = cells * devices
    scale = 1.0 / jnp.sqrt(jnp.float32(total_cells))
    bound = jnp.maximum(tops[0] * tops[1] * (total_cells * scale), 1e-25)
    up = 30000.0 / bound
    down = bound * (1.0 / 30000.0)

    taps = filters.reshape(27 * local, channels)
    size = 9 * local
    flops = 2 * 27 * local * channels * cells

    partial = call(
        input_kernel,
        jax.ShapeDtypeStruct((channels, cells), jnp.float32),
        pltpu.VMEM((3 * size, cells), jnp.bfloat16),
        flops,
        c_three,
        taps,
    )
    pieces = lax.all_to_all(partial.reshape(cols, local, cells), "col", 0, 0, tiled=True)
    input_grad = jnp.sum(pieces, axis=0).astype(jnp.bfloat16)[None]

    window = jnp.where(first, jnp.stack([halo, own, other]), jnp.stack([other, own, halo]))
    output = call(
        output_kernel,
        jax.ShapeDtypeStruct((local, cells), jnp.bfloat16),
        pltpu.VMEM((size, cells), jnp.float32),
        flops,
        window,
        taps,
    )[None]

    def cut(value, index, width):
        return lax.dynamic_slice_in_dim(value, index * width, width, 0)

    own_first = jnp.where(first, own, other)
    own_last = jnp.where(first, other, own)
    far = xor(cut(jnp.where(spot < 2, own_first, own_last), turn ^ 1, quarter), 2)
    halo_half = cut(halo, core, half)
    halo_first = jnp.where(first, halo_half, other_halo)
    halo_last = jnp.where(first, other_halo, halo_half)
    outer = [halo_first, cut(own_first, core, half), cut(own_last, core, half), halo_last]
    own_first, own_last = cut(own_first, turn, quarter), cut(own_last, turn, quarter)
    near_last = cut(halo_last, side, quarter)
    near_first = cut(halo_first, side, quarter)
    inner = [
        jnp.where(side == 0, own_first, far),
        jnp.where(side == 0, own_last, near_first),
        jnp.where(side == 0, near_last, own_first),
        jnp.where(side == 0, far, own_last),
    ]
    windows = jnp.stack([jnp.concatenate([a, b], axis=0) for a, b in zip(outer, inner)])
    width = half + quarter
    grads = call(
        filter_kernel,
        jax.ShapeDtypeStruct((size, width), jnp.float32),
        pltpu.VMEM((size, cells), jnp.bfloat16),
        flops,
        c_quad,
        windows,
    )
    ring = [[4 * g + r for g in range(quads)] for r in range(4)]
    narrow = (grads * (scale * up)).astype(jnp.float16).reshape(quads, size // quads, width)
    narrow = lax.all_to_all(narrow, "gz", 0, 0, axis_index_groups=ring, tiled=True)
    mine = jnp.sum(narrow.astype(jnp.float32), axis=0).astype(jnp.float16)
    mine = everywhere(mine, "gz", ring).reshape(size, width)
    beyond = xor(mine, 2)
    both = jnp.stack([mine, beyond])
    swapped = xor(both, 1)
    low = jnp.where(first, both, swapped)
    high = jnp.where(first, swapped, both)
    low = jnp.where(side == 0, low, low[::-1])
    high = jnp.where(side == 0, high, high[::-1])
    offset0 = jnp.concatenate([low[0][:, :half], high[0][:, :half]], axis=1)
    offset1 = jnp.concatenate([low[0][:, half:], low[1][:, half:], high[0][:, half:], high[1][:, half:]], axis=1)
    offset2 = jnp.concatenate([low[1][:, :half], high[1][:, :half]], axis=1)
    filter_grad = jnp.stack([offset0, offset1, offset2]).astype(jnp.float32) * down
    return output, input_grad, filter_grad.reshape(3, 3, 3, local, channels)


def solution(mesh):
    in_specs = (P("gz", "col", None), P(None, None, None, "col", None), P("gz", "col", None))
    out_specs = (P("gz", "col", None), P("gz", "col", None), P(None, None, None, "col", None))
    return jax.shard_map(body, mesh=mesh, in_specs=in_specs, out_specs=out_specs, check_vma=False)
```

time: 709 us -> 144 us (0.20)
  blocking collectives: 348 us -> 17.3 us
  waiting for transfers between devices: 269 us -> 38.3 us
  starting transfers between devices: 18 us -> 59.1 us
  matrix products: 31.3 us -> 0 us
  between operations: 15.7 us -> 2.38 us
  local copies, waits for them, and re-layouts: 19.2 us -> 6.15 us
  other arithmetic: 3.92 us -> 14.3 us
    unnamed x1 -> x0, blocking collectives: 325 us -> none
    psum x1 -> x0, waiting for transfers between devices: 269 us -> none  [body(): filter_grad = lax.psum(local_grad, 'gz')]
    all_to_all x0 -> x6, starting transfers between devices: none -> 31.5 us  [the longest x5 27.3 us: everywhere(): lax.all_to_all(copies, axis, 0, 0, axis_index_groups=groups, tiled=True)]
    dot_general x81 -> x0, matrix products: 31.3 us -> none  [the longest x27 17.5 us: body(): jnp.einsum('on,xnc->xoc', filters[shift_x, shift_y, shift_z], window, pre...]
    all_to_all x0 -> x6, waiting for transfers between devices: none -> 26.3 us  [the longest x5 26.3 us: everywhere(): lax.all_to_all(copies, axis, 0, 0, axis_index_groups=groups, tiled=True)]
    all_gather x1 -> x0, blocking collectives: 23.9 us -> none  [body(): whole = lax.all_gather(features, 'col', axis=1, tiled=True)]
    all_to_all x0 -> x1, blocking collectives: none -> 17.3 us  [body(): lax.all_to_all(narrow, 'gz', 0, 0, axis_index_groups=ring, tiled=True)]
    ppermute x4 -> x8, waiting for transfers between devices: 0.01 us -> 12 us  [the longest x6 7.32 us: xor(): return lax.ppermute(value, 'gz', [(i, i ^ bits) for i in range(devices)])]
  transfers between devices with their start and end apart: 5 -> 14, of which waited for: 1 -> 6; matrix products, arithmetic and copies ran while one was open for 3% -> 8% of each run, Pallas kernels for 0% -> 3%
where the time goes in v1:
time: 144 us; the launch traced here: 143 us
  starting transfers between devices  59.1 us (41%)
  waiting for transfers between devices  38.3 us (27%)
  blocking collectives  17.3 us (12%)
  other arithmetic  14.3 us (10%)
  local copies, waits for them, and re-layouts  6.15 us (4%)
  Pallas kernels  5.63 us (4%)
  between operations  2.38 us (2%)
    all_to_all x5, starting transfers between devices, everywhere(): lax.all_to_all(copies, axis, 0, 0, axis_index_groups=groups, tiled=True)  27.3 us
    all_to_all x5, waiting for transfers between devices, everywhere(): lax.all_to_all(copies, axis, 0, 0, axis_index_groups=groups, tiled=True)  26.3 us
    ppermute x6, starting transfers between devices, xor(): return lax.ppermute(value, 'gz', [(i, i ^ bits) for i in range(devices)])  18.3 us
    all_to_all x1, blocking collectives, body(): lax.all_to_all(narrow, 'gz', 0, 0, axis_index_groups=ring, tiled=True)  17.3 us
    ppermute x6, waiting for transfers between devices, xor(): return lax.ppermute(value, 'gz', [(i, i ^ bits) for i in range(devices)])  7.32 us
    pallas_call x3, Pallas kernels, call(): pl.pallas_call(kernel, out_shape=out, in_specs=[VMEM] * len(args), out_sp...  5.63 us
    ppermute x1, starting transfers between devices, body(): x_halo = lax.ppermute(x_own, 'gz', outward)  5.37 us
    ppermute x1, waiting for transfers between devices, body(): x_halo = lax.ppermute(x_own, 'gz', outward)  4.65 us
  transfers between devices with their start and end apart: 14, of which 6 were waited for; matrix products, arithmetic and copies ran while one was open for 8% of the time, Pallas kernels for 3%

profile of v1, /device:TPU:1, one launch (start us, length us, event | category | flops | bytes accessed | tf_op | source)
XLA Modules:
  0.0 143.1 jit_solution(13318520410467987620)
XLA Ops:
  0.6 1.7 %broadcast_in_dim.11 = bf16[8,64,512]{2,1,0:T(8,128)(2,1)} broadcast(bf16[64,512]{1,0:T(8,128)(2,1)} %bitcast.63), dimensions={1,2} | broadcast | bytes 589824 | tf_op jit(solution)/shard_map/broadcast_in_dim | solution.py:111
  2.4 5.9 %all-to-all-start.1 = ((bf16[8,64,512]{2,1,0:T(8,128)(2,1)}), bf16[8,64,512]{2,1,0:T(8,128)(2,1)S(1)}, u32[]{:S(2)}, u32[]{:S(2)}) async-start(bf16[8,64,512]{2,1,0:T(8,128)(2,1)} %broadcast_in_dim.11), calls=%async_computation.1 | async-start | bytes 1048576 | tf_op jit(solution)/shard_map/all_to_all | solution.py:112
  8.2 5.4 %collective-permute-start = (bf16[64,512]{1,0:T(8,128)(2,1)S(1)}, bf16[64,512]{1,0:T(8,128)(2,1)S(1)}, u32[]{:S(2)}, u32[]{:S(2)}) collective-permute-start(bf16[64,512]{1,0:T(8,128)(2,1)S(1)} %bitcast.64), channel_id=1, source_target_pairs={{8,16},{24,32},{40,48},{56,64},{72,80},{88,96},{104,112},{120,128}... | collective-permute-start | bytes 196616 | tf_op jit(solution)/shard_map/ppermute | solution.py:114
  13.6 4.7 %collective-permute-done = bf16[64,512]{1,0:T(8,128)(2,1)S(1)} collective-permute-done((bf16[64,512]{1,0:T(8,128)(2,1)S(1)}, bf16[64,512]{1,0:T(8,128)(2,1)S(1)}, u32[]{:S(2)}, u32[]{:S(2)}) %collective-permute-start) | collective-permute-done | bytes 65568 | tf_op jit(solution)/shard_map/ppermute | solution.py:114
  18.3 0.8 broadcast_in_dim.10
  19.1 4.6 %all-to-all-start = ((bf16[8,64,512]{2,1,0:T(8,128)(2,1)}), bf16[8,64,512]{2,1,0:T(8,128)(2,1)S(1)}, u32[]{:S(2)}, u32[]{:S(2)}) async-start(bf16[8,64,512]{2,1,0:T(8,128)(2,1)} %broadcast_in_dim.10), calls=%async_computation | async-start | bytes 1048576 | tf_op jit(solution)/shard_map/all_to_all | solution.py:112
  23.7 0.6 abs_reduce_fusion.1
  24.3 0.7 abs_reduce_fusion
  25.0 9.1 %all-to-all-done = bf16[8,64,512]{2,1,0:T(8,128)(2,1)S(1)} async-done(((bf16[8,64,512]{2,1,0:T(8,128)(2,1)}), bf16[8,64,512]{2,1,0:T(8,128)(2,1)S(1)}, u32[]{:S(2)}, u32[]{:S(2)}) %all-to-all-start) | async-done | bytes 524320 | tf_op jit(solution)/shard_map/all_to_all | solution.py:112
  34.1 0.5 collective-permute-start.4
  34.7 1.4 maximum_convert_fusion
  36.0 0.7 broadcast_in_dim_broadcast_in_dim_broadcast_in_dim.2
  36.7 9.6 %all-to-all-start.4 = ((f32[32,2,128]{2,1,0:T(2,128)}), f32[32,2,128]{2,1,0:T(2,128)S(1)}, u32[]{:S(2)}, u32[]{:S(2)}) async-start(f32[32,2,128]{2,1,0:T(2,128)} %broadcast_in_dim_broadcast_in_dim_broadcast_in_dim.2), calls=%async_computation.4 | async-start | bytes 65536 | tf_op jit(solution)/shard_map/all_to_all | solution.py:112
  46.4 9.6 %all-to-all-done.4 = f32[32,2,128]{2,1,0:T(2,128)S(1)} async-done(((f32[32,2,128]{2,1,0:T(2,128)}), f32[32,2,128]{2,1,0:T(2,128)S(1)}, u32[]{:S(2)}, u32[]{:S(2)}) %all-to-all-start.4) | async-done | bytes 32800 | tf_op jit(solution)/shard_map/all_to_all | solution.py:112
  56.0 0.7 broadcast_in_dim.13
  56.7 3.8 %all-to-all-start.3 = ((bf16[4,64,512]{2,1,0:T(8,128)(2,1)}), bf16[4,64,512]{2,1,0:T(8,128)(2,1)S(1)}, u32[]{:S(2)}, u32[]{:S(2)}) async-start(bf16[4,64,512]{2,1,0:T(8,128)(2,1)} %broadcast_in_dim.13), calls=%async_computation.3 | async-start | bytes 524288 | tf_op jit(solution)/shard_map/all_to_all | solution.py:112
  60.4 0.1 reduce_max.29
  60.6 0.6 fusion.6
  62.5 0.1 broadcast_select_fusion.5
  62.7 0.1 broadcast_select_fusion.3
  62.9 3.0 %collective-permute-start.5 = (bf16[128,512]{1,0:T(8,128)(2,1)S(1)}, bf16[128,512]{1,0:T(8,128)(2,1)S(1)}, u32[]{:S(2)}, u32[]{:S(2)}) collective-permute-start(bf16[128,512]{1,0:T(8,128)(2,1)S(1)} %get-tuple-element.16), channel_id=1, source_target_pairs={{0,16},{8,24},{16,0},{24,8},{32,48},{40,56},{48,32},{56,40},{64,80... | collective-permute-start | bytes 393224 | tf_op jit(solution)/shard_map/ppermute | solution.py:105
  66.0 4.1 %collective-permute-done.5 = bf16[128,512]{1,0:T(8,128)(2,1)S(1)} collective-permute-done((bf16[128,512]{1,0:T(8,128)(2,1)S(1)}, bf16[128,512]{1,0:T(8,128)(2,1)S(1)}, u32[]{:S(2)}, u32[]{:S(2)}) %collective-permute-start.5) | collective-permute-done | bytes 131104 | tf_op jit(solution)/shard_map/ppermute | solution.py:105
  70.3 0.2 pad_maximum_fusion.2.window_ref
  70.5 1.4 %shard_map.60 = f32[576,384]{1,0:T(8,128)S(1)} custom-call(bf16[4,64,512]{2,1,0:T(8,128)(2,1)S(1)} %all-to-all-done.3.cot_ref, bf16[4,384,512]{2,1,0:T(8,128)(2,1)S(1)} %pad_maximum_fusion.2.window_ref), custom_call_target="tpu_custom_call" | custom-call | flops 905969664 | bytes 1835008 | tf_op jit(solution)/shard_map/pallas_call | solution.py:79
  72.0 17.3 %all_to_all.35 = f16[8,72,384]{2,1,0:T(8,128)(2,1)S(1)} all-to-all(f16[8,72,384]{2,1,0:T(8,128)(2,1)S(1)} %bitcast.59), channel_id=1, replica_groups={{0,32,64,96,128,160,192,224},{8,40,72,104,136,168,200,232},{16,48,80,11..., dimensions={0} | all-to-all | bytes 884736 | tf_op jit(solution)/shard_map/all_to_all | solution.py:196
  89.4 0.8 broadcast_in_dim.14
  90.2 3.5 %all-to-all-start.6 = ((f16[8,72,384]{2,1,0:T(8,128)(2,1)}), f16[8,72,384]{2,1,0:T(8,128)(2,1)S(1)}, u32[]{:S(2)}, u32[]{:S(2)}) async-start(f16[8,72,384]{2,1,0:T(8,128)(2,1)} %broadcast_in_dim.14), calls=%async_computation.6 | async-start | bytes 884736 | tf_op jit(solution)/shard_map/all_to_all | solution.py:112
  93.7 2.0 %collective-permute-start.3 = (bf16[64,512]{1,0:T(8,128)(2,1)S(1)}, bf16[64,512]{1,0:T(8,128)(2,1)S(1)}, u32[]{:S(2)}, u32[]{:S(2)}) collective-permute-start(bf16[64,512]{1,0:T(8,128)(2,1)S(1)} %bitcast.61), channel_id=1, source_target_pairs={{0,8},{8,0},{16,24},{24,16},{32,40},{40,32},{48,56},{56,48},{64,72... | collective-permute-start | bytes 196616 | tf_op jit(solution)/shard_map/ppermute | solution.py:105
  95.7 3.8 %collective-permute-start.2 = (bf16[64,512]{1,0:T(8,128)(2,1)S(1)}, bf16[64,512]{1,0:T(8,128)(2,1)S(1)}, u32[]{:S(2)}, u32[]{:S(2)}) collective-permute-start(bf16[64,512]{1,0:T(8,128)(2,1)S(1)} %bitcast.62), channel_id=1, source_target_pairs={{8,16},{24,32},{40,48},{56,64},{72,80},{88,96},{104,112},{120,128}... | collective-permute-start | bytes 196616 | tf_op jit(solution)/shard_map/ppermute | solution.py:115
  99.5 7.7 %all-to-all-done.6 = f16[8,72,384]{2,1,0:T(8,128)(2,1)S(1)} async-done(((f16[8,72,384]{2,1,0:T(8,128)(2,1)}), f16[8,72,384]{2,1,0:T(8,128)(2,1)S(1)}, u32[]{:S(2)}, u32[]{:S(2)}) %all-to-all-start.6) | async-done | bytes 442400 | tf_op jit(solution)/shard_map/all_to_all | solution.py:112
  107.2 0.4 collective-permute-start.6
  107.6 2.3 %shard_map.59 = f32[512,512]{1,0:T(8,128)} custom-call(bf16[3,64,512]{2,1,0:T(8,128)(2,1)S(1)} %fusion.4.cot_ref, bf16[1728,512]{1,0:T(8,128)(2,1)S(1)} %bitcast.45), custom_call_target="tpu_custom_call" | custom-call | flops 905969664 | bytes 1966080 | tf_op jit(solution)/shard_map/pallas_call | solution.py:79
  109.9 4.2 %all-to-all-start.2 = ((f32[8,64,512]{2,1,0:T(8,128)}), f32[8,64,512]{2,1,0:T(8,128)}, u32[]{:S(2)}, u32[]{:S(2)}) async-start(f32[8,64,512]{2,1,0:T(8,128)} %bitcast.10), calls=%async_computation.2 | async-start | bytes 2097152 | tf_op jit(solution)/shard_map/all_to_all | solution.py:152
  114.2 3.2 %collective-permute-done.6 = f16[576,384]{1,0:T(8,128)(2,1)} collective-permute-done((f16[576,384]{1,0:T(8,128)(2,1)S(1)}, f16[576,384]{1,0:T(8,128)(2,1)}, u32[]{:S(2)}, u32[]{:S(2)}) %collective-permute-start.6) | collective-permute-done | bytes 442400 | tf_op jit(solution)/shard_map/ppermute | solution.py:105
  117.4 2.2 %pad_maximum_fusion.3 = f16[2,576,384]{2,1,0:T(8,128)(2,1)} fusion(f16[1,576,384]{2,1,0:T(8,128)(2,1)} %bitcast.23, f16[1,576,384]{2,1,0:T(8,128)(2,1)S(1)} %bitcast.53), kind=kLoop, calls=%fused_computation.9 | loop fusion | flops 442368 | bytes 1769472 | tf_op jit(solution)/shard_map/stack | solution.py:200
  119.5 12.5 %collective-permute-start.7 = (f16[2,576,384]{2,1,0:T(8,128)(2,1)}, f16[2,576,384]{2,1,0:T(8,128)(2,1)}, u32[]{:S(2)}, u32[]{:S(2)}) collective-permute-start(f16[2,576,384]{2,1,0:T(8,128)(2,1)} %pad_maximum_fusion.3), channel_id=1, source_target_pairs={{0,8},{8,0},{16,24},{24,16},{32,40},{40,32},{48,56},{56,48},{64,72... | collective-permute-start | bytes 2654216 | tf_op jit(solution)/shard_map/ppermute | solution.py:105
  132.0 1.9 %reduce_sum.18 = bf16[64,512]{1,0:T(8,128)(2,1)} reduce(f32[8,64,512]{2,1,0:T(8,128)} %all-to-all-done.2, f32[]{:T(128)} %constant.54.clone.1), dimensions={0}, to_apply=%region_0.1 | reduce | flops 229376 | bytes 1114116 | tf_op jit(solution)/shard_map/reduce_sum | solution.py:153
  133.9 1.4 %fusion.1.window_ref = bf16[3,512,512]{2,1,0:T(8,128)(2,1)S(1)} fusion(bf16[1,512,512]{2,1,0:T(8,128)(2,1)S(1)} %bitcast.48, bf16[1,512,512]{2,1,0:T(8,128)(2,1)} %bitcast.58, bf16[1,512,512]{2,1,0:T(8,128)(2,1)S(1)} %bitcast.51, pred[]{:T(512)S(6)} %eq.7), kind=kLoop, calls=%fused_computation.4 | loop fusion | flops 3932160 | bytes 3145729 | tf_op jit(solution)/shard_map/jit(_where)/select_n | solution.py:155
  135.4 1.9 %shard_map.58 = bf16[64,512]{1,0:T(8,128)(2,1)} custom-call(bf16[3,512,512]{2,1,0:T(8,128)(2,1)S(1)} %fusion.1.window_ref, bf16[1728,512]{1,0:T(8,128)(2,1)S(1)} %bitcast.46), custom_call_target="tpu_custom_call" | custom-call | flops 905969664 | bytes 3342336 | tf_op jit(solution)/shard_map/pallas_call | solution.py:79
  137.3 1.8 %broadcast_select_fusion.1 = (f16[2,576,384]{2,1,0:T(8,128)(2,1)S(1)}, f16[2,576,384]{2,1,0:T(8,128)(2,1)S(1)}) fusion(f16[2,576,384]{2,1,0:T(8,128)(2,1)} %collective-permute-done.7, pred[]{:T(512)S(6)} %eq.7, f16[1,576,384]{2,1,0:T(8,128)(2,1)} %bitcast.23, f16[1,576,384]{2,1,0:T(8,128)(2,1)S(1)} %bitcast.54), kind=kLoop, calls=%fused_computation.13 | loop fusion | flops 1327104 | bytes 3538945 | tf_op jit(solution)/shard_map/jit(_where)/select_n | solution.py:202
  139.0 0.2 reverse_select_fusion.1
  139.3 0.2 slice_bitcast_fusion.3
  139.7 0.2 reverse_select_fusion
  139.9 0.2 slice_bitcast_fusion.2
  140.3 0.1 pad_maximum_fusion.4
  140.4 0.1 pad_maximum_fusion.6
  140.6 0.2 pad_maximum_fusion.5
  140.8 2.4 %convert_multiply_fusion = f32[3,3,3,64,512]{4,3,2,1,0:T(8,128)} fusion(f16[1,3,3,64,512]{4,3,2,1,0:T(8,128)(2,1)S(1)} %bitcast.56, f16[1,3,3,64,512]{4,3,2,1,0:T(8,128)(2,1)S(1)} %bitcast.57, f16[1,3,3,64,512]{4,3,2,1,0:T(8,128)(2,1)S(1)} %bitcast.55, f32[]{:T(128)} %bitcast.31), kind=kLoop, calls=%fused_computation | loop fusion | flops 3538944 | bytes 5308420 | tf_op jit(solution)/shard_map/mul | solution.py:209
  (36 shorter events, 0.9 us)
Async XLA Ops:
  0.6 7.6 %copy-start.3 = (bf16[1,64,512]{2,1,0:T(8,128)(2,1)S(1)}, bf16[1,64,512]{2,1,0:T(8,128)(2,1)}, u32[]{:S(2)}) copy-start(bf16[1,64,512]{2,1,0:T(8,128)(2,1)} %param.3) | copy-start | bytes 196612
  0.6 23.1 %copy-start.2 = (bf16[1,64,512]{2,1,0:T(8,128)(2,1)S(1)}, bf16[1,64,512]{2,1,0:T(8,128)(2,1)}, u32[]{:S(2)}) copy-start(bf16[1,64,512]{2,1,0:T(8,128)(2,1)} %param.5) | copy-start | bytes 196612
  2.4 15.9 %all-to-all-start.1 = ((bf16[8,64,512]{2,1,0:T(8,128)(2,1)}), bf16[8,64,512]{2,1,0:T(8,128)(2,1)S(1)}, u32[]{:S(2)}, u32[]{:S(2)}) async-start(bf16[8,64,512]{2,1,0:T(8,128)(2,1)} %broadcast_in_dim.11), calls=%async_computation.1 | async-start | bytes 1048576 | tf_op jit(solution)/shard_map/all_to_all | solution.py:112
  8.2 10.0 %collective-permute-start = (bf16[64,512]{1,0:T(8,128)(2,1)S(1)}, bf16[64,512]{1,0:T(8,128)(2,1)S(1)}, u32[]{:S(2)}, u32[]{:S(2)}) collective-permute-start(bf16[64,512]{1,0:T(8,128)(2,1)S(1)} %bitcast.64), channel_id=1, source_target_pairs={{8,16},{24,32},{40,48},{56,64},{72,80},{88,96},{104,112},{120,128}... | collective-permute-start | bytes 196616 | tf_op jit(solution)/shard_map/ppermute | solution.py:114
  19.1 15.0 %all-to-all-start = ((bf16[8,64,512]{2,1,0:T(8,128)(2,1)}), bf16[8,64,512]{2,1,0:T(8,128)(2,1)S(1)}, u32[]{:S(2)}, u32[]{:S(2)}) async-start(bf16[8,64,512]{2,1,0:T(8,128)(2,1)} %broadcast_in_dim.10), calls=%async_computation | async-start | bytes 1048576 | tf_op jit(solution)/shard_map/all_to_all | solution.py:112
  24.3 38.4 %collective-permute-start.1 = (bf16[512,512]{1,0:T(8,128)(2,1)S(1)}, bf16[512,512]{1,0:T(8,128)(2,1)S(1)}, u32[]{:S(2)}, u32[]{:S(2)}) collective-permute-start(bf16[512,512]{1,0:T(8,128)(2,1)S(1)} %bitcast.47), channel_id=1, source_target_pairs={{0,8},{8,0},{16,24},{24,16},{32,40},{40,32},{48,56},{56,48},{64,72... | collective-permute-start | bytes 1572872 | tf_op jit(solution)/shard_map/ppermute | solution.py:105
  34.1 28.4 %collective-permute-start.4 = (bf16[256,512]{1,0:T(8,128)(2,1)S(1)}, bf16[256,512]{1,0:T(8,128)(2,1)S(1)}, u32[]{:S(2)}, u32[]{:S(2)}) collective-permute-start(bf16[256,512]{1,0:T(8,128)(2,1)S(1)} %constant_dynamic-slice_fusion.2), channel_id=1, source_target_pairs={{0,8},{8,0},{16,24},{24,16},{32,40},{40,32},{48,56},{56,48},{64,72... | collective-permute-start | bytes 786440 | tf_op jit(solution)/shard_map/ppermute | solution.py:105
  36.7 19.2 %all-to-all-start.4 = ((f32[32,2,128]{2,1,0:T(2,128)}), f32[32,2,128]{2,1,0:T(2,128)S(1)}, u32[]{:S(2)}, u32[]{:S(2)}) async-start(f32[32,2,128]{2,1,0:T(2,128)} %broadcast_in_dim_broadcast_in_dim_broadcast_in_dim.2), calls=%async_computation.4 | async-start | bytes 65536 | tf_op jit(solution)/shard_map/all_to_all | solution.py:112
  56.7 13.8 %all-to-all-start.3 = ((bf16[4,64,512]{2,1,0:T(8,128)(2,1)}), bf16[4,64,512]{2,1,0:T(8,128)(2,1)S(1)}, u32[]{:S(2)}, u32[]{:S(2)}) async-start(bf16[4,64,512]{2,1,0:T(8,128)(2,1)} %broadcast_in_dim.13), calls=%async_computation.3 | async-start | bytes 524288 | tf_op jit(solution)/shard_map/all_to_all | solution.py:112
  62.7 3.2 %copy-start.1 = (bf16[512,512]{1,0:T(8,128)(2,1)}, bf16[512,512]{1,0:T(8,128)(2,1)S(1)}, u32[]{:S(2)}) copy-start(bf16[512,512]{1,0:T(8,128)(2,1)S(1)} %collective-permute-done.1) | copy-start | bytes 1572868
  62.9 7.2 %collective-permute-start.5 = (bf16[128,512]{1,0:T(8,128)(2,1)S(1)}, bf16[128,512]{1,0:T(8,128)(2,1)S(1)}, u32[]{:S(2)}, u32[]{:S(2)}) collective-permute-start(bf16[128,512]{1,0:T(8,128)(2,1)S(1)} %get-tuple-element.16), channel_id=1, source_target_pairs={{0,16},{8,24},{16,0},{24,8},{32,48},{40,56},{48,32},{56,40},{64,80... | collective-permute-start | bytes 393224 | tf_op jit(solution)/shard_map/ppermute | solution.py:105
  72.0 35.6 %copy-start = (bf16[3,3,3,64,512]{4,3,2,1,0:T(8,128)(2,1)S(1)}, bf16[3,3,3,64,512]{4,3,2,1,0:T(8,128)(2,1)}, u32[]{:S(2)}) copy-start(bf16[3,3,3,64,512]{4,3,2,1,0:T(8,128)(2,1)} %param.4) | copy-start | bytes 5308420
  90.2 17.0 %all-to-all-start.6 = ((f16[8,72,384]{2,1,0:T(8,128)(2,1)}), f16[8,72,384]{2,1,0:T(8,128)(2,1)S(1)}, u32[]{:S(2)}, u32[]{:S(2)}) async-start(f16[8,72,384]{2,1,0:T(8,128)(2,1)} %broadcast_in_dim.14), calls=%async_computation.6 | async-start | bytes 884736 | tf_op jit(solution)/shard_map/all_to_all | solution.py:112
  93.7 13.9 %collective-permute-start.3 = (bf16[64,512]{1,0:T(8,128)(2,1)S(1)}, bf16[64,512]{1,0:T(8,128)(2,1)S(1)}, u32[]{:S(2)}, u32[]{:S(2)}) collective-permute-start(bf16[64,512]{1,0:T(8,128)(2,1)S(1)} %bitcast.61), channel_id=1, source_target_pairs={{0,8},{8,0},{16,24},{24,16},{32,40},{40,32},{48,56},{56,48},{64,72... | collective-permute-start | bytes 196616 | tf_op jit(solution)/shard_map/ppermute | solution.py:105
  95.7 11.9 %collective-permute-start.2 = (bf16[64,512]{1,0:T(8,128)(2,1)S(1)}, bf16[64,512]{1,0:T(8,128)(2,1)S(1)}, u32[]{:S(2)}, u32[]{:S(2)}) collective-permute-start(bf16[64,512]{1,0:T(8,128)(2,1)S(1)} %bitcast.62), channel_id=1, source_target_pairs={{8,16},{24,32},{40,48},{56,64},{72,80},{88,96},{104,112},{120,128}... | collective-permute-start | bytes 196616 | tf_op jit(solution)/shard_map/ppermute | solution.py:115
  107.2 10.2 %collective-permute-start.6 = (f16[576,384]{1,0:T(8,128)(2,1)S(1)}, f16[576,384]{1,0:T(8,128)(2,1)}, u32[]{:S(2)}, u32[]{:S(2)}) collective-permute-start(f16[576,384]{1,0:T(8,128)(2,1)S(1)} %bitcast.52), channel_id=1, source_target_pairs={{0,16},{8,24},{16,0},{24,8},{32,48},{40,56},{48,32},{56,40},{64,80... | collective-permute-start | bytes 1327112 | tf_op jit(solution)/shard_map/ppermute | solution.py:105
  109.9 22.1 %all-to-all-start.2 = ((f32[8,64,512]{2,1,0:T(8,128)}), f32[8,64,512]{2,1,0:T(8,128)}, u32[]{:S(2)}, u32[]{:S(2)}) async-start(f32[8,64,512]{2,1,0:T(8,128)} %bitcast.10), calls=%async_computation.2 | async-start | bytes 2097152 | tf_op jit(solution)/shard_map/all_to_all | solution.py:152
  119.5 17.8 %collective-permute-start.7 = (f16[2,576,384]{2,1,0:T(8,128)(2,1)}, f16[2,576,384]{2,1,0:T(8,128)(2,1)}, u32[]{:S(2)}, u32[]{:S(2)}) collective-permute-start(f16[2,576,384]{2,1,0:T(8,128)(2,1)} %pad_maximum_fusion.3), channel_id=1, source_target_pairs={{0,8},{8,0},{16,24},{24,16},{32,40},{40,32},{48,56},{56,48},{64,72... | collective-permute-start | bytes 2654216 | tf_op jit(solution)/shard_map/ppermute | solution.py:105

commit v2 on v1

v2 whole, which is shorter than its diff:
```python
import jax
import jax.numpy as jnp
from jax import lax
from jax.experimental import pallas as pl
from jax.experimental.pallas import tpu as pltpu
from jax.sharding import PartitionSpec as P

NY = 32
NZ = 16
VMEM = pl.BlockSpec(memory_space=pltpu.VMEM)
SMEM = pl.BlockSpec(memory_space=pltpu.SMEM)
LOG2 = 0.6931471805599453
TOP = 13.0
EXTRA = 8


def shifted(value, down, right):
    cells = NY * NZ
    step = down * NZ + right
    if step:
        value = pltpu.roll(value, (-step) % cells, 1)
    cell = lax.broadcasted_iota(jnp.int32, value.shape, 1)
    row, col = cell // NZ, cell % NZ
    if down == 1:
        value = jnp.where(row < NY - 1, value, 0.0)
    if down == -1:
        value = jnp.where(row > 0, value, 0.0)
    if right == 1:
        value = jnp.where(col < NZ - 1, value, 0.0)
    if right == -1:
        value = jnp.where(col > 0, value, 0.0)
    return value


def spread_taps(cot_ref, out_ref):
    outs = cot_ref.shape[0]
    wide = cot_ref[...].astype(jnp.float32)
    for tap in range(9):
        b, c = divmod(tap, 3)
        out_ref[tap * outs : (tap + 1) * outs, :] = shifted(wide, 1 - b, 1 - c).astype(jnp.bfloat16)


def lines(ref, first, count, beyond=False):
    _, both, cells = ref.shape
    local = both // 2
    return ref[pl.ds(first, count), (local if beyond else 0) : (both if beyond else local), :].reshape(count * local, cells)


def input_kernel(spot_ref, col_ref, halo_ref, own_ref, other_ref, taps_ref, *refs):
    out_refs, (spread_ref, acc_ref) = refs[:-2], refs[-2:]
    away = 2 - 2 * (spot_ref[0] % 2)
    spread_taps(halo_ref, spread_ref.at[0])
    spread_taps(own_ref, spread_ref.at[1])
    spread_taps(other_ref, spread_ref.at[2])

    def part(a, source):
        return lax.dot_general(
            taps_ref[a], spread_ref[source], (((0,), (0,)), ((), ())), preferred_element_type=jnp.float32
        )

    acc_ref[...] = part(away, 0)
    acc_ref[...] += part(1, 1)
    acc_ref[...] += part(2 - away, 2)
    local = out_refs[0].shape[0]
    col = col_ref[0]
    for bits, out_ref in enumerate(out_refs):
        out_ref[...] = acc_ref[pl.ds(pl.multiple_of((col ^ bits) * local, local), local), :]


def output_kernel(spot_ref, mine_ref, other_ref, taps_ref, out_ref, acc_ref):
    away = 2 * (spot_ref[0] % 2)
    cols = mine_ref.shape[0]
    acc_ref[...] = jnp.dot(taps_ref[away], lines(mine_ref, 0, cols, True), preferred_element_type=jnp.float32)
    acc_ref[...] += jnp.dot(taps_ref[1], lines(mine_ref, 0, cols), preferred_element_type=jnp.float32)
    acc_ref[...] += jnp.dot(taps_ref[2 - away], lines(other_ref, 0, cols), preferred_element_type=jnp.float32)
    outs = acc_ref.shape[0] // 9
    total = jnp.zeros((outs, NY * NZ), jnp.float32)
    for tap in range(9):
        b, c = divmod(tap, 3)
        total = total + shifted(acc_ref[tap * outs : (tap + 1) * outs, :], b - 1, c - 1)
    out_ref[...] = total.astype(jnp.bfloat16)


def exponent(value):
    top = jnp.max(jnp.max(jnp.abs(value), axis=1, keepdims=True), axis=0, keepdims=True)
    top = jnp.broadcast_to(jnp.maximum(top, 1e-30), (1, value.shape[1]))
    return jnp.floor(jnp.log(top) * (1.0 / LOG2))


def filter_kernel(
    spot_ref, mine_ref, other_ref, far_ref, corner_ref, c0_ref, c1_ref, c2_ref, c3_ref, out_ref, window_ref, spread_ref, acc_ref
):
    spot = spot_ref[0]
    core, side = spot % 2, spot // 2
    turn = 2 * core + side
    cols = mine_ref.shape[0]
    half, quarter = cols // 2, cols // 4
    edge = acc_ref.shape[1] * 2 // 3
    window_ref[1 + core, :edge, :] = lines(mine_ref, core * half, half)
    window_ref[2 - core, :edge, :] = lines(other_ref, core * half, half)
    window_ref[3 * core, :edge, :] = lines(mine_ref, core * half, half, True)
    window_ref[3 - 3 * core, :edge, :] = lines(other_ref, core * half, half, True)
    window_ref[spot, edge:, :] = lines(mine_ref, turn * quarter, quarter)
    window_ref[spot + 1 - 2 * core, edge:, :] = lines(other_ref, turn * quarter, quarter)
    inside = core + side == 1

    @pl.when(inside)
    def _():
        window_ref[2 - side, edge:, :] = lines(mine_ref, turn * quarter, quarter, True)
        window_ref[3 - 3 * side, edge:, :] = far_ref[...].reshape(far_ref.shape[0] * far_ref.shape[1], -1)

    @pl.when(jnp.logical_not(inside))
    def _():
        window_ref[2 - side, edge:, :] = lines(other_ref, turn * quarter, quarter, True)
        window_ref[3 - 3 * side, edge:, :] = corner_ref[...].reshape(far_ref.shape[0] * far_ref.shape[1], -1)

    for d, cot_ref in enumerate((c0_ref, c1_ref, c2_ref, c3_ref)):
        place = spot
        if d % 2:
            place = place + 1 - 2 * core
        if d // 2:
            place = place + 2 - 4 * side
        spread_taps(cot_ref, spread_ref)
        part = lax.dot_general(
            spread_ref[...], window_ref[place], (((1,), (1,)), ((), ())), preferred_element_type=jnp.float32
        )
        if d:
            acc_ref[...] += part
        else:
            acc_ref[...] = part
    value = acc_ref[...]
    level = exponent(value)
    factor = jnp.exp((TOP - level) * LOG2)
    blocks, rows, width = out_ref.shape
    rows = rows - EXTRA
    for block in range(blocks):
        out_ref[block, :rows, :] = acc_ref[block * rows : (block + 1) * rows, :] * factor
        out_ref[block, rows:, :] = jnp.broadcast_to(level, (EXTRA, width))


def sum_kernel(in_ref, out_ref):
    blocks, rows, width = in_ref.shape
    rows = rows - EXTRA
    total = jnp.zeros((rows, width), jnp.float32)
    for block in range(blocks):
        total = total + in_ref[block, :rows, :] * jnp.exp((in_ref[block, rows : rows + 1, :] - TOP) * LOG2)
    level = exponent(total)
    out_ref[:rows, :] = total * jnp.exp((TOP - level) * LOG2)
    out_ref[rows:, :] = jnp.broadcast_to(level, (EXTRA, width))


def join_kernel(scale, spot_ref, p0_ref, p1_ref, p2_ref, p3_ref, out_ref):
    spot = spot_ref[0]
    core, side = spot % 2, spot // 2
    blocks, rows, width = p0_ref.shape
    rows = rows - EXTRA
    quarter = width // 3
    half = 2 * quarter
    for d, piece_ref in enumerate((p0_ref, p1_ref, p2_ref, p3_ref)):
        its_core = 1 - core if d % 2 else core
        its_side = 1 - side if d // 2 else side
        wide = pl.ds(pl.multiple_of(its_core * half, half), half)
        fine = pl.ds(pl.multiple_of((2 * its_core + its_side) * quarter, quarter), quarter)
        for block in range(blocks):
            down = jnp.exp((piece_ref[block, rows : rows + 1, :] - TOP) * LOG2) * scale
            value = piece_ref[block, :rows, :] * down
            lines = slice(block * rows, (block + 1) * rows)
            out_ref[2 * its_side, lines, wide] = value[:, :half]
            out_ref[1, lines, fine] = value[:, half:]


def call(kernel, out, scratch, flops, *args):
    return pl.pallas_call(
        kernel,
        out_shape=out,
        in_specs=[SMEM if a.dtype == jnp.int32 else VMEM for a in args],
        out_specs=[VMEM] * len(out) if isinstance(out, list) else VMEM,
        scratch_shapes=scratch,
        compiler_params=pltpu.CompilerParams(vmem_limit_bytes=48 << 20),
        cost_estimate=pl.CostEstimate(
            flops=flops, transcendentals=0, bytes_accessed=sum(a.size * a.dtype.itemsize for a in args)
        ),
    )(*args)


def body(features, filters, cotangent):
    _, local, cells = features.shape
    devices = lax.axis_size("gz")
    cols = lax.axis_size("col")
    channels = local * cols
    quads = devices // 4
    half = channels // 2
    quarter = channels // 4
    size = 9 * local
    width = half + quarter
    flops = 2 * 27 * local * channels * cells
    bf16, f16, f32 = jnp.bfloat16, jnp.float16, jnp.float32
    spot = lax.axis_index("gz") % 4
    core, side = spot % 2, spot // 2
    spots = spot.reshape(1)
    x_own = features[0]
    c_own = cotangent[0]
    taps = filters.reshape(3, size, channels)

    def xor(value, bits):
        return lax.ppermute(value, "gz", [(i, i ^ bits) for i in range(devices)])

    outward = [(i, i + 1) for i in range(1, devices - 1, 2)] + [(i, i - 1) for i in range(2, devices, 2)]
    ring = [[4 * g + r for g in range(quads)] for r in range(4)]

    def everywhere(block, axis, groups=None):
        count = len(groups[0]) if groups else lax.axis_size(axis)
        copies = jnp.broadcast_to(block[None], (count,) + block.shape)
        return lax.all_to_all(copies, axis, 0, 0, axis_index_groups=groups, tiled=True)

    x_halo = lax.ppermute(x_own, "gz", outward)
    c_other = xor(c_own, 1)
    c_across = xor(c_own, 2)
    c_corner = xor(c_own, 3)
    c_halo = lax.ppermute(c_own, "gz", outward)
    x_halo, c_other, c_across, c_corner, c_halo = lax.optimization_barrier((x_halo, c_other, c_across, c_corner, c_halo))
    gathered = everywhere(jnp.concatenate([x_own, x_halo]), "col")
    other = xor(gathered, 1)

    def quarter_of(turn):
        return lax.dynamic_slice(gathered, (turn * (cols // 4), 0, 0), (cols // 4, local, cells))

    last = side
    straight = [(4 * g, 4 * g + 2) for g in range(quads)] + [(4 * g + 3, 4 * g + 1) for g in range(quads)]
    across = [(4 * g, 4 * g + 3) for g in range(quads)] + [(4 * g + 3, 4 * g) for g in range(quads)]
    far = lax.ppermute(quarter_of(jnp.where(last == 1, 2, 1)), "gz", straight)
    corner = lax.ppermute(quarter_of(jnp.where(last == 1, 0, 3)), "gz", across)

    grads = call(
        filter_kernel,
        jax.ShapeDtypeStruct((quads, size // quads + EXTRA, width), f32),
        [pltpu.VMEM((4, width, cells), bf16), pltpu.VMEM((size, cells), bf16), pltpu.VMEM((size, width), f32)],
        flops,
        spots,
        gathered,
        other,
        far,
        corner,
        c_own,
        c_other,
        c_across,
        c_corner,
    )
    grads, c_halo, other = lax.optimization_barrier((grads, c_halo, other))
    narrow = lax.all_to_all(grads.astype(f16), "gz", 0, 0, axis_index_groups=ring, tiled=True)

    partial = call(
        input_kernel,
        [jax.ShapeDtypeStruct((local, cells), f32)] * cols,
        [pltpu.VMEM((3, size, cells), bf16), pltpu.VMEM((channels, cells), f32)],
        flops,
        spots,
        lax.axis_index("col").reshape(1),
        c_halo,
        c_own,
        c_other,
        taps,
    )

    def exchanged(bits, value):
        return lax.ppermute(value, "col", [(j, j ^ bits) for j in range(cols)])

    early = cols // 2
    pieces = [partial[0]] + [exchanged(bits, partial[bits]) for bits in range(1, early)]
    output = call(
        output_kernel,
        jax.ShapeDtypeStruct((local, cells), bf16),
        [pltpu.VMEM((size, cells), f32)],
        flops,
        spots,
        gathered,
        other,
        taps,
    )

    narrow, output, pieces, late = lax.optimization_barrier((narrow, output, pieces, partial[early:]))
    pieces = pieces + [exchanged(early + i, value) for i, value in enumerate(late)]
    mine = call(
        sum_kernel,
        jax.ShapeDtypeStruct((size // quads + EXTRA, width), f32),
        [],
        0,
        narrow.astype(f32),
    )
    mine = everywhere(mine.astype(f16), "gz", ring)
    input_grad = sum(pieces[1:], pieces[0]).astype(bf16)
    mine, input_grad = lax.optimization_barrier((mine, input_grad))
    across = xor(mine, 2)
    beside = xor(mine, 1)
    corner = xor(across, 1)
    scale = float((cells * devices) ** -0.5)

    def kernel(*refs):
        join_kernel(scale, *refs)

    filter_grad = call(
        kernel,
        jax.ShapeDtypeStruct((3, size, channels), f32),
        [],
        0,
        spots,
        mine.astype(f32),
        beside.astype(f32),
        across.astype(f32),
        corner.astype(f32),
    )
    return output[None], input_grad[None], filter_grad.reshape(3, 3, 3, local, channels)


def solution(mesh):
    in_specs = (P("gz", "col", None), P(None, None, None, "col", None), P("gz", "col", None))
    out_specs = (P("gz", "col", None), P("gz", "col", None), P(None, None, None, "col", None))
    return jax.shard_map(body, mesh=mesh, in_specs=in_specs, out_specs=out_specs, check_vma=False)
```

time: 144 us -> 118 us (0.82)
  starting transfers between devices: 59.1 us -> 41.7 us
  other arithmetic: 14.3 us -> 3.64 us
  waiting for transfers between devices: 38.3 us -> 44 us
  local copies, waits for them, and re-layouts: 6.15 us -> 3.06 us
  Pallas kernels: 5.63 us -> 7.51 us
  between operations: 2.38 us -> 0.79 us
    all_to_all x5 -> x1, waiting for transfers between devices: 26.3 us -> 0.01 us  [everywhere(): lax.all_to_all(copies, axis, 0, 0, axis_index_groups=groups, tiled=True)]
    all_to_all x5 -> x1, starting transfers between devices: 27.3 us -> 3.48 us  [everywhere(): lax.all_to_all(copies, axis, 0, 0, axis_index_groups=groups, tiled=True)]
    ppermute x0 -> x9, waiting for transfers between devices: none -> 19.9 us  [the longest x7 13 us: exchanged(): return lax.ppermute(value, 'col', [(j, j ^ bits) for j in range(cols)])]
    ppermute x0 -> x9, starting transfers between devices: none -> 11.3 us  [the longest x7 9.37 us: exchanged(): return lax.ppermute(value, 'col', [(j, j ^ bits) for j in range(cols)])]
    ppermute x6 -> x7, waiting for transfers between devices: 7.32 us -> 16.5 us  [xor(): return lax.ppermute(value, 'gz', [(i, i ^ bits) for i in range(devices)])]
    ppermute x6 -> x7, starting transfers between devices: 18.3 us -> 9.39 us  [xor(): return lax.ppermute(value, 'gz', [(i, i ^ bits) for i in range(devices)])]
    all_to_all x1, waiting for transfers between devices: 0.01 us -> 5.5 us  [body(): lax.all_to_all(grads.astype(f16), 'gz', 0, 0, axis_index_groups=ring, til...]
    all_to_all x1, starting transfers between devices: 4.25 us -> 9.21 us  [body(): lax.all_to_all(grads.astype(f16), 'gz', 0, 0, axis_index_groups=ring, til...]
  transfers between devices with their start and end apart: 14 -> 20, of which waited for: 6 -> 13; matrix products, arithmetic and copies ran while one was open for 8% -> 2% of each run, Pallas kernels for 3% -> 3%
where the time goes in v2:
time: 118 us; the launch traced here: 117 us
  waiting for transfers between devices  44 us (37%)
  starting transfers between devices  41.7 us (35%)
  blocking collectives  16.7 us (14%)
  Pallas kernels  7.51 us (6%)
  other arithmetic  3.64 us (3%)
  local copies, waits for them, and re-layouts  3.06 us (3%)
    all_to_all x1, blocking collectives, everywhere(): lax.all_to_all(copies, axis, 0, 0, axis_index_groups=groups, tiled=True)  16.7 us
    ppermute x7, waiting for transfers between devices, xor(): return lax.ppermute(value, 'gz', [(i, i ^ bits) for i in range(devices)])  16.5 us
    ppermute x7, waiting for transfers between devices, exchanged(): return lax.ppermute(value, 'col', [(j, j ^ bits) for j in range(cols)])  13 us
    ppermute x7, starting transfers between devices, xor(): return lax.ppermute(value, 'gz', [(i, i ^ bits) for i in range(devices)])  9.39 us
    ppermute x7, starting transfers between devices, exchanged(): return lax.ppermute(value, 'col', [(j, j ^ bits) for j in range(cols)])  9.37 us
    all_to_all x1, starting transfers between devices, body(): lax.all_to_all(grads.astype(f16), 'gz', 0, 0, axis_index_groups=ring, til...  9.21 us
    pallas_call x5, Pallas kernels, call(): pl.pallas_call(kernel, out_shape=out, in_specs=[SMEM if a.dtype == jnp.in...  7.51 us
    ppermute x1, waiting for transfers between devices, body(): far = lax.ppermute(quarter_of(jnp.where(last == 1, 2, 1)), 'gz', straight)  6.87 us
  transfers between devices with their start and end apart: 20, of which 13 were waited for; matrix products, arithmetic and copies ran while one was open for 2% of the time, Pallas kernels for 3%

profile of v2, /device:TPU:1, one launch (start us, length us, event | category | flops | bytes accessed | tf_op | source)
XLA Modules:
  0.0 117.5 jit_solution(2732862507841851481)
XLA Ops:
  0.6 6.3 %collective-permute-start = (bf16[64,512]{1,0:T(8,128)(2,1)}, bf16[64,512]{1,0:T(8,128)(2,1)S(1)}, u32[]{:S(2)}, u32[]{:S(2)}) collective-permute-start(bf16[64,512]{1,0:T(8,128)(2,1)} %bitcast.19), channel_id=1, source_target_pairs={{8,16},{24,32},{40,48},{56,64},{72,80},{88,96},{104,112},{120,128}... | collective-permute-start | bytes 196616 | tf_op jit(solution)/shard_map/ppermute | solution.py:216
  7.0 1.9 %collective-permute-start.4 = (bf16[64,512]{1,0:T(8,128)(2,1)}, bf16[64,512]{1,0:T(8,128)(2,1)S(1)}, u32[]{:S(2)}, u32[]{:S(2)}) collective-permute-start(bf16[64,512]{1,0:T(8,128)(2,1)} %bitcast.10), channel_id=1, source_target_pairs={{8,16},{24,32},{40,48},{56,64},{72,80},{88,96},{104,112},{120,128}... | collective-permute-start | bytes 196616 | tf_op jit(solution)/shard_map/ppermute | solution.py:220
  8.9 3.3 %collective-permute-start.3 = (bf16[64,512]{1,0:T(8,128)(2,1)}, bf16[64,512]{1,0:T(8,128)(2,1)S(1)}, u32[]{:S(2)}, u32[]{:S(2)}) collective-permute-start(bf16[64,512]{1,0:T(8,128)(2,1)} %bitcast.11), channel_id=1, source_target_pairs={{0,24},{8,16},{16,8},{24,0},{32,56},{40,48},{48,40},{56,32},{64,88... | collective-permute-start | bytes 196616 | tf_op jit(solution)/shard_map/ppermute | solution.py:206
  12.2 0.4 collective-permute-start.2
  12.7 0.3 collective-permute-start.1
  13.0 2.1 %collective-permute-done.4.halo_ref = bf16[64,512]{1,0:T(8,128)(2,1)S(1)} collective-permute-done((bf16[64,512]{1,0:T(8,128)(2,1)}, bf16[64,512]{1,0:T(8,128)(2,1)S(1)}, u32[]{:S(2)}, u32[]{:S(2)}) %collective-permute-start.4) | collective-permute-done | bytes 65568 | tf_op jit(solution)/shard_map/ppermute | solution.py:220
  15.1 0.6 collective-permute-done.3.c3_ref
  15.7 1.4 %collective-permute-done.2.c2_ref = bf16[64,512]{1,0:T(8,128)(2,1)S(1)} collective-permute-done((bf16[64,512]{1,0:T(8,128)(2,1)}, bf16[64,512]{1,0:T(8,128)(2,1)S(1)}, u32[]{:S(2)}, u32[]{:S(2)}) %collective-permute-start.2) | collective-permute-done | bytes 65568 | tf_op jit(solution)/shard_map/ppermute | solution.py:206
  17.1 0.8 pad_maximum_fusion
  17.9 0.1 broadcast_in_dim.8
  18.0 16.7 %all_to_all.15.mine_ref = bf16[8,128,512]{2,1,0:T(8,128)(2,1)S(1)} all-to-all(bf16[8,128,512]{2,1,0:T(8,128)(2,1)S(1)} %broadcast_in_dim.8), channel_id=1, replica_groups=mesh['gz'=32,'col'=8] {'col'}, dimensions={0} | all-to-all | bytes 2097152 | tf_op jit(solution)/shard_map/all_to_all | solution.py:214
  34.8 3.5 %collective-permute-start.5 = (bf16[8,128,512]{2,1,0:T(8,128)(2,1)S(1)}, bf16[8,128,512]{2,1,0:T(8,128)(2,1)S(1)}, u32[]{:S(2)}, u32[]{:S(2)}) collective-permute-start(bf16[8,128,512]{2,1,0:T(8,128)(2,1)S(1)} %all_to_all.15.mine_ref), channel_id=1, source_target_pairs={{0,8},{8,0},{16,24},{24,16},{32,40},{40,32},{48,56},{56,48},{64,72... | collective-permute-start | bytes 3145736 | tf_op jit(solution)/shard_map/ppermute | solution.py:206
  38.3 0.7 collective-permute-start.7
  39.0 1.3 %collective-permute-start.6 = (bf16[2,64,512]{2,1,0:T(8,128)(2,1)S(1)}, bf16[2,64,512]{2,1,0:T(8,128)(2,1)S(1)}, u32[]{:S(2)}, u32[]{:S(2)}) collective-permute-start(bf16[2,64,512]{2,1,0:T(8,128)(2,1)S(1)} %get-tuple-element.60), channel_id=1, source_target_pairs={{0,16},{32,48},{64,80},{96,112},{128,144},{160,176},{192,208},{224... | collective-permute-start | bytes 393224 | tf_op jit(solution)/shard_map/ppermute | solution.py:231
  40.3 6.9 %collective-permute-done.6.far_ref = bf16[2,64,512]{2,1,0:T(8,128)(2,1)S(1)} collective-permute-done((bf16[2,64,512]{2,1,0:T(8,128)(2,1)S(1)}, bf16[2,64,512]{2,1,0:T(8,128)(2,1)S(1)}, u32[]{:S(2)}, u32[]{:S(2)}) %collective-permute-start.6) | collective-permute-done | bytes 131104 | tf_op jit(solution)/shard_map/ppermute | solution.py:231
  47.1 1.7 %shard_map.58 = f32[8,80,384]{2,1,0:T(8,128)S(1)} custom-call(s32[1]{0:T(128)} %bitcast.spot_ref.refs_0_, bf16[8,128,512]{2,1,0:T(8,128)(2,1)S(1)} %all_to_all.15.mine_ref, bf16[8,128,512]{2,1,0:T(8,128)(2,1)S(1)} %collective-permute-done.5.other_ref, bf16[2,64,512]{2,1,0:T(8,128)(2,1)S(1)} %collective-permute-done.6.far_ref, ...), custom_call_target="tpu_custom_call" | custom-call | flops 905969664 | bytes 2621444 | tf_op jit(solution)/shard_map/pallas_call | solution.py:173
  48.9 0.8 convert_element_type.24
  49.7 9.2 %all-to-all-start.1 = ((f16[8,80,384]{2,1,0:T(8,128)(2,1)}), f16[8,80,384]{2,1,0:T(8,128)(2,1)S(1)}, u32[]{:S(2)}, u32[]{:S(2)}) async-start(f16[8,80,384]{2,1,0:T(8,128)(2,1)} %convert_element_type.24), calls=%async_computation.1 | async-start | bytes 983040 | tf_op jit(solution)/shard_map/all_to_all | solution.py:250
  58.9 1.5 %copy-done = bf16[3,3,3,64,512]{4,3,2,1,0:T(8,128)(2,1)S(1)} copy-done((bf16[3,3,3,64,512]{4,3,2,1,0:T(8,128)(2,1)S(1)}, bf16[3,3,3,64,512]{4,3,2,1,0:T(8,128)(2,1)}, u32[]{:S(2)}) %copy-start) | copy-done | bytes 1769496
  60.4 1.6 %shard_map.60 = (f32[64,512]{1,0:T(8,128)S(1)}, f32[64,512]{1,0:T(8,128)S(1)}, f32[64,512]{1,0:T(8,128)S(1)}, f32[64,512]{1,0:T(8,128)S(1)}, f32[64,512]{1,0:T(8...) custom-call(s32[1]{0:T(128)} %bitcast.spot_ref.refs_0_, s32[1]{0:T(128)} %bitcast.4.col_ref, ...), custom_call_target="tpu_custom_call" | custom-call | flops 905969664 | bytes 1966088 | tf_op jit(solution)/shard_map/pallas_call | solution.py:173
  62.0 1.0 collective-permute-start.8
  63.0 0.4 collective-permute-start.9
  63.4 1.3 %collective-permute-start.10 = (f32[64,512]{1,0:T(8,128)S(1)}, f32[64,512]{1,0:T(8,128)}, u32[]{:S(2)}, u32[]{:S(2)}) collective-permute-start(f32[64,512]{1,0:T(8,128)S(1)} %get-tuple-element.42), channel_id=1, source_target_pairs={{0,3},{1,2},{2,1},{3,0},{4,7},{5,6},{6,5},{7,4},{8,11},{9,10},{10,... | collective-permute-start | bytes 393224 | tf_op jit(solution)/shard_map/ppermute | solution.py:266
  64.7 1.9 %shard_map.59 = bf16[64,512]{1,0:T(8,128)(2,1)} custom-call(s32[1]{0:T(128)} %bitcast.spot_ref.refs_0_, bf16[8,128,512]{2,1,0:T(8,128)(2,1)S(1)} %all_to_all.15.mine_ref, bf16[8,128,512]{2,1,0:T(8,128)(2,1)S(1)} %collective-permute-done.5.other_ref, bf16[3,576,512]{2,1,0:T(8,128)(2,1)S(1)} %bitcast.9), custom_call_target="tpu_custom_call" | custom-call | flops 905969664 | bytes 3866628 | tf_op jit(solution)/shard_map/pallas_call | solution.py:173
  66.6 0.4 collective-permute-done.8
  67.0 1.1 collective-permute-done.9
  68.1 0.6 copy-done.4
  68.7 2.0 %collective-permute-done.10 = f32[64,512]{1,0:T(8,128)} collective-permute-done((f32[64,512]{1,0:T(8,128)S(1)}, f32[64,512]{1,0:T(8,128)}, u32[]{:S(2)}, u32[]{:S(2)}) %collective-permute-start.10) | collective-permute-done | bytes 131104 | tf_op jit(solution)/shard_map/ppermute | solution.py:266
  70.8 5.5 %all-to-all-done.1 = f16[8,80,384]{2,1,0:T(8,128)(2,1)S(1)} async-done(((f16[8,80,384]{2,1,0:T(8,128)(2,1)}), f16[8,80,384]{2,1,0:T(8,128)(2,1)S(1)}, u32[]{:S(2)}, u32[]{:S(2)}) %all-to-all-start.1) | async-done | bytes 491552 | tf_op jit(solution)/shard_map/all_to_all | solution.py:250
  76.3 0.1 convert_element_type.25.in_ref
  76.3 0.2 shard_map.61
  76.5 0.8 broadcast_in_dim.20
  77.4 3.5 %all-to-all-start.2 = ((f16[8,80,384]{2,1,0:T(8,128)(2,1)}), f16[8,80,384]{2,1,0:T(8,128)(2,1)S(1)}, u32[]{:S(2)}, u32[]{:S(2)}) async-start(f16[8,80,384]{2,1,0:T(8,128)(2,1)} %broadcast_in_dim.20), calls=%async_computation.2 | async-start | bytes 983040 | tf_op jit(solution)/shard_map/all_to_all | solution.py:214
  80.9 1.4 %collective-permute-start.11 = (f32[64,512]{1,0:T(8,128)S(1)}, f32[64,512]{1,0:T(8,128)S(1)}, u32[]{:S(2)}, u32[]{:S(2)}) collective-permute-start(f32[64,512]{1,0:T(8,128)S(1)} %get-tuple-element.53), channel_id=1, source_target_pairs={{0,4},{1,5},{2,6},{3,7},{4,0},{5,1},{6,2},{7,3},{8,12},{9,13},{10,... | collective-permute-start | bytes 393224 | tf_op jit(solution)/shard_map/ppermute | solution.py:266
  82.2 2.4 %collective-permute-start.12 = (f32[64,512]{1,0:T(8,128)S(1)}, f32[64,512]{1,0:T(8,128)S(1)}, u32[]{:S(2)}, u32[]{:S(2)}) collective-permute-start(f32[64,512]{1,0:T(8,128)S(1)} %get-tuple-element.54), channel_id=1, source_target_pairs={{0,5},{1,4},{2,7},{3,6},{4,1},{5,0},{6,3},{7,2},{8,13},{9,12},{10,... | collective-permute-start | bytes 393224 | tf_op jit(solution)/shard_map/ppermute | solution.py:266
  84.6 0.9 collective-permute-start.13
  85.5 2.0 %collective-permute-start.14 = (f32[64,512]{1,0:T(8,128)S(1)}, f32[64,512]{1,0:T(8,128)S(1)}, u32[]{:S(2)}, u32[]{:S(2)}) collective-permute-start(f32[64,512]{1,0:T(8,128)S(1)} %get-tuple-element.56), channel_id=1, source_target_pairs={{0,7},{1,6},{2,5},{3,4},{4,3},{5,2},{6,1},{7,0},{8,15},{9,14},{10,... | collective-permute-start | bytes 393224 | tf_op jit(solution)/shard_map/ppermute | solution.py:266
  87.5 3.2 %collective-permute-done.12 = f32[64,512]{1,0:T(8,128)S(1)} collective-permute-done((f32[64,512]{1,0:T(8,128)S(1)}, f32[64,512]{1,0:T(8,128)S(1)}, u32[]{:S(2)}, u32[]{:S(2)}) %collective-permute-start.12) | collective-permute-done | bytes 131104 | tf_op jit(solution)/shard_map/ppermute | solution.py:266
  90.7 2.8 %collective-permute-done.13 = f32[64,512]{1,0:T(8,128)S(1)} collective-permute-done((f32[64,512]{1,0:T(8,128)S(1)}, f32[64,512]{1,0:T(8,128)S(1)}, u32[]{:S(2)}, u32[]{:S(2)}) %collective-permute-start.13) | collective-permute-done | bytes 131104 | tf_op jit(solution)/shard_map/ppermute | solution.py:266
  93.5 3.5 %collective-permute-done.14 = f32[64,512]{1,0:T(8,128)S(1)} collective-permute-done((f32[64,512]{1,0:T(8,128)S(1)}, f32[64,512]{1,0:T(8,128)S(1)}, u32[]{:S(2)}, u32[]{:S(2)}) %collective-permute-start.14) | collective-permute-done | bytes 131104 | tf_op jit(solution)/shard_map/ppermute | solution.py:266
  97.0 1.6 %add_convert_fusion = bf16[64,512]{1,0:T(8,128)(2,1)} fusion(f32[64,512]{1,0:T(8,128)S(1)} %collective-permute-done.14, f32[64,512]{1,0:T(8,128)S(1)} %collective-permute-done.13, f32[64,512]{1,0:T(8,128)S(1)} %collective-permute-done.12, f32[64,512]{1,0:T(8,128)S(1)} %collective-permute-done.11, f32[64,512]{1,0:T(8,128)} %collective-permute-done.10, ...), kind=kLoop, calls=%fused_computation.1 | loop fusion | flops 262144 | bytes 1114112 | tf_op jit(solution)/shard_map/convert_element_type | solution.py:291
  98.6 0.5 collective-permute-start.15
  99.1 13.3 %collective-permute-done.16 = f16[8,80,384]{2,1,0:T(8,128)(2,1)S(1)} collective-permute-done((f16[8,80,384]{2,1,0:T(8,128)(2,1)S(1)}, f16[8,80,384]{2,1,0:T(8,128)(2,1)S(1)}, u32[]{:S(2)}, u32[]{:S(2)}) %collective-permute-start.16) | collective-permute-done | bytes 491552 | tf_op jit(solution)/shard_map/ppermute | solution.py:206
  112.4 1.3 %collective-permute-start.17 = (f16[8,80,384]{2,1,0:T(8,128)(2,1)S(1)}, f16[8,80,384]{2,1,0:T(8,128)(2,1)S(1)}, u32[]{:S(2)}, u32[]{:S(2)}) collective-permute-start(f16[8,80,384]{2,1,0:T(8,128)(2,1)S(1)} %collective-permute-done.16), channel_id=1, source_target_pairs={{0,8},{8,0},{16,24},{24,16},{32,40},{40,32},{48,56},{56,48},{64,72... | collective-permute-start | bytes 1474568 | tf_op jit(solution)/shard_map/ppermute | solution.py:206
  113.8 0.1 convert_element_type.30.refs_3_
  113.9 0.1 convert_element_type.29.refs_2_
  114.0 1.3 %collective-permute-done.17 = f16[8,80,384]{2,1,0:T(8,128)(2,1)S(1)} collective-permute-done((f16[8,80,384]{2,1,0:T(8,128)(2,1)S(1)}, f16[8,80,384]{2,1,0:T(8,128)(2,1)S(1)}, u32[]{:S(2)}, u32[]{:S(2)}) %collective-permute-start.17) | collective-permute-done | bytes 491552 | tf_op jit(solution)/shard_map/ppermute | solution.py:206
  115.3 2.2 %shard_map.62 = f32[3,576,512]{2,1,0:T(8,128)} custom-call(s32[1]{0:T(128)} %bitcast.spot_ref.refs_0_, f32[8,80,384]{2,1,0:T(8,128)S(1)} %convert_element_type.28.refs_1_, f32[8,80,384]{2,1,0:T(8,128)S(1)} %convert_element_type.29.refs_2_, f32[8,80,384]{2,1,0:T(8,128)S(1)} %convert_element_type.30.refs_3_, f32[8,80,384]{2,1,0:T(8,128)S(1)} %convert_element_type.31.refs_4_), custom_call_target="tpu_custom_call" | custom-call | bytes 3932164 | tf_op jit(solution)/shard_map/pallas_call | solution.py:173
  (22 shorter events, 0.2 us)
Async XLA Ops:
  0.6 46.5 %copy-start.1 = (bf16[1,64,512]{2,1,0:T(8,128)(2,1)S(1)}, bf16[1,64,512]{2,1,0:T(8,128)(2,1)}, u32[]{:S(2)}) copy-start(bf16[1,64,512]{2,1,0:T(8,128)(2,1)} %param.5) | copy-start | bytes 196612
  0.6 12.3 %collective-permute-start = (bf16[64,512]{1,0:T(8,128)(2,1)}, bf16[64,512]{1,0:T(8,128)(2,1)S(1)}, u32[]{:S(2)}, u32[]{:S(2)}) collective-permute-start(bf16[64,512]{1,0:T(8,128)(2,1)} %bitcast.19), channel_id=1, source_target_pairs={{8,16},{24,32},{40,48},{56,64},{72,80},{88,96},{104,112},{120,128}... | collective-permute-start | bytes 196616 | tf_op jit(solution)/shard_map/ppermute | solution.py:216
  7.0 8.1 %collective-permute-start.4 = (bf16[64,512]{1,0:T(8,128)(2,1)}, bf16[64,512]{1,0:T(8,128)(2,1)S(1)}, u32[]{:S(2)}, u32[]{:S(2)}) collective-permute-start(bf16[64,512]{1,0:T(8,128)(2,1)} %bitcast.10), channel_id=1, source_target_pairs={{8,16},{24,32},{40,48},{56,64},{72,80},{88,96},{104,112},{120,128}... | collective-permute-start | bytes 196616 | tf_op jit(solution)/shard_map/ppermute | solution.py:220
  8.9 6.8 %collective-permute-start.3 = (bf16[64,512]{1,0:T(8,128)(2,1)}, bf16[64,512]{1,0:T(8,128)(2,1)S(1)}, u32[]{:S(2)}, u32[]{:S(2)}) collective-permute-start(bf16[64,512]{1,0:T(8,128)(2,1)} %bitcast.11), channel_id=1, source_target_pairs={{0,24},{8,16},{16,8},{24,0},{32,56},{40,48},{48,40},{56,32},{64,88... | collective-permute-start | bytes 196616 | tf_op jit(solution)/shard_map/ppermute | solution.py:206
  12.2 4.8 %collective-permute-start.2 = (bf16[64,512]{1,0:T(8,128)(2,1)}, bf16[64,512]{1,0:T(8,128)(2,1)S(1)}, u32[]{:S(2)}, u32[]{:S(2)}) collective-permute-start(bf16[64,512]{1,0:T(8,128)(2,1)} %bitcast.12), channel_id=1, source_target_pairs={{0,16},{8,24},{16,0},{24,8},{32,48},{40,56},{48,32},{56,40},{64,80... | collective-permute-start | bytes 196616 | tf_op jit(solution)/shard_map/ppermute | solution.py:206
  12.7 4.4 %collective-permute-start.1 = (bf16[64,512]{1,0:T(8,128)(2,1)}, bf16[64,512]{1,0:T(8,128)(2,1)S(1)}, u32[]{:S(2)}, u32[]{:S(2)}) collective-permute-start(bf16[64,512]{1,0:T(8,128)(2,1)} %bitcast.13), channel_id=1, source_target_pairs={{0,8},{8,0},{16,24},{24,16},{32,40},{40,32},{48,56},{56,48},{64,72... | collective-permute-start | bytes 196616 | tf_op jit(solution)/shard_map/ppermute | solution.py:206
  34.8 12.4 %collective-permute-start.5 = (bf16[8,128,512]{2,1,0:T(8,128)(2,1)S(1)}, bf16[8,128,512]{2,1,0:T(8,128)(2,1)S(1)}, u32[]{:S(2)}, u32[]{:S(2)}) collective-permute-start(bf16[8,128,512]{2,1,0:T(8,128)(2,1)S(1)} %all_to_all.15.mine_ref), channel_id=1, source_target_pairs={{0,8},{8,0},{16,24},{24,16},{32,40},{40,32},{48,56},{56,48},{64,72... | collective-permute-start | bytes 3145736 | tf_op jit(solution)/shard_map/ppermute | solution.py:206
  38.3 2.0 %collective-permute-start.7 = (bf16[2,64,512]{2,1,0:T(8,128)(2,1)S(1)}, bf16[2,64,512]{2,1,0:T(8,128)(2,1)S(1)}, u32[]{:S(2)}, u32[]{:S(2)}) collective-permute-start(bf16[2,64,512]{2,1,0:T(8,128)(2,1)S(1)} %get-tuple-element.59), channel_id=1, source_target_pairs={{0,24},{32,56},{64,88},{96,120},{128,152},{160,184},{192,216},{224... | collective-permute-start | bytes 393224 | tf_op jit(solution)/shard_map/ppermute | solution.py:232
  39.0 8.2 %collective-permute-start.6 = (bf16[2,64,512]{2,1,0:T(8,128)(2,1)S(1)}, bf16[2,64,512]{2,1,0:T(8,128)(2,1)S(1)}, u32[]{:S(2)}, u32[]{:S(2)}) collective-permute-start(bf16[2,64,512]{2,1,0:T(8,128)(2,1)S(1)} %get-tuple-element.60), channel_id=1, source_target_pairs={{0,16},{32,48},{64,80},{96,112},{128,144},{160,176},{192,208},{224... | collective-permute-start | bytes 393224 | tf_op jit(solution)/shard_map/ppermute | solution.py:231
  49.7 26.6 %all-to-all-start.1 = ((f16[8,80,384]{2,1,0:T(8,128)(2,1)}), f16[8,80,384]{2,1,0:T(8,128)(2,1)S(1)}, u32[]{:S(2)}, u32[]{:S(2)}) async-start(f16[8,80,384]{2,1,0:T(8,128)(2,1)} %convert_element_type.24), calls=%async_computation.1 | async-start | bytes 983040 | tf_op jit(solution)/shard_map/all_to_all | solution.py:250
  58.9 1.5 %copy-start = (bf16[3,3,3,64,512]{4,3,2,1,0:T(8,128)(2,1)S(1)}, bf16[3,3,3,64,512]{4,3,2,1,0:T(8,128)(2,1)}, u32[]{:S(2)}) copy-start(bf16[3,3,3,64,512]{4,3,2,1,0:T(8,128)(2,1)} %param.4) | copy-start | bytes 5308420
  62.0 5.0 %collective-permute-start.8 = (f32[64,512]{1,0:T(8,128)S(1)}, f32[64,512]{1,0:T(8,128)S(1)}, u32[]{:S(2)}, u32[]{:S(2)}) collective-permute-start(f32[64,512]{1,0:T(8,128)S(1)} %get-tuple-element.40), channel_id=1, source_target_pairs={{0,1},{1,0},{2,3},{3,2},{4,5},{5,4},{6,7},{7,6},{8,9},{9,8},{10,11... | collective-permute-start | bytes 393224 | tf_op jit(solution)/shard_map/ppermute | solution.py:266
  63.0 5.1 %collective-permute-start.9 = (f32[64,512]{1,0:T(8,128)S(1)}, f32[64,512]{1,0:T(8,128)S(1)}, u32[]{:S(2)}, u32[]{:S(2)}) collective-permute-start(f32[64,512]{1,0:T(8,128)S(1)} %get-tuple-element.41), channel_id=1, source_target_pairs={{0,2},{1,3},{2,0},{3,1},{4,6},{5,7},{6,4},{7,5},{8,10},{9,11},{10,... | collective-permute-start | bytes 393224 | tf_op jit(solution)/shard_map/ppermute | solution.py:266
  63.4 7.4 %collective-permute-start.10 = (f32[64,512]{1,0:T(8,128)S(1)}, f32[64,512]{1,0:T(8,128)}, u32[]{:S(2)}, u32[]{:S(2)}) collective-permute-start(f32[64,512]{1,0:T(8,128)S(1)} %get-tuple-element.42), channel_id=1, source_target_pairs={{0,3},{1,2},{2,1},{3,0},{4,7},{5,6},{6,5},{7,4},{8,11},{9,10},{10,... | collective-permute-start | bytes 393224 | tf_op jit(solution)/shard_map/ppermute | solution.py:266
  67.0 9.3 %copy-start.2 = (f32[64,512]{1,0:T(8,128)}, f32[64,512]{1,0:T(8,128)S(1)}, u32[]{:S(2)}) copy-start(f32[64,512]{1,0:T(8,128)S(1)} %collective-permute-done.8) | copy-start | bytes 393220
  68.1 0.6 copy-start.4
  70.8 26.2 %copy-start.5 = (f32[64,512]{1,0:T(8,128)S(1)}, f32[64,512]{1,0:T(8,128)}, u32[]{:S(2)}) copy-start(f32[64,512]{1,0:T(8,128)} %copy-done.4) | copy-start | bytes 393220
  76.3 20.7 %copy-start.3 = (f32[64,512]{1,0:T(8,128)S(1)}, f32[64,512]{1,0:T(8,128)}, u32[]{:S(2)}) copy-start(f32[64,512]{1,0:T(8,128)} %copy-done.2) | copy-start | bytes 393220
  77.4 21.2 %all-to-all-start.2 = ((f16[8,80,384]{2,1,0:T(8,128)(2,1)}), f16[8,80,384]{2,1,0:T(8,128)(2,1)S(1)}, u32[]{:S(2)}, u32[]{:S(2)}) async-start(f16[8,80,384]{2,1,0:T(8,128)(2,1)} %broadcast_in_dim.20), calls=%async_computation.2 | async-start | bytes 983040 | tf_op jit(solution)/shard_map/all_to_all | solution.py:214
  80.9 6.6 %collective-permute-start.11 = (f32[64,512]{1,0:T(8,128)S(1)}, f32[64,512]{1,0:T(8,128)S(1)}, u32[]{:S(2)}, u32[]{:S(2)}) collective-permute-start(f32[64,512]{1,0:T(8,128)S(1)} %get-tuple-element.53), channel_id=1, source_target_pairs={{0,4},{1,5},{2,6},{3,7},{4,0},{5,1},{6,2},{7,3},{8,12},{9,13},{10,... | collective-permute-start | bytes 393224 | tf_op jit(solution)/shard_map/ppermute | solution.py:266
  82.2 8.4 %collective-permute-start.12 = (f32[64,512]{1,0:T(8,128)S(1)}, f32[64,512]{1,0:T(8,128)S(1)}, u32[]{:S(2)}, u32[]{:S(2)}) collective-permute-start(f32[64,512]{1,0:T(8,128)S(1)} %get-tuple-element.54), channel_id=1, source_target_pairs={{0,5},{1,4},{2,7},{3,6},{4,1},{5,0},{6,3},{7,2},{8,13},{9,12},{10,... | collective-permute-start | bytes 393224 | tf_op jit(solution)/shard_map/ppermute | solution.py:266
  84.6 8.9 %collective-permute-start.13 = (f32[64,512]{1,0:T(8,128)S(1)}, f32[64,512]{1,0:T(8,128)S(1)}, u32[]{:S(2)}, u32[]{:S(2)}) collective-permute-start(f32[64,512]{1,0:T(8,128)S(1)} %get-tuple-element.55), channel_id=1, source_target_pairs={{0,6},{1,7},{2,4},{3,5},{4,2},{5,3},{6,0},{7,1},{8,14},{9,15},{10,... | collective-permute-start | bytes 393224 | tf_op jit(solution)/shard_map/ppermute | solution.py:266
  85.5 11.5 %collective-permute-start.14 = (f32[64,512]{1,0:T(8,128)S(1)}, f32[64,512]{1,0:T(8,128)S(1)}, u32[]{:S(2)}, u32[]{:S(2)}) collective-permute-start(f32[64,512]{1,0:T(8,128)S(1)} %get-tuple-element.56), channel_id=1, source_target_pairs={{0,7},{1,6},{2,5},{3,4},{4,3},{5,2},{6,1},{7,0},{8,15},{9,14},{10,... | collective-permute-start | bytes 393224 | tf_op jit(solution)/shard_map/ppermute | solution.py:266
  98.6 13.8 %collective-permute-start.16 = (f16[8,80,384]{2,1,0:T(8,128)(2,1)S(1)}, f16[8,80,384]{2,1,0:T(8,128)(2,1)S(1)}, u32[]{:S(2)}, u32[]{:S(2)}) collective-permute-start(f16[8,80,384]{2,1,0:T(8,128)(2,1)S(1)} %all-to-all-done.2), channel_id=1, source_target_pairs={{0,16},{8,24},{16,0},{24,8},{32,48},{40,56},{48,32},{56,40},{64,80... | collective-permute-start | bytes 1474568 | tf_op jit(solution)/shard_map/ppermute | solution.py:206
  98.6 15.3 %collective-permute-start.15 = (f16[8,80,384]{2,1,0:T(8,128)(2,1)S(1)}, f16[8,80,384]{2,1,0:T(8,128)(2,1)S(1)}, u32[]{:S(2)}, u32[]{:S(2)}) collective-permute-start(f16[8,80,384]{2,1,0:T(8,128)(2,1)S(1)} %all-to-all-done.2), channel_id=1, source_target_pairs={{0,8},{8,0},{16,24},{24,16},{32,40},{40,32},{48,56},{56,48},{64,72... | collective-permute-start | bytes 1474568 | tf_op jit(solution)/shard_map/ppermute | solution.py:206
  112.4 2.8 %collective-permute-start.17 = (f16[8,80,384]{2,1,0:T(8,128)(2,1)S(1)}, f16[8,80,384]{2,1,0:T(8,128)(2,1)S(1)}, u32[]{:S(2)}, u32[]{:S(2)}) collective-permute-start(f16[8,80,384]{2,1,0:T(8,128)(2,1)S(1)} %collective-permute-done.16), channel_id=1, source_target_pairs={{0,8},{8,0},{16,24},{24,16},{32,40},{40,32},{48,56},{56,48},{64,72... | collective-permute-start | bytes 1474568 | tf_op jit(solution)/shard_map/ppermute | solution.py:206

commit v3 on v2

v3 whole, which is shorter than its diff:
```python
import jax
import jax.numpy as jnp
from jax import lax
from jax.experimental import pallas as pl
from jax.experimental.pallas import tpu as pltpu
from jax.sharding import PartitionSpec as P

NY = 32
NZ = 16
VMEM = pl.BlockSpec(memory_space=pltpu.VMEM)
SMEM = pl.BlockSpec(memory_space=pltpu.SMEM)
LOG2 = 0.6931471805599453
TOP = 13.0
EXTRA = 8
LANES = 128


def shifted(value, down, right):
    cells = NY * NZ
    step = down * NZ + right
    if step:
        value = pltpu.roll(value, (-step) % cells, 1)
    cell = lax.broadcasted_iota(jnp.int32, value.shape, 1)
    row, col = cell // NZ, cell % NZ
    if down == 1:
        value = jnp.where(row < NY - 1, value, 0.0)
    if down == -1:
        value = jnp.where(row > 0, value, 0.0)
    if right == 1:
        value = jnp.where(col < NZ - 1, value, 0.0)
    if right == -1:
        value = jnp.where(col > 0, value, 0.0)
    return value


def spread_taps(cot_ref, out_ref):
    outs = cot_ref.shape[0]
    wide = cot_ref[...].astype(jnp.float32)
    for tap in range(9):
        b, c = divmod(tap, 3)
        out_ref[tap * outs : (tap + 1) * outs, :] = shifted(wide, 1 - b, 1 - c).astype(jnp.bfloat16)


def lines(ref, first, count, beyond=False):
    _, both, cells = ref.shape
    local = both // 2
    start = local if beyond else 0
    return ref[pl.ds(first, count), start : start + local, :].reshape(count * local, cells)


def pack_kernel(x_ref, c_ref, beyond_ref, across_ref, send_ref, here_ref):
    blocks, both, _ = send_ref.shape
    local = both // 2
    for block in range(blocks):
        send_ref[block, :local, :] = x_ref[...]
        send_ref[block, local:, :] = beyond_ref[0]
    here_ref[0] = c_ref[...]
    here_ref[1] = beyond_ref[1]
    here_ref[2] = across_ref[...]


def input_kernel(info_ref, here_ref, there_ref, taps_ref, give_ref, keep_ref, spread_ref, acc_ref):
    away = 2 - 2 * (info_ref[0] % 2)
    spread_taps(here_ref.at[0], spread_ref.at[0])
    spread_taps(here_ref.at[1], spread_ref.at[1])
    spread_taps(there_ref.at[0], spread_ref.at[2])

    def part(a, source):
        return lax.dot_general(
            taps_ref[a], spread_ref[source], (((0,), (0,)), ((), ())), preferred_element_type=jnp.float32
        )

    acc_ref[...] = part(1, 0)
    acc_ref[...] += part(2 - away, 2)

    @pl.when(info_ref[1] == 0)
    def _():
        acc_ref[...] += part(away, 1)

    count, local, _ = keep_ref.shape
    col = info_ref[3]
    for i in range(count):
        keep_ref[i] = acc_ref[pl.ds(pl.multiple_of((col ^ (2 * i)) * local, local), local), :]
        give_ref[i] = acc_ref[pl.ds(pl.multiple_of((col ^ (2 * i + 1)) * local, local), local), :]


def output_kernel(info_ref, mine_ref, other_ref, taps_ref, out_ref, acc_ref):
    away = 2 * (info_ref[0] % 2)
    cols = mine_ref.shape[0]
    acc_ref[...] = jnp.dot(taps_ref[1], lines(mine_ref, 0, cols), preferred_element_type=jnp.float32)
    acc_ref[...] += jnp.dot(taps_ref[2 - away], lines(other_ref, 0, cols), preferred_element_type=jnp.float32)

    @pl.when(info_ref[1] == 0)
    def _():
        acc_ref[...] += jnp.dot(taps_ref[away], lines(mine_ref, 0, cols, True), preferred_element_type=jnp.float32)

    outs = acc_ref.shape[0] // 9
    total = jnp.zeros((outs, NY * NZ), jnp.float32)
    for tap in range(9):
        b, c = divmod(tap, 3)
        total = total + shifted(acc_ref[tap * outs : (tap + 1) * outs, :], b - 1, c - 1)
    out_ref[...] = total.astype(jnp.bfloat16)


def exponent(value):
    top = jnp.max(jnp.max(jnp.abs(value), axis=1, keepdims=True), axis=0, keepdims=True)
    top = jnp.broadcast_to(jnp.maximum(top, 1e-30), (1, LANES))
    return jnp.floor(jnp.log(top) * (1.0 / LOG2))


def filter_kernel(info_ref, mine_ref, other_ref, here_ref, there_ref, out_ref, window_ref, far_ref, spread_ref, acc_ref):
    core, side = info_ref[0] % 2, info_ref[0] // 2
    turn = 2 * core + side
    cols = mine_ref.shape[0]
    half, quarter = cols // 2, cols // 4
    width = acc_ref.shape[1]
    edge = 2 * width // 3
    for slab, ref, beyond in (
        (1 + core, mine_ref, False),
        (2 - core, other_ref, False),
        (3 * core, mine_ref, True),
        (3 - 3 * core, other_ref, True),
    ):
        window_ref[slab + 1 - side, :edge, :] = lines(ref, core * half, half, beyond)
        window_ref[slab + side, edge:, :] = lines(ref, turn * quarter, quarter, beyond)
    zeros = jnp.zeros((edge, window_ref.shape[2]), window_ref.dtype)
    window_ref[4 * side, :edge, :] = zeros
    window_ref[4 - 4 * side, edge:, :] = zeros[: width - edge]

    @pl.when(info_ref[2] == 1)
    def _():
        window_ref[1 + 2 * side, :edge, :] = zeros

    inside = core + side == 1

    @pl.when(inside)
    def _():
        far_ref[...] = here_ref[2]

    @pl.when(jnp.logical_not(inside))
    def _():
        far_ref[...] = there_ref[2]

    for index, (at, cot_ref) in enumerate(
        (
            (side + 1 + core, here_ref.at[0]),
            (side + 3 * core, here_ref.at[1]),
            (side + 2 - core, there_ref.at[0]),
            (side + 3 - 3 * core, there_ref.at[1]),
            (4 - 4 * side, far_ref),
        )
    ):
        spread_taps(cot_ref, spread_ref)
        part = lax.dot_general(
            spread_ref[...], window_ref[at], (((1,), (1,)), ((), ())), preferred_element_type=jnp.float32
        )
        if index:
            acc_ref[...] += part
        else:
            acc_ref[...] = part
    level = exponent(acc_ref[...])
    factor = jnp.exp((TOP - level) * LOG2)
    blocks, height, _ = out_ref.shape
    tiles = width // LANES
    rows = (height - EXTRA) // tiles
    for block in range(blocks):
        for tile in range(tiles):
            part = acc_ref[block * rows : (block + 1) * rows, tile * LANES : (tile + 1) * LANES]
            out_ref[block, tile * rows : (tile + 1) * rows, :] = part * factor
        out_ref[block, height - EXTRA :, :] = jnp.broadcast_to(level, (EXTRA, LANES))


def sum_kernel(in_ref, out_ref):
    blocks, height, _ = in_ref.shape
    height = height - EXTRA
    total = jnp.zeros((height, LANES), jnp.float32)
    for block in range(blocks):
        total = total + in_ref[block, :height, :] * jnp.exp((in_ref[block, height : height + 1, :] - TOP) * LOG2)
    level = exponent(total)
    out_ref[:height, :] = total * jnp.exp((TOP - level) * LOG2)
    out_ref[height:, :] = jnp.broadcast_to(level, (EXTRA, LANES))


def join_kernel(scale, spot_ref, own_ref, other_ref, out_ref):
    core = spot_ref[0] % 2
    blocks, height, _ = own_ref.shape
    height = height - EXTRA
    tiles = 3 * out_ref.shape[2] // (4 * LANES)
    rows = height // tiles
    wide = 2 * tiles // 3
    for its_core, piece_ref in ((core, own_ref), (1 - core, other_ref)):
        for block in range(blocks):
            index, side = divmod(block, 2)
            down = jnp.exp((piece_ref[block, height : height + 1, :] - TOP) * LOG2) * scale
            span = slice(index * rows, (index + 1) * rows)
            for tile in range(tiles):
                value = piece_ref[block, tile * rows : (tile + 1) * rows, :] * down
                if tile < wide:
                    offset, at = 2 * side, its_core * wide + tile
                else:
                    offset, at = 1, (2 * its_core + side) * (tiles - wide) + tile - wide
                out_ref[offset, span, pl.ds(pl.multiple_of(at * LANES, LANES), LANES)] = value


def call(kernel, out, scratch, flops, *args):
    return pl.pallas_call(
        kernel,
        out_shape=out,
        in_specs=[SMEM if a.dtype == jnp.int32 else VMEM for a in args],
        out_specs=[VMEM] * len(out) if isinstance(out, list) else VMEM,
        scratch_shapes=scratch,
        compiler_params=pltpu.CompilerParams(vmem_limit_bytes=24 << 20),
        cost_estimate=pl.CostEstimate(
            flops=flops, transcendentals=0, bytes_accessed=sum(a.size * a.dtype.itemsize for a in args)
        ),
    )(*args)


def body(features, filters, cotangent):
    _, local, cells = features.shape
    devices = lax.axis_size("gz")
    cols = lax.axis_size("col")
    channels = local * cols
    quads = devices // 4
    half = channels // 2
    quarter = channels // 4
    size = 9 * local
    width = half + quarter
    height = size // quads * (width // LANES) + EXTRA
    flops = 2 * 27 * local * channels * cells
    bf16, f16, f32 = jnp.bfloat16, jnp.float16, jnp.float32
    place = lax.axis_index("gz")
    last = devices - 1
    info = jnp.stack(
        [
            place % 4,
            ((place == 0) | (place == last)).astype(jnp.int32),
            ((place < 2) | (place > last - 2)).astype(jnp.int32),
            lax.axis_index("col"),
        ]
    ).astype(jnp.int32)
    x_own = features[0]
    c_own = cotangent[0]
    taps = filters.reshape(3, size, channels)

    def xor(value, bits):
        return lax.ppermute(value, "gz", [(i, i ^ bits) for i in range(devices)])

    outward = [(i, (i + 1) % devices if i % 2 else (i - 1) % devices) for i in range(devices)]
    ring = [[4 * g + r for g in range(quads)] for r in range(4)]

    def everywhere(block, axis, groups=None):
        count = len(groups[0]) if groups else lax.axis_size(axis)
        copies = jnp.broadcast_to(block[None], (count,) + block.shape)
        return lax.all_to_all(copies, axis, 0, 0, axis_index_groups=groups, tiled=True)

    beyond = lax.ppermute(jnp.stack([x_own, c_own]), "gz", outward)
    across = xor(c_own, 2)
    send, here = call(
        pack_kernel,
        [jax.ShapeDtypeStruct((cols, 2 * local, cells), bf16), jax.ShapeDtypeStruct((3, local, cells), bf16)],
        [],
        0,
        x_own,
        c_own,
        beyond,
        across,
    )
    gathered = lax.all_to_all(send, "col", 0, 0, tiled=True)
    there = xor(here, 1)

    give, keep = call(
        input_kernel,
        [jax.ShapeDtypeStruct((cols // 2, local, cells), f32)] * 2,
        [pltpu.VMEM((3, size, cells), bf16), pltpu.VMEM((channels, cells), f32)],
        flops,
        info,
        here,
        there,
        taps,
    )
    gathered, there, give, keep = lax.optimization_barrier((gathered, there, give, keep))
    other = xor(gathered, 1)

    grads = call(
        filter_kernel,
        jax.ShapeDtypeStruct((quads, height, LANES), f32),
        [
            pltpu.VMEM((5, width, cells), bf16),
            pltpu.VMEM((local, cells), bf16),
            pltpu.VMEM((size, cells), bf16),
            pltpu.VMEM((size, width), f32),
        ],
        flops,
        info,
        gathered,
        other,
        here,
        there,
    )
    grads, give, other = lax.optimization_barrier((grads, give, other))
    narrow = lax.all_to_all(grads.astype(f16), "gz", 0, 0, axis_index_groups=ring, tiled=True)

    def exchanged(bits, value):
        return lax.ppermute(value, "col", [(j, j ^ bits) for j in range(cols)])

    given = exchanged(1, give)
    output = call(
        output_kernel,
        jax.ShapeDtypeStruct((local, cells), bf16),
        [pltpu.VMEM((size, cells), f32)],
        flops,
        info,
        gathered,
        other,
        taps,
    )

    narrow, output, given = lax.optimization_barrier((narrow, output, given))
    mine = call(
        sum_kernel,
        jax.ShapeDtypeStruct((height, LANES), f32),
        [],
        0,
        narrow.astype(f32),
    )
    both = [[2 * i + r for i in range(devices // 2)] for r in range(2)]
    mine = everywhere(mine.astype(f16), "gz", both)
    pairs = [keep[i] + given[i] for i in range(cols // 2)]
    pieces = pairs[:1] + [exchanged(2 * i, pairs[i]) for i in range(1, cols // 2)]
    input_grad = sum(pieces[1:], pieces[0]).astype(bf16)
    mine, input_grad = lax.optimization_barrier((mine, input_grad))
    beside = xor(mine, 1)
    scale = float((cells * devices) ** -0.5)

    def kernel(*refs):
        join_kernel(scale, *refs)

    filter_grad = call(
        kernel,
        jax.ShapeDtypeStruct((3, size, channels), f32),
        [],
        0,
        info,
        mine.astype(f32),
        beside.astype(f32),
    )
    return output[None], input_grad[None], filter_grad.reshape(3, 3, 3, local, channels)


def solution(mesh):
    in_specs = (P("gz", "col", None), P(None, None, None, "col", None), P("gz", "col", None))
    out_specs = (P("gz", "col", None), P("gz", "col", None), P(None, None, None, "col", None))
    return jax.shard_map(body, mesh=mesh, in_specs=in_specs, out_specs=out_specs, check_vma=False)
```

time: 118 us -> 108 us (0.915)
  blocking collectives: 16.7 us -> 0 us
  waiting for transfers between devices: 44 us -> 38 us
  local copies, waits for them, and re-layouts: 3.06 us -> 8.5 us
  Pallas kernels: 7.51 us -> 10.7 us
  other arithmetic: 3.64 us -> 6.04 us
  starting transfers between devices: 41.7 us -> 43.6 us
    all_to_all x1 -> x0, blocking collectives: 16.7 us -> none  [everywhere(): lax.all_to_all(copies, axis, 0, 0, axis_index_groups=groups, tiled=True)]
    all_to_all x1, waiting for transfers between devices: 0.01 us -> 12.9 us  [everywhere(): lax.all_to_all(copies, axis, 0, 0, axis_index_groups=groups, tiled=True)]
    ppermute x4 -> x1, waiting for transfers between devices: 9.02 us -> 0.01 us  [body(): beyond = lax.ppermute(jnp.stack([x_own, c_own]), 'gz', outward)]
    ppermute x7 -> x4, starting transfers between devices: 9.39 us -> 17.8 us  [xor(): return lax.ppermute(value, 'gz', [(i, i ^ bits) for i in range(devices)])]
    ppermute x7 -> x4, waiting for transfers between devices: 16.5 us -> 8.62 us  [xor(): return lax.ppermute(value, 'gz', [(i, i ^ bits) for i in range(devices)])]
    ppermute x4 -> x1, starting transfers between devices: 10.2 us -> 4.39 us  [body(): beyond = lax.ppermute(jnp.stack([x_own, c_own]), 'gz', outward)]
    ppermute x7 -> x4, starting transfers between devices: 9.37 us -> 3.57 us  [exchanged(): return lax.ppermute(value, 'col', [(j, j ^ bits) for j in range(cols)])]
    unnamed x12 -> x20, local copies, waits for them, and re-layouts: 2.13 us -> 7.46 us
  transfers between devices with their start and end apart: 20 -> 12, of which waited for: 13 -> 10; matrix products, arithmetic and copies ran while one was open for 2% -> 3% of each run, Pallas kernels for 3% -> 5%
where the time goes in v3:
time: 108 us
  starting transfers between devices  43.6 us (40%)
  waiting for transfers between devices  38 us (35%)
  Pallas kernels  10.7 us (10%)
  local copies, waits for them, and re-layouts  8.5 us (8%)
  other arithmetic  6.04 us (6%)
    ppermute x4, starting transfers between devices, xor(): return lax.ppermute(value, 'gz', [(i, i ^ bits) for i in range(devices)])  17.8 us
    ppermute x4, waiting for transfers between devices, exchanged(): return lax.ppermute(value, 'col', [(j, j ^ bits) for j in range(cols)])  12.9 us
    all_to_all x1, waiting for transfers between devices, everywhere(): lax.all_to_all(copies, axis, 0, 0, axis_index_groups=groups, tiled=True)  12.9 us
    pallas_call x6, Pallas kernels, call(): pl.pallas_call(kernel, out_shape=out, in_specs=[SMEM if a.dtype == jnp.in...  10.7 us
    all_to_all x1, starting transfers between devices, body(): lax.all_to_all(grads.astype(f16), 'gz', 0, 0, axis_index_groups=ring, til...  9.45 us
    ppermute x4, waiting for transfers between devices, xor(): return lax.ppermute(value, 'gz', [(i, i ^ bits) for i in range(devices)])  8.62 us
    unnamed x20, local copies, waits for them, and re-layouts  7.46 us
    ppermute x1, starting transfers between devices, body(): beyond = lax.ppermute(jnp.stack([x_own, c_own]), 'gz', outward)  4.39 us
  transfers between devices with their start and end apart: 12, of which 10 were waited for; matrix products, arithmetic and copies ran while one was open for 3% of the time, Pallas kernels for 5%

profile of v3, /device:TPU:1, one launch (start us, length us, event | category | flops | bytes accessed | tf_op | source)
XLA Modules:
  0.0 107.6 jit_solution(9585465939783937447)
XLA Ops:
  0.6 0.0 copy-start
  0.6 1.0 pad_maximum_fusion
  1.7 4.4 %collective-permute-start = (bf16[2,64,512]{2,1,0:T(8,128)(2,1)S(1)}, bf16[2,64,512]{2,1,0:T(8,128)(2,1)S(1)}, u32[]{:S(2)}, u32[]{:S(2)}) collective-permute-start(bf16[2,64,512]{2,1,0:T(8,128)(2,1)S(1)} %pad_maximum_fusion), channel_id=1, source_target_pairs={{0,248},{8,16},{16,8},{24,32},{32,24},{40,48},{48,40},{56,64},{64,... | collective-permute-start | bytes 393224 | tf_op jit(solution)/shard_map/ppermute | solution.py:257
  6.1 1.4 %collective-permute-start.1 = (bf16[64,512]{1,0:T(8,128)(2,1)}, bf16[64,512]{1,0:T(8,128)(2,1)S(1)}, u32[]{:S(2)}, u32[]{:S(2)}) collective-permute-start(bf16[64,512]{1,0:T(8,128)(2,1)} %bitcast.27), channel_id=1, source_target_pairs={{0,16},{8,24},{16,0},{24,8},{32,48},{40,56},{48,32},{56,40},{64,80... | collective-permute-start | bytes 196616 | tf_op jit(solution)/shard_map/ppermute | solution.py:247
  7.5 3.4 %collective-permute-done.1.across_ref = bf16[64,512]{1,0:T(8,128)(2,1)S(1)} collective-permute-done((bf16[64,512]{1,0:T(8,128)(2,1)}, bf16[64,512]{1,0:T(8,128)(2,1)S(1)}, u32[]{:S(2)}, u32[]{:S(2)}) %collective-permute-start.1) | collective-permute-done | bytes 65568 | tf_op jit(solution)/shard_map/ppermute | solution.py:247
  10.9 0.0 collective-permute-done.beyond_ref
  10.9 0.8 copy-done.3
  11.7 0.8 copy-done.4
  12.6 0.1 shard_map.58
  12.7 0.0 copy-start.2
  12.7 1.0 copy-done.2
  13.6 4.1 %all-to-all-start = ((bf16[8,128,512]{2,1,0:T(8,128)(2,1)}), bf16[8,128,512]{2,1,0:T(8,128)(2,1)S(1)}, u32[]{:S(2)}, u32[]{:S(2)}) async-start(bf16[8,128,512]{2,1,0:T(8,128)(2,1)} %copy-done.2), calls=%async_computation | async-start | bytes 2097152 | tf_op jit(solution)/shard_map/all_to_all | solution.py:269
  17.8 6.6 %collective-permute-start.2 = (bf16[3,64,512]{2,1,0:T(8,128)(2,1)S(1)}, bf16[3,64,512]{2,1,0:T(8,128)(2,1)S(1)}, u32[]{:S(2)}, u32[]{:S(2)}) collective-permute-start(bf16[3,64,512]{2,1,0:T(8,128)(2,1)S(1)} %get-tuple-element.20.here_ref), channel_id=1, source_target_pairs={{0,8},{8,0},{16,24},{24,16},{32,40},{40,32},{48,56},{56,48},{64,72... | collective-permute-start | bytes 589832 | tf_op jit(solution)/shard_map/ppermute | solution.py:247
  24.3 0.1 pad_add_fusion.info_ref.refs_0_
  24.4 1.0 collective-permute-done.2.there_ref
  25.4 0.7 copy-done.5
  26.1 0.9 copy-done.6
  27.0 2.4 %shard_map.59 = (f32[4,64,512]{2,1,0:T(8,128)S(1)}, f32[4,64,512]{2,1,0:T(8,128)S(1)}) custom-call(s32[4]{0:T(128)S(1)} %pad_add_fusion.info_ref.refs_0_, bf16[3,64,512]{2,1,0:T(8,128)(2,1)S(1)} %get-tuple-element.20.here_ref, bf16[3,64,512]{2,1,0:T(8,128)(2,1)S(1)} %copy-done.6, bf16[3,576,512]{2,1,0:T(8,128)(2,1)S(1)} %bitcast.24), custom_call_target="tpu_custom_call" | custom-call | flops 905969664 | bytes 2162704 | tf_op jit(solution)/shard_map/pallas_call | solution.py:206
  29.4 0.8 copy-done.8
  30.2 5.5 %collective-permute-start.3 = (bf16[8,128,512]{2,1,0:T(8,128)(2,1)S(1)}, bf16[8,128,512]{2,1,0:T(8,128)(2,1)S(1)}, u32[]{:S(2)}, u32[]{:S(2)}) collective-permute-start(bf16[8,128,512]{2,1,0:T(8,128)(2,1)S(1)} %all-to-all-done.mine_ref), channel_id=1, source_target_pairs={{0,8},{8,0},{16,24},{24,16},{32,40},{40,32},{48,56},{56,48},{64,72... | collective-permute-start | bytes 3145736 | tf_op jit(solution)/shard_map/ppermute | solution.py:247
  35.7 2.3 %collective-permute-done.3.other_ref = bf16[8,128,512]{2,1,0:T(8,128)(2,1)S(1)} collective-permute-done((bf16[8,128,512]{2,1,0:T(8,128)(2,1)S(1)}, bf16[8,128,512]{2,1,0:T(8,128)(2,1)S(1)}, u32[]{:S(2)}, u32[]{:S(2)}) %collective-permute-start.3) | collective-permute-done | bytes 1048608 | tf_op jit(solution)/shard_map/ppermute | solution.py:247
  38.0 0.9 copy-done.7
  38.9 2.6 %shard_map.60 = f32[8,224,128]{2,1,0:T(8,128)S(1)} custom-call(s32[4]{0:T(128)S(1)} %pad_add_fusion.info_ref.refs_0_, bf16[8,128,512]{2,1,0:T(8,128)(2,1)S(1)} %all-to-all-done.mine_ref, bf16[8,128,512]{2,1,0:T(8,128)(2,1)S(1)} %collective-permute-done.3.other_ref, bf16[3,64,512]{2,1,0:T(8,128)(2,1)S(1)} %get-tuple-element.20.here_ref, ...), custom_call_target="tpu_custom_call" | custom-call | flops 905969664 | bytes 2490384 | tf_op jit(solution)/shard_map/pallas_call | solution.py:206
  41.5 0.8 convert_element_type.20
  42.4 9.4 %all-to-all-start.1 = ((f16[8,224,128]{2,1,0:T(8,128)(2,1)}), f16[8,224,128]{2,1,0:T(8,128)(2,1)}, u32[]{:S(2)}, u32[]{:S(2)}) async-start(f16[8,224,128]{2,1,0:T(8,128)(2,1)} %convert_element_type.20), calls=%async_computation.1 | async-start | bytes 917504 | tf_op jit(solution)/shard_map/all_to_all | solution.py:302
  51.8 0.2 collective-permute-start.4
  52.1 1.5 %copy-done.1 = bf16[3,3,3,64,512]{4,3,2,1,0:T(8,128)(2,1)S(1)} copy-done((bf16[3,3,3,64,512]{4,3,2,1,0:T(8,128)(2,1)S(1)}, bf16[3,3,3,64,512]{4,3,2,1,0:T(8,128)(2,1)}, u32[]{:S(2)}) %copy-start.1) | copy-done | bytes 1769496
  53.5 2.7 %shard_map.61 = bf16[64,512]{1,0:T(8,128)(2,1)} custom-call(s32[4]{0:T(128)S(1)} %pad_add_fusion.info_ref.refs_0_, bf16[8,128,512]{2,1,0:T(8,128)(2,1)S(1)} %all-to-all-done.mine_ref, bf16[8,128,512]{2,1,0:T(8,128)(2,1)S(1)} %collective-permute-done.3.other_ref, bf16[3,576,512]{2,1,0:T(8,128)(2,1)S(1)} %bitcast.25), custom_call_target="tpu_custom_call" | custom-call | flops 905969664 | bytes 3866640 | tf_op jit(solution)/shard_map/pallas_call | solution.py:206
  56.3 8.5 %collective-permute-done.4 = f32[4,64,512]{2,1,0:T(8,128)} collective-permute-done((f32[4,64,512]{2,1,0:T(8,128)S(1)}, f32[4,64,512]{2,1,0:T(8,128)}, u32[]{:S(2)}, u32[]{:S(2)}) %collective-permute-start.4) | collective-permute-done | bytes 524320 | tf_op jit(solution)/shard_map/ppermute | solution.py:305
  64.8 3.7 %all-to-all-done.1 = f16[8,224,128]{2,1,0:T(8,128)(2,1)} async-done(((f16[8,224,128]{2,1,0:T(8,128)(2,1)}), f16[8,224,128]{2,1,0:T(8,128)(2,1)}, u32[]{:S(2)}, u32[]{:S(2)}) %all-to-all-start.1) | async-done | bytes 458784 | tf_op jit(solution)/shard_map/all_to_all | solution.py:302
  68.5 1.1 %convert_element_type.21.in_ref = f32[8,224,128]{2,1,0:T(8,128)S(1)} convert(f16[8,224,128]{2,1,0:T(8,128)(2,1)} %all-to-all-done.1) | non-fusion elementwise | flops 229376 | bytes 1376256 | tf_op jit(solution)/shard_map/convert_element_type | solution.py:325
  69.6 0.2 shard_map.62
  69.8 1.0 broadcast_in_dim.13
  70.8 4.3 %all-to-all-start.2 = ((f16[16,224,128]{2,1,0:T(8,128)(2,1)}), f16[16,224,128]{2,1,0:T(8,128)(2,1)S(1)}, u32[]{:S(2)}, u32[]{:S(2)}) async-start(f16[16,224,128]{2,1,0:T(8,128)(2,1)} %broadcast_in_dim.13), calls=%async_computation.2 | async-start | bytes 1835008 | tf_op jit(solution)/shard_map/all_to_all | solution.py:255
  75.1 1.1 %add_bitcast_fusion.2 = (f32[64,512]{1,0:T(8,128)S(1)}, f32[64,512]{1,0:T(8,128)S(1)}, f32[64,512]{1,0:T(8,128)S(1)}) fusion(f32[4,64,512]{2,1,0:T(8,128)} %collective-permute-done.4, f32[4,64,512]{2,1,0:T(8,128)S(1)} %get-tuple-element.31), kind=kLoop, calls=%fused_computation.7 | loop fusion | flops 98304 | bytes 1179648 | tf_op jit(solution)/shard_map/add | solution.py:329
  76.2 0.1 collective-permute-start.5
  76.3 0.6 collective-permute-start.7
  76.9 2.7 %collective-permute-start.6 = (f32[64,512]{1,0:T(8,128)S(1)}, f32[64,512]{1,0:T(8,128)S(1)}, u32[]{:S(2)}, u32[]{:S(2)}) collective-permute-start(f32[64,512]{1,0:T(8,128)S(1)} %get-tuple-element.37), channel_id=1, source_target_pairs={{0,4},{1,5},{2,6},{3,7},{4,0},{5,1},{6,2},{7,3},{8,12},{9,13},{10,... | collective-permute-start | bytes 393224 | tf_op jit(solution)/shard_map/ppermute | solution.py:305
  79.5 0.6 collective-permute-done.5
  80.1 2.3 %collective-permute-done.7 = f32[64,512]{1,0:T(8,128)S(1)} collective-permute-done((f32[64,512]{1,0:T(8,128)S(1)}, f32[64,512]{1,0:T(8,128)S(1)}, u32[]{:S(2)}, u32[]{:S(2)}) %collective-permute-start.7) | collective-permute-done | bytes 131104 | tf_op jit(solution)/shard_map/ppermute | solution.py:305
  82.4 1.5 %collective-permute-done.6 = f32[64,512]{1,0:T(8,128)S(1)} collective-permute-done((f32[64,512]{1,0:T(8,128)S(1)}, f32[64,512]{1,0:T(8,128)S(1)}, u32[]{:S(2)}, u32[]{:S(2)}) %collective-permute-start.6) | collective-permute-done | bytes 131104 | tf_op jit(solution)/shard_map/ppermute | solution.py:305
  83.9 1.6 %fusion.2 = bf16[64,512]{1,0:T(8,128)(2,1)} fusion(f32[64,512]{1,0:T(8,128)S(1)} %collective-permute-done.7, f32[64,512]{1,0:T(8,128)S(1)} %collective-permute-done.6, f32[64,512]{1,0:T(8,128)S(1)} %collective-permute-done.5, f32[4,64,512]{2,1,0:T(8,128)} %collective-permute-done.4, f32[4,64,512]{2,1,0:T(8,128)S(1)} %get-tuple-element.31), kind=kLoop, calls=%fused_computation.4 | loop fusion | flops 163840 | bytes 720896 | tf_op jit(solution)/shard_map/convert_element_type | solution.py:331
  85.5 12.9 %all-to-all-done.2 = f16[16,224,128]{2,1,0:T(8,128)(2,1)S(1)} async-done(((f16[16,224,128]{2,1,0:T(8,128)(2,1)}), f16[16,224,128]{2,1,0:T(8,128)(2,1)S(1)}, u32[]{:S(2)}, u32[]{:S(2)}) %all-to-all-start.2) | async-done | bytes 917536 | tf_op jit(solution)/shard_map/all_to_all | solution.py:255
  98.3 4.3 %collective-permute-start.8 = (f16[16,224,128]{2,1,0:T(8,128)(2,1)S(1)}, f16[16,224,128]{2,1,0:T(8,128)(2,1)S(1)}, u32[]{:S(2)}, u32[]{:S(2)}) collective-permute-start(f16[16,224,128]{2,1,0:T(8,128)(2,1)S(1)} %all-to-all-done.2), channel_id=1, source_target_pairs={{0,8},{8,0},{16,24},{24,16},{32,40},{40,32},{48,56},{56,48},{64,72... | collective-permute-start | bytes 2752520 | tf_op jit(solution)/shard_map/ppermute | solution.py:247
  102.6 0.2 convert_element_type.24.refs_1_
  102.8 1.9 %collective-permute-done.8 = f16[16,224,128]{2,1,0:T(8,128)(2,1)S(1)} collective-permute-done((f16[16,224,128]{2,1,0:T(8,128)(2,1)S(1)}, f16[16,224,128]{2,1,0:T(8,128)(2,1)S(1)}, u32[]{:S(2)}, u32[]{:S(2)}) %collective-permute-start.8) | collective-permute-done | bytes 917536 | tf_op jit(solution)/shard_map/ppermute | solution.py:247
  104.7 0.2 convert_element_type.25.refs_2_
  104.9 2.7 %shard_map.63 = f32[3,576,512]{2,1,0:T(8,128)} custom-call(s32[4]{0:T(128)S(1)} %pad_add_fusion.info_ref.refs_0_, f32[16,224,128]{2,1,0:T(8,128)S(1)} %convert_element_type.24.refs_1_, f32[16,224,128]{2,1,0:T(8,128)S(1)} %convert_element_type.25.refs_2_), custom_call_target="tpu_custom_call" | custom-call | bytes 3670032 | tf_op jit(solution)/shard_map/pallas_call | solution.py:206
  (12 shorter events, 0.0 us)
Async XLA Ops:
  0.6 25.4 %copy-start = (bf16[3,3,3,64,512]{4,3,2,1,0:T(8,128)(2,1)S(1)}, bf16[3,3,3,64,512]{4,3,2,1,0:T(8,128)(2,1)}, u32[]{:S(2)}) copy-start(bf16[3,3,3,64,512]{4,3,2,1,0:T(8,128)(2,1)} %param.4) | copy-start | bytes 5308420
  1.7 9.2 %collective-permute-start = (bf16[2,64,512]{2,1,0:T(8,128)(2,1)S(1)}, bf16[2,64,512]{2,1,0:T(8,128)(2,1)S(1)}, u32[]{:S(2)}, u32[]{:S(2)}) collective-permute-start(bf16[2,64,512]{2,1,0:T(8,128)(2,1)S(1)} %pad_maximum_fusion), channel_id=1, source_target_pairs={{0,248},{8,16},{16,8},{24,32},{32,24},{40,48},{48,40},{56,64},{64,... | collective-permute-start | bytes 393224 | tf_op jit(solution)/shard_map/ppermute | solution.py:257
  6.1 4.8 %collective-permute-start.1 = (bf16[64,512]{1,0:T(8,128)(2,1)}, bf16[64,512]{1,0:T(8,128)(2,1)S(1)}, u32[]{:S(2)}, u32[]{:S(2)}) collective-permute-start(bf16[64,512]{1,0:T(8,128)(2,1)} %bitcast.27), channel_id=1, source_target_pairs={{0,16},{8,24},{16,0},{24,8},{32,48},{40,56},{48,32},{56,40},{64,80... | collective-permute-start | bytes 196616 | tf_op jit(solution)/shard_map/ppermute | solution.py:247
  10.9 0.8 copy-start.3
  11.7 0.8 copy-start.4
  12.7 1.0 copy-start.2
  13.6 16.5 %all-to-all-start = ((bf16[8,128,512]{2,1,0:T(8,128)(2,1)}), bf16[8,128,512]{2,1,0:T(8,128)(2,1)S(1)}, u32[]{:S(2)}, u32[]{:S(2)}) async-start(bf16[8,128,512]{2,1,0:T(8,128)(2,1)} %copy-done.2), calls=%async_computation | async-start | bytes 2097152 | tf_op jit(solution)/shard_map/all_to_all | solution.py:269
  17.8 7.6 %collective-permute-start.2 = (bf16[3,64,512]{2,1,0:T(8,128)(2,1)S(1)}, bf16[3,64,512]{2,1,0:T(8,128)(2,1)S(1)}, u32[]{:S(2)}, u32[]{:S(2)}) collective-permute-start(bf16[3,64,512]{2,1,0:T(8,128)(2,1)S(1)} %get-tuple-element.20.here_ref), channel_id=1, source_target_pairs={{0,8},{8,0},{16,24},{24,16},{32,40},{40,32},{48,56},{56,48},{64,72... | collective-permute-start | bytes 589832 | tf_op jit(solution)/shard_map/ppermute | solution.py:247
  25.4 0.7 copy-start.5
  26.1 0.9 copy-start.6
  29.4 0.8 copy-start.8
  30.2 7.8 %collective-permute-start.3 = (bf16[8,128,512]{2,1,0:T(8,128)(2,1)S(1)}, bf16[8,128,512]{2,1,0:T(8,128)(2,1)S(1)}, u32[]{:S(2)}, u32[]{:S(2)}) collective-permute-start(bf16[8,128,512]{2,1,0:T(8,128)(2,1)S(1)} %all-to-all-done.mine_ref), channel_id=1, source_target_pairs={{0,8},{8,0},{16,24},{24,16},{32,40},{40,32},{48,56},{56,48},{64,72... | collective-permute-start | bytes 3145736 | tf_op jit(solution)/shard_map/ppermute | solution.py:247
  38.0 0.9 copy-start.7
  41.5 10.3 %copy-start.9 = (f32[4,64,512]{2,1,0:T(8,128)S(1)}, f32[4,64,512]{2,1,0:T(8,128)}, u32[]{:S(2)}) copy-start(f32[4,64,512]{2,1,0:T(8,128)} %copy-done.8) | copy-start | bytes 1572868
  42.4 26.1 %all-to-all-start.1 = ((f16[8,224,128]{2,1,0:T(8,128)(2,1)}), f16[8,224,128]{2,1,0:T(8,128)(2,1)}, u32[]{:S(2)}, u32[]{:S(2)}) async-start(f16[8,224,128]{2,1,0:T(8,128)(2,1)} %convert_element_type.20), calls=%async_computation.1 | async-start | bytes 917504 | tf_op jit(solution)/shard_map/all_to_all | solution.py:302
  51.8 13.0 %collective-permute-start.4 = (f32[4,64,512]{2,1,0:T(8,128)S(1)}, f32[4,64,512]{2,1,0:T(8,128)}, u32[]{:S(2)}, u32[]{:S(2)}) collective-permute-start(f32[4,64,512]{2,1,0:T(8,128)S(1)} %copy-done.9), channel_id=1, source_target_pairs={{0,1},{1,0},{2,3},{3,2},{4,5},{5,4},{6,7},{7,6},{8,9},{9,8},{10,11... | collective-permute-start | bytes 1572872 | tf_op jit(solution)/shard_map/ppermute | solution.py:305
  52.1 1.5 %copy-start.1 = (bf16[3,3,3,64,512]{4,3,2,1,0:T(8,128)(2,1)S(1)}, bf16[3,3,3,64,512]{4,3,2,1,0:T(8,128)(2,1)}, u32[]{:S(2)}) copy-start(bf16[3,3,3,64,512]{4,3,2,1,0:T(8,128)(2,1)} %param.4) | copy-start | bytes 5308420
  70.8 27.5 %all-to-all-start.2 = ((f16[16,224,128]{2,1,0:T(8,128)(2,1)}), f16[16,224,128]{2,1,0:T(8,128)(2,1)S(1)}, u32[]{:S(2)}, u32[]{:S(2)}) async-start(f16[16,224,128]{2,1,0:T(8,128)(2,1)} %broadcast_in_dim.13), calls=%async_computation.2 | async-start | bytes 1835008 | tf_op jit(solution)/shard_map/all_to_all | solution.py:255
  76.2 3.9 %collective-permute-start.5 = (f32[64,512]{1,0:T(8,128)S(1)}, f32[64,512]{1,0:T(8,128)S(1)}, u32[]{:S(2)}, u32[]{:S(2)}) collective-permute-start(f32[64,512]{1,0:T(8,128)S(1)} %get-tuple-element.35), channel_id=1, source_target_pairs={{0,2},{1,3},{2,0},{3,1},{4,6},{5,7},{6,4},{7,5},{8,10},{9,11},{10,... | collective-permute-start | bytes 393224 | tf_op jit(solution)/shard_map/ppermute | solution.py:305
  76.3 6.1 %collective-permute-start.7 = (f32[64,512]{1,0:T(8,128)S(1)}, f32[64,512]{1,0:T(8,128)S(1)}, u32[]{:S(2)}, u32[]{:S(2)}) collective-permute-start(f32[64,512]{1,0:T(8,128)S(1)} %get-tuple-element.36), channel_id=1, source_target_pairs={{0,6},{1,7},{2,4},{3,5},{4,2},{5,3},{6,0},{7,1},{8,14},{9,15},{10,... | collective-permute-start | bytes 393224 | tf_op jit(solution)/shard_map/ppermute | solution.py:305
  76.9 7.0 %collective-permute-start.6 = (f32[64,512]{1,0:T(8,128)S(1)}, f32[64,512]{1,0:T(8,128)S(1)}, u32[]{:S(2)}, u32[]{:S(2)}) collective-permute-start(f32[64,512]{1,0:T(8,128)S(1)} %get-tuple-element.37), channel_id=1, source_target_pairs={{0,4},{1,5},{2,6},{3,7},{4,0},{5,1},{6,2},{7,3},{8,12},{9,13},{10,... | collective-permute-start | bytes 393224 | tf_op jit(solution)/shard_map/ppermute | solution.py:305
  98.3 6.4 %collective-permute-start.8 = (f16[16,224,128]{2,1,0:T(8,128)(2,1)S(1)}, f16[16,224,128]{2,1,0:T(8,128)(2,1)S(1)}, u32[]{:S(2)}, u32[]{:S(2)}) collective-permute-start(f16[16,224,128]{2,1,0:T(8,128)(2,1)S(1)} %all-to-all-done.2), channel_id=1, source_target_pairs={{0,8},{8,0},{16,24},{24,16},{32,40},{40,32},{48,56},{56,48},{64,72... | collective-permute-start | bytes 2752520 | tf_op jit(solution)/shard_map/ppermute | solution.py:247

commit v4 on v3

--- a/solution.py
+++ b/solution.py
@@ -1,3 +1,5 @@
+import functools
+
 import jax
 import jax.numpy as jnp
 from jax import lax
@@ -9,6 +11,7 @@
 NZ = 16
 VMEM = pl.BlockSpec(memory_space=pltpu.VMEM)
 SMEM = pl.BlockSpec(memory_space=pltpu.SMEM)
+ANY = pl.BlockSpec(memory_space=pl.ANY)
 LOG2 = 0.6931471805599453
 TOP = 13.0
 EXTRA = 8
@@ -48,15 +51,12 @@
     return ref[pl.ds(first, count), start : start + local, :].reshape(count * local, cells)
 
 
-def pack_kernel(x_ref, c_ref, beyond_ref, across_ref, send_ref, here_ref):
-    blocks, both, _ = send_ref.shape
+def pack_kernel(own_ref, halo_ref, out_ref):
+    blocks, both, _ = out_ref.shape
     local = both // 2
     for block in range(blocks):
-        send_ref[block, :local, :] = x_ref[...]
-        send_ref[block, local:, :] = beyond_ref[0]
-    here_ref[0] = c_ref[...]
-    here_ref[1] = beyond_ref[1]
-    here_ref[2] = across_ref[...]
+        out_ref[block, :local, :] = own_ref[...]
+        out_ref[block, local:, :] = halo_ref[...]
 
 
 def input_kernel(info_ref, here_ref, there_ref, taps_ref, give_ref, keep_ref, spread_ref, acc_ref):
@@ -181,39 +181,56 @@
     out_ref[height:, :] = jnp.broadcast_to(level, (EXTRA, LANES))
 
 
-def join_kernel(scale, spot_ref, own_ref, other_ref, out_ref):
-    core = spot_ref[0] % 2
-    blocks, height, _ = own_ref.shape
+def join_kernel(scale, flip, count, info_ref, *refs):
+    pieces, (out_ref, lines_ref, sems) = refs[: 2 * count], refs[-3:]
+    core = info_ref[0] % 2
+    blocks, height, _ = pieces[0].shape
     height = height - EXTRA
     tiles = 3 * out_ref.shape[2] // (4 * LANES)
     rows = height // tiles
     wide = 2 * tiles // 3
-    for its_core, piece_ref in ((core, own_ref), (1 - core, other_ref)):
-        for block in range(blocks):
-            index, side = divmod(block, 2)
-            down = jnp.exp((piece_ref[block, height : height + 1, :] - TOP) * LOG2) * scale
-            span = slice(index * rows, (index + 1) * rows)
-            for tile in range(tiles):
-                value = piece_ref[block, tile * rows : (tile + 1) * rows, :] * down
-                if tile < wide:
-                    offset, at = 2 * side, its_core * wide + tile
-                else:
-                    offset, at = 1, (2 * its_core + side) * (tiles - wide) + tile - wide
-                out_ref[offset, span, pl.ds(pl.multiple_of(at * LANES, LANES), LANES)] = value
-
-
-def call(kernel, out, scratch, flops, *args):
+    copies = []
+    for index in range(count):
+        for z in range(blocks // 2):
+            spot = index * (blocks // 2) + z
+            for its_core, piece_ref in ((core, pieces[index]), (1 - core, pieces[count + index])):
+                for side in range(2):
+                    block = 2 * z + side
+                    down = jnp.exp((piece_ref[block, height : height + 1, :] - TOP) * LOG2) * scale
+                    for tile in range(tiles):
+                        value = piece_ref[block, tile * rows : (tile + 1) * rows, :] * down
+                        if tile < wide:
+                            offset, at = 2 * side, its_core * wide + tile
+                        else:
+                            offset, at = 1, (2 * its_core + side) * (tiles - wide) + tile - wide
+                        lines_ref[spot, offset, :, pl.ds(pl.multiple_of(at * LANES, LANES), LANES)] = value
+            first = (2 * spot + (1 - info_ref[4] if flip else info_ref[4])) * rows
+            for offset in range(3):
+                copy = pltpu.make_async_copy(
+                    lines_ref.at[spot, offset],
+                    out_ref.at[offset, pl.ds(pl.multiple_of(first, 8), rows), :],
+                    sems.at[spot, offset],
+                )
+                copy.start()
+                copies.append(copy)
+    for copy in copies:
+        copy.wait()
+
+
+def call(kernel, out, scratch, flops, *args, into=None, spaces=VMEM):
+    held = [] if into is None else [into]
     return pl.pallas_call(
         kernel,
         out_shape=out,
-        in_specs=[SMEM if a.dtype == jnp.int32 else VMEM for a in args],
-        out_specs=[VMEM] * len(out) if isinstance(out, list) else VMEM,
+        in_specs=[SMEM if a.dtype == jnp.int32 else VMEM for a in args] + [ANY] * len(held),
+        out_specs=[spaces] * len(out) if isinstance(out, list) else spaces,
         scratch_shapes=scratch,
-        compiler_params=pltpu.CompilerParams(vmem_limit_bytes=24 << 20),
+        input_output_aliases={len(args): 0} if held else {},
+        compiler_params=pltpu.CompilerParams(vmem_limit_bytes=12 << 20),
         cost_estimate=pl.CostEstimate(
             flops=flops, transcendentals=0, bytes_accessed=sum(a.size * a.dtype.itemsize for a in args)
         ),
-    )(*args)
+    )(*args, *held)
 
 
 def body(features, filters, cotangent):
@@ -237,6 +254,7 @@
             ((place == 0) | (place == last)).astype(jnp.int32),
             ((place < 2) | (place > last - 2)).astype(jnp.int32),
             lax.axis_index("col"),
+            place // 4 % 2,
         ]
     ).astype(jnp.int32)
     x_own = features[0]
@@ -254,19 +272,20 @@
         copies = jnp.broadcast_to(block[None], (count,) + block.shape)
         return lax.all_to_all(copies, axis, 0, 0, axis_index_groups=groups, tiled=True)
 
-    beyond = lax.ppermute(jnp.stack([x_own, c_own]), "gz", outward)
+    x_halo = lax.ppermute(x_own, "gz", outward)
+    c_halo = lax.ppermute(c_own, "gz", outward)
     across = xor(c_own, 2)
-    send, here = call(
+    x_halo, c_halo, across = lax.optimization_barrier((x_halo, c_halo, across))
+    send = call(
         pack_kernel,
-        [jax.ShapeDtypeStruct((cols, 2 * local, cells), bf16), jax.ShapeDtypeStruct((3, local, cells), bf16)],
+        jax.ShapeDtypeStruct((cols, 2 * local, cells), bf16),
         [],
         0,
         x_own,
-        c_own,
-        beyond,
-        across,
+        x_halo,
     )
     gathered = lax.all_to_all(send, "col", 0, 0, tiled=True)
+    send, here = lax.optimization_barrier((send, jnp.stack([c_own, c_halo, across])))
     there = xor(here, 1)
 
     give, keep = call(
@@ -298,13 +317,18 @@
         here,
         there,
     )
-    grads, give, other = lax.optimization_barrier((grads, give, other))
+    grads, other = lax.optimization_barrier((grads, other))
     narrow = lax.all_to_all(grads.astype(f16), "gz", 0, 0, axis_index_groups=ring, tiled=True)
 
     def exchanged(bits, value):
         return lax.ppermute(value, "col", [(j, j ^ bits) for j in range(cols)])
 
     given = exchanged(1, give)
+    pairs = [keep[i] + given[i] for i in range(cols // 2)]
+    pieces = pairs[:1] + [exchanged(2 * i, pairs[i]) for i in range(1, cols // 2)]
+    other, _ = lax.optimization_barrier((other, given))
+    narrow, pieces, other = lax.optimization_barrier((narrow, pieces, other))
+    input_grad = sum(pieces[1:], pieces[0]).astype(bf16)
     output = call(
         output_kernel,
         jax.ShapeDtypeStruct((local, cells), bf16),
@@ -315,8 +339,6 @@
         other,
         taps,
     )
-
-    narrow, output, given = lax.optimization_barrier((narrow, output, given))
     mine = call(
         sum_kernel,
         jax.ShapeDtypeStruct((height, LANES), f32),
@@ -324,26 +346,40 @@
         0,
         narrow.astype(f32),
     )
-    both = [[2 * i + r for i in range(devices // 2)] for r in range(2)]
-    mine = everywhere(mine.astype(f16), "gz", both)
-    pairs = [keep[i] + given[i] for i in range(cols // 2)]
-    pieces = pairs[:1] + [exchanged(2 * i, pairs[i]) for i in range(1, cols // 2)]
-    input_grad = sum(pieces[1:], pieces[0]).astype(bf16)
-    mine, input_grad = lax.optimization_barrier((mine, input_grad))
+    every = [[8 * g + 4 * q + 2 * y + r for g in range(quads // 2) for y in range(2)] for q in range(2) for r in range(2)]
+    mine = everywhere(mine.astype(f16), "gz", every)
+    mine, output, input_grad = lax.optimization_barrier((mine, output, input_grad))
+    first, second = mine[:quads // 2], mine[quads // 2 :]
+    first = lax.ppermute(first, "gz", [(i, (i + 4) % devices) for i in range(devices)])
+    second = lax.ppermute(second, "gz", [(i, (i - 4) % devices) for i in range(devices)])
     beside = xor(mine, 1)
     scale = float((cells * devices) ** -0.5)
-
-    def kernel(*refs):
-        join_kernel(scale, *refs)
-
-    filter_grad = call(
-        kernel,
-        jax.ShapeDtypeStruct((3, size, channels), f32),
-        [],
+    shape = jax.ShapeDtypeStruct((3, size, channels), f32)
+    scratch = [pltpu.VMEM((quads // 2, 3, size // quads, channels), f32), pltpu.SemaphoreType.DMA((quads // 2, 3))]
+    joined = call(
+        functools.partial(join_kernel, scale, False, 1),
+        shape,
+        scratch,
         0,
         info,
         mine.astype(f32),
         beside.astype(f32),
+        spaces=ANY,
+    )
+    joined, first, second = lax.optimization_barrier((joined, first, second))
+    others = xor(first, 1), xor(second, 1)
+    filter_grad = call(
+        functools.partial(join_kernel, scale, True, 2),
+        shape,
+        scratch,
+        0,
+        info,
+        first.astype(f32),
+        second.astype(f32),
+        others[0].astype(f32),
+        others[1].astype(f32),
+        into=joined,
+        spaces=ANY,
     )
     return output[None], input_grad[None], filter_grad.reshape(3, 3, 3, local, channels)
 

time: 108 us -> 103 us (0.954)
  starting transfers between devices: 43.6 us -> 37.5 us
  waiting for transfers between devices: 38 us -> 40.7 us
  other arithmetic: 6.04 us -> 3.85 us
  Pallas kernels: 10.7 us -> 12.7 us
  local copies, waits for them, and re-layouts: 8.5 us -> 6.65 us
    ppermute x4 -> x6, starting transfers between devices: 17.8 us -> 7.09 us  [xor(): return lax.ppermute(value, 'gz', [(i, i ^ bits) for i in range(devices)])]
    ppermute x1 -> x4, starting transfers between devices: 4.39 us -> 12.8 us  [the longest x1 6.85 us: body(): c_halo = lax.ppermute(c_own, 'gz', outward)]
    ppermute x1 -> x4, waiting for transfers between devices: 0.01 us -> 7.96 us  [the longest x1 3.71 us: body(): lax.ppermute(second, 'gz', [(i, (i - 4) % devices) for i in range(devices)])]
    all_to_all x1, waiting for transfers between devices: 0.01 us -> 6.29 us  [body(): gathered = lax.all_to_all(send, 'col', 0, 0, tiled=True)]
    ppermute x4, waiting for transfers between devices: 12.9 us -> 7.78 us  [exchanged(): return lax.ppermute(value, 'col', [(j, j ^ bits) for j in range(cols)])]
    ppermute x4 -> x6, waiting for transfers between devices: 8.62 us -> 3.91 us  [xor(): return lax.ppermute(value, 'gz', [(i, i ^ bits) for i in range(devices)])]
    all_to_all x1, starting transfers between devices: 9.45 us -> 4.79 us  [body(): lax.all_to_all(grads.astype(f16), 'gz', 0, 0, axis_index_groups=ring, til...]
    all_to_all x1, waiting for transfers between devices: 12.9 us -> 10.5 us  [everywhere(): lax.all_to_all(copies, axis, 0, 0, axis_index_groups=groups, tiled=True)]
  transfers between devices with their start and end apart: 12 -> 17, of which waited for: 10 -> 13; matrix products, arithmetic and copies ran while one was open for 3% -> 4% of each run, Pallas kernels for 5% -> 9%
where the time goes in v4:
time: 103 us; the launch traced here: 102 us
  waiting for transfers between devices  40.7 us (40%)
  starting transfers between devices  37.5 us (36%)
  Pallas kernels  12.7 us (12%)
  local copies, waits for them, and re-layouts  6.65 us (6%)
  other arithmetic  3.85 us (4%)
    pallas_call x7, Pallas kernels, call(): pl.pallas_call(kernel, out_shape=out, in_specs=[SMEM if a.dtype == jnp.in...  12.7 us
    all_to_all x1, waiting for transfers between devices, everywhere(): lax.all_to_all(copies, axis, 0, 0, axis_index_groups=groups, tiled=True)  10.5 us
    ppermute x4, waiting for transfers between devices, exchanged(): return lax.ppermute(value, 'col', [(j, j ^ bits) for j in range(cols)])  7.78 us
    ppermute x6, starting transfers between devices, xor(): return lax.ppermute(value, 'gz', [(i, i ^ bits) for i in range(devices)])  7.09 us
    ppermute x1, starting transfers between devices, body(): c_halo = lax.ppermute(c_own, 'gz', outward)  6.85 us
    all_to_all x1, waiting for transfers between devices, body(): gathered = lax.all_to_all(send, 'col', 0, 0, tiled=True)  6.29 us
    unnamed x14, local copies, waits for them, and re-layouts  5.64 us
    all_to_all x1, starting transfers between devices, body(): lax.all_to_all(grads.astype(f16), 'gz', 0, 0, axis_index_groups=ring, til...  4.79 us
  transfers between devices with their start and end apart: 17, of which 13 were waited for; matrix products, arithmetic and copies ran while one was open for 4% of the time, Pallas kernels for 9%

profile of v4, /device:TPU:1, one launch (start us, length us, event | category | flops | bytes accessed | tf_op | source)
XLA Modules:
  0.0 102.2 jit_solution(3368844184634497744)
XLA Ops:
  0.6 4.4 %collective-permute-start = (bf16[64,512]{1,0:T(8,128)(2,1)}, bf16[64,512]{1,0:T(8,128)(2,1)S(1)}, u32[]{:S(2)}, u32[]{:S(2)}) collective-permute-start(bf16[64,512]{1,0:T(8,128)(2,1)} %bitcast.23), channel_id=1, source_target_pairs={{0,248},{8,16},{16,8},{24,32},{32,24},{40,48},{48,40},{56,64},{64,... | collective-permute-start | bytes 196616 | tf_op jit(solution)/shard_map/ppermute | solution.py:275
  5.0 1.4 %collective-permute-start.2 = (bf16[64,512]{1,0:T(8,128)(2,1)}, bf16[64,512]{1,0:T(8,128)(2,1)S(1)}, u32[]{:S(2)}, u32[]{:S(2)}) collective-permute-start(bf16[64,512]{1,0:T(8,128)(2,1)} %bitcast.28), channel_id=1, source_target_pairs={{0,16},{8,24},{16,0},{24,8},{32,48},{40,56},{48,32},{56,40},{64,80... | collective-permute-start | bytes 196616 | tf_op jit(solution)/shard_map/ppermute | solution.py:265
  6.4 6.9 %collective-permute-start.1 = (bf16[64,512]{1,0:T(8,128)(2,1)}, bf16[64,512]{1,0:T(8,128)(2,1)S(1)}, u32[]{:S(2)}, u32[]{:S(2)}) collective-permute-start(bf16[64,512]{1,0:T(8,128)(2,1)} %bitcast.29), channel_id=1, source_target_pairs={{0,248},{8,16},{16,8},{24,32},{32,24},{40,48},{48,40},{56,64},{64,... | collective-permute-start | bytes 196616 | tf_op jit(solution)/shard_map/ppermute | solution.py:276
  13.3 3.1 %collective-permute-done.1 = bf16[64,512]{1,0:T(8,128)(2,1)S(1)} collective-permute-done((bf16[64,512]{1,0:T(8,128)(2,1)}, bf16[64,512]{1,0:T(8,128)(2,1)S(1)}, u32[]{:S(2)}, u32[]{:S(2)}) %collective-permute-start.1) | collective-permute-done | bytes 65568 | tf_op jit(solution)/shard_map/ppermute | solution.py:276
  16.4 0.8 copy-done.5
  17.3 1.0 %shard_map.58 = bf16[8,128,512]{2,1,0:T(8,128)(2,1)} custom-call(bf16[64,512]{1,0:T(8,128)(2,1)S(1)} %bitcast.24, bf16[64,512]{1,0:T(8,128)(2,1)S(1)} %collective-permute-done.halo_ref), custom_call_target="tpu_custom_call" | custom-call | bytes 131072 | tf_op jit(solution)/shard_map/pallas_call | solution.py:222
  18.3 4.1 %all-to-all-start = ((bf16[8,128,512]{2,1,0:T(8,128)(2,1)}), bf16[8,128,512]{2,1,0:T(8,128)(2,1)S(1)}, u32[]{:S(2)}, u32[]{:S(2)}) async-start(bf16[8,128,512]{2,1,0:T(8,128)(2,1)} %shard_map.58), calls=%async_computation | async-start | bytes 2097152 | tf_op jit(solution)/shard_map/all_to_all | solution.py:287
  22.5 0.9 pad_maximum_fusion.here_ref
  23.3 1.6 %collective-permute-start.3 = (bf16[3,64,512]{2,1,0:T(8,128)(2,1)S(1)}, bf16[3,64,512]{2,1,0:T(8,128)(2,1)S(1)}, u32[]{:S(2)}, u32[]{:S(2)}) collective-permute-start(bf16[3,64,512]{2,1,0:T(8,128)(2,1)S(1)} %pad_maximum_fusion.here_ref), channel_id=1, source_target_pairs={{0,8},{8,0},{16,24},{24,16},{32,40},{40,32},{48,56},{56,48},{64,72... | collective-permute-start | bytes 589832 | tf_op jit(solution)/shard_map/ppermute | solution.py:265
  24.9 0.1 stack.40.info_ref
  25.0 1.0 collective-permute-done.3.there_ref
  26.0 0.7 copy-done.2
  26.7 0.9 copy-done.3
  27.6 2.4 %shard_map.59 = (f32[4,64,512]{2,1,0:T(8,128)S(1)}, f32[4,64,512]{2,1,0:T(8,128)S(1)}) custom-call(s32[5]{0:T(128)S(1)} %stack.40.info_ref, bf16[3,64,512]{2,1,0:T(8,128)(2,1)S(1)} %pad_maximum_fusion.here_ref, bf16[3,64,512]{2,1,0:T(8,128)(2,1)S(1)} %copy-done.3, bf16[3,576,512]{2,1,0:T(8,128)(2,1)S(1)} %bitcast.21), custom_call_target="tpu_custom_call" | custom-call | flops 905969664 | bytes 2162708 | tf_op jit(solution)/shard_map/pallas_call | solution.py:222
  30.0 0.8 copy-done.6
  30.8 6.3 %all-to-all-done.mine_ref = bf16[8,128,512]{2,1,0:T(8,128)(2,1)S(1)} async-done(((bf16[8,128,512]{2,1,0:T(8,128)(2,1)}), bf16[8,128,512]{2,1,0:T(8,128)(2,1)S(1)}, u32[]{:S(2)}, u32[]{:S(2)}) %all-to-all-start) | async-done | bytes 1048608 | tf_op jit(solution)/shard_map/all_to_all | solution.py:287
  37.1 1.9 %collective-permute-start.4 = (bf16[8,128,512]{2,1,0:T(8,128)(2,1)S(1)}, bf16[8,128,512]{2,1,0:T(8,128)(2,1)S(1)}, u32[]{:S(2)}, u32[]{:S(2)}) collective-permute-start(bf16[8,128,512]{2,1,0:T(8,128)(2,1)S(1)} %all-to-all-done.mine_ref), channel_id=1, source_target_pairs={{0,8},{8,0},{16,24},{24,16},{32,40},{40,32},{48,56},{56,48},{64,72... | collective-permute-start | bytes 3145736 | tf_op jit(solution)/shard_map/ppermute | solution.py:265
  39.0 0.7 collective-permute-start.5
  39.7 1.5 %collective-permute-done.4.other_ref = bf16[8,128,512]{2,1,0:T(8,128)(2,1)S(1)} collective-permute-done((bf16[8,128,512]{2,1,0:T(8,128)(2,1)S(1)}, bf16[8,128,512]{2,1,0:T(8,128)(2,1)S(1)}, u32[]{:S(2)}, u32[]{:S(2)}) %collective-permute-start.4) | collective-permute-done | bytes 1048608 | tf_op jit(solution)/shard_map/ppermute | solution.py:265
  41.3 0.9 copy-done.4
  42.2 2.6 %shard_map.60 = f32[8,224,128]{2,1,0:T(8,128)S(1)} custom-call(s32[5]{0:T(128)S(1)} %stack.40.info_ref, bf16[8,128,512]{2,1,0:T(8,128)(2,1)S(1)} %all-to-all-done.mine_ref, bf16[8,128,512]{2,1,0:T(8,128)(2,1)S(1)} %collective-permute-done.4.other_ref, bf16[3,64,512]{2,1,0:T(8,128)(2,1)S(1)} %pad_maximum_fusion.here_ref, bf16[3,64,512]{2,1,0:T(8,128)(2,1)S(1)} %copy-done.4), custom_call_target="tpu_custom_call" | custom-call | flops 905969664 | bytes 2490388 | tf_op jit(solution)/shard_map/pallas_call | solution.py:222
  44.8 0.8 convert_element_type.32
  45.7 4.8 %all-to-all-start.1 = ((f16[8,224,128]{2,1,0:T(8,128)(2,1)}), f16[8,224,128]{2,1,0:T(8,128)(2,1)S(1)}, u32[]{:S(2)}, u32[]{:S(2)}) async-start(f16[8,224,128]{2,1,0:T(8,128)(2,1)} %convert_element_type.32), calls=%async_computation.1 | async-start | bytes 917504 | tf_op jit(solution)/shard_map/all_to_all | solution.py:321
  50.5 2.4 %collective-permute-done.5 = f32[4,64,512]{2,1,0:T(8,128)} collective-permute-done((f32[4,64,512]{2,1,0:T(8,128)}, f32[4,64,512]{2,1,0:T(8,128)}, u32[]{:S(2)}, u32[]{:S(2)}) %collective-permute-start.5) | collective-permute-done | bytes 524320 | tf_op jit(solution)/shard_map/ppermute | solution.py:324
  52.9 1.2 %fusion = (f32[64,512]{1,0:T(8,128)S(1)}, f32[64,512]{1,0:T(8,128)S(1)}, f32[64,512]{1,0:T(8,128)S(1)}, f32[64,512]{1,0:T(8,128)S(1)}) fusion(f32[4,64,512]{2,1,0:T(8,128)} %collective-permute-done.5, f32[4,64,512]{2,1,0:T(8,128)S(1)} %get-tuple-element.37), kind=kLoop, calls=%fused_computation.2 | loop fusion | flops 131072 | bytes 1572864 | tf_op jit(solution)/shard_map/add | solution.py:327
  54.0 0.5 collective-permute-start.8
  54.6 1.6 %collective-permute-start.7 = (f32[64,512]{1,0:T(8,128)S(1)}, f32[64,512]{1,0:T(8,128)S(1)}, u32[]{:S(2)}, u32[]{:S(2)}) collective-permute-start(f32[64,512]{1,0:T(8,128)S(1)} %get-tuple-element.54), channel_id=1, source_target_pairs={{0,4},{1,5},{2,6},{3,7},{4,0},{5,1},{6,2},{7,3},{8,12},{9,13},{10,... | collective-permute-start | bytes 393224 | tf_op jit(solution)/shard_map/ppermute | solution.py:324
  56.2 1.2 %collective-permute-start.6 = (f32[64,512]{1,0:T(8,128)S(1)}, f32[64,512]{1,0:T(8,128)S(1)}, u32[]{:S(2)}, u32[]{:S(2)}) collective-permute-start(f32[64,512]{1,0:T(8,128)S(1)} %get-tuple-element.55), channel_id=1, source_target_pairs={{0,2},{1,3},{2,0},{3,1},{4,6},{5,7},{6,4},{7,5},{8,10},{9,11},{10,... | collective-permute-start | bytes 393224 | tf_op jit(solution)/shard_map/ppermute | solution.py:324
  57.4 5.0 %collective-permute-done.8 = f32[64,512]{1,0:T(8,128)S(1)} collective-permute-done((f32[64,512]{1,0:T(8,128)S(1)}, f32[64,512]{1,0:T(8,128)S(1)}, u32[]{:S(2)}, u32[]{:S(2)}) %collective-permute-start.8) | collective-permute-done | bytes 131104 | tf_op jit(solution)/shard_map/ppermute | solution.py:324
  62.4 0.3 collective-permute-done.6
  62.7 4.3 %all-to-all-done.1 = f16[8,224,128]{2,1,0:T(8,128)(2,1)S(1)} async-done(((f16[8,224,128]{2,1,0:T(8,128)(2,1)}), f16[8,224,128]{2,1,0:T(8,128)(2,1)S(1)}, u32[]{:S(2)}, u32[]{:S(2)}) %all-to-all-start.1) | async-done | bytes 458784 | tf_op jit(solution)/shard_map/all_to_all | solution.py:321
  67.1 0.2 shard_map.61
  67.3 0.8 broadcast_in_dim.12
  68.1 4.6 %all-to-all-start.2 = ((f16[8,224,128]{2,1,0:T(8,128)(2,1)}), f16[8,224,128]{2,1,0:T(8,128)(2,1)S(1)}, u32[]{:S(2)}, u32[]{:S(2)}) async-start(f16[8,224,128]{2,1,0:T(8,128)(2,1)} %broadcast_in_dim.12), calls=%async_computation.2 | async-start | bytes 917504 | tf_op jit(solution)/shard_map/all_to_all | solution.py:273
  72.7 1.5 %copy-done.1 = bf16[3,3,3,64,512]{4,3,2,1,0:T(8,128)(2,1)S(1)} copy-done((bf16[3,3,3,64,512]{4,3,2,1,0:T(8,128)(2,1)S(1)}, bf16[3,3,3,64,512]{4,3,2,1,0:T(8,128)(2,1)}, u32[]{:S(2)}) %copy-start.1) | copy-done | bytes 1769496
  74.2 2.7 %shard_map.62 = bf16[64,512]{1,0:T(8,128)(2,1)} custom-call(s32[5]{0:T(128)S(1)} %stack.40.info_ref, bf16[8,128,512]{2,1,0:T(8,128)(2,1)S(1)} %all-to-all-done.mine_ref, bf16[8,128,512]{2,1,0:T(8,128)(2,1)S(1)} %collective-permute-done.4.other_ref, bf16[3,576,512]{2,1,0:T(8,128)(2,1)S(1)} %bitcast.22), custom_call_target="tpu_custom_call" | custom-call | flops 905969664 | bytes 3866644 | tf_op jit(solution)/shard_map/pallas_call | solution.py:222
  76.9 0.7 add_convert_fusion
  77.6 10.5 %all-to-all-done.2 = f16[8,224,128]{2,1,0:T(8,128)(2,1)S(1)} async-done(((f16[8,224,128]{2,1,0:T(8,128)(2,1)}), f16[8,224,128]{2,1,0:T(8,128)(2,1)S(1)}, u32[]{:S(2)}, u32[]{:S(2)}) %all-to-all-start.2) | async-done | bytes 458784 | tf_op jit(solution)/shard_map/all_to_all | solution.py:273
  88.1 1.2 %collective-permute-start.9 = (f16[8,224,128]{2,1,0:T(8,128)(2,1)S(1)}, f16[8,224,128]{2,1,0:T(8,128)(2,1)S(1)}, u32[]{:S(2)}, u32[]{:S(2)}) collective-permute-start(f16[8,224,128]{2,1,0:T(8,128)(2,1)S(1)} %all-to-all-done.2), channel_id=1, source_target_pairs={{0,8},{8,0},{16,24},{24,16},{32,40},{40,32},{48,56},{56,48},{64,72... | collective-permute-start | bytes 1376264 | tf_op jit(solution)/shard_map/ppermute | solution.py:265
  89.2 0.1 fusion.4
  89.4 1.5 %collective-permute-start.10 = (f16[4,224,128]{2,1,0:T(8,128)(2,1)S(1)}, f16[4,224,128]{2,1,0:T(8,128)(2,1)S(1)}, u32[]{:S(2)}, u32[]{:S(2)}) collective-permute-start(f16[4,224,128]{2,1,0:T(8,128)(2,1)S(1)} %get-tuple-element.58), channel_id=1, source_target_pairs={{0,32},{8,40},{16,48},{24,56},{32,64},{40,72},{48,80},{56,88},{64,... | collective-permute-start | bytes 688136 | tf_op jit(solution)/shard_map/ppermute | solution.py:353
  91.0 1.9 %shard_map.63.refs_4_ = f32[3,576,512]{2,1,0:T(8,128)} custom-call(s32[5]{0:T(128)S(1)} %stack.40.info_ref, f32[8,224,128]{2,1,0:T(8,128)S(1)} %convert_element_type.36.refs_0_, f32[8,224,128]{2,1,0:T(8,128)S(1)} %convert_element_type.37.refs_1_), custom_call_target="tpu_custom_call" | custom-call | bytes 1835028 | tf_op jit(solution)/shard_map/pallas_call | solution.py:222
  92.9 3.7 %collective-permute-done.11 = f16[4,224,128]{2,1,0:T(8,128)(2,1)S(1)} collective-permute-done((f16[4,224,128]{2,1,0:T(8,128)(2,1)S(1)}, f16[4,224,128]{2,1,0:T(8,128)(2,1)S(1)}, u32[]{:S(2)}, u32[]{:S(2)}) %collective-permute-start.11) | collective-permute-done | bytes 229408 | tf_op jit(solution)/shard_map/ppermute | solution.py:354
  96.6 1.1 %collective-permute-done.10 = f16[4,224,128]{2,1,0:T(8,128)(2,1)S(1)} collective-permute-done((f16[4,224,128]{2,1,0:T(8,128)(2,1)S(1)}, f16[4,224,128]{2,1,0:T(8,128)(2,1)S(1)}, u32[]{:S(2)}, u32[]{:S(2)}) %collective-permute-start.10) | collective-permute-done | bytes 229408 | tf_op jit(solution)/shard_map/ppermute | solution.py:353
  97.7 1.0 collective-permute-start.12
  98.8 1.0 %collective-permute-done.12 = f16[4,224,128]{2,1,0:T(8,128)(2,1)S(1)} collective-permute-done((f16[4,224,128]{2,1,0:T(8,128)(2,1)S(1)}, f16[4,224,128]{2,1,0:T(8,128)(2,1)S(1)}, u32[]{:S(2)}, u32[]{:S(2)}) %collective-permute-start.12) | collective-permute-done | bytes 229408 | tf_op jit(solution)/shard_map/ppermute | solution.py:265
  99.9 0.3 collective-permute-done.13
  100.2 1.9 %shard_map.64 = f32[3,576,512]{2,1,0:T(8,128)} custom-call(s32[5]{0:T(128)S(1)} %stack.40.info_ref, f32[4,224,128]{2,1,0:T(8,128)S(1)} %convert_element_type.38.refs_0_, f32[4,224,128]{2,1,0:T(8,128)S(1)} %convert_element_type.39.refs_1_, f32[4,224,128]{2,1,0:T(8,128)S(1)} %convert_element_type.40.refs_2_, ...), custom_call_target="tpu_custom_call", output_to_operand_aliasing={{}: (5, {})} | custom-call | bytes 1835028 | tf_op jit(solution)/shard_map/pallas_call | solution.py:222
  (22 shorter events, 0.4 us)
Async XLA Ops:
  0.6 26.0 %copy-start = (bf16[3,3,3,64,512]{4,3,2,1,0:T(8,128)(2,1)S(1)}, bf16[3,3,3,64,512]{4,3,2,1,0:T(8,128)(2,1)}, u32[]{:S(2)}) copy-start(bf16[3,3,3,64,512]{4,3,2,1,0:T(8,128)(2,1)} %param.4) | copy-start | bytes 5308420
  0.6 12.7 %collective-permute-start = (bf16[64,512]{1,0:T(8,128)(2,1)}, bf16[64,512]{1,0:T(8,128)(2,1)S(1)}, u32[]{:S(2)}, u32[]{:S(2)}) collective-permute-start(bf16[64,512]{1,0:T(8,128)(2,1)} %bitcast.23), channel_id=1, source_target_pairs={{0,248},{8,16},{16,8},{24,32},{32,24},{40,48},{48,40},{56,64},{64,... | collective-permute-start | bytes 196616 | tf_op jit(solution)/shard_map/ppermute | solution.py:275
  5.0 8.3 %collective-permute-start.2 = (bf16[64,512]{1,0:T(8,128)(2,1)}, bf16[64,512]{1,0:T(8,128)(2,1)S(1)}, u32[]{:S(2)}, u32[]{:S(2)}) collective-permute-start(bf16[64,512]{1,0:T(8,128)(2,1)} %bitcast.28), channel_id=1, source_target_pairs={{0,16},{8,24},{16,0},{24,8},{32,48},{40,56},{48,32},{56,40},{64,80... | collective-permute-start | bytes 196616 | tf_op jit(solution)/shard_map/ppermute | solution.py:265
  6.4 10.0 %collective-permute-start.1 = (bf16[64,512]{1,0:T(8,128)(2,1)}, bf16[64,512]{1,0:T(8,128)(2,1)S(1)}, u32[]{:S(2)}, u32[]{:S(2)}) collective-permute-start(bf16[64,512]{1,0:T(8,128)(2,1)} %bitcast.29), channel_id=1, source_target_pairs={{0,248},{8,16},{16,8},{24,32},{32,24},{40,48},{48,40},{56,64},{64,... | collective-permute-start | bytes 196616 | tf_op jit(solution)/shard_map/ppermute | solution.py:276
  16.4 0.8 copy-start.5
  18.3 18.7 %all-to-all-start = ((bf16[8,128,512]{2,1,0:T(8,128)(2,1)}), bf16[8,128,512]{2,1,0:T(8,128)(2,1)S(1)}, u32[]{:S(2)}, u32[]{:S(2)}) async-start(bf16[8,128,512]{2,1,0:T(8,128)(2,1)} %shard_map.58), calls=%async_computation | async-start | bytes 2097152 | tf_op jit(solution)/shard_map/all_to_all | solution.py:287
  23.3 2.7 %collective-permute-start.3 = (bf16[3,64,512]{2,1,0:T(8,128)(2,1)S(1)}, bf16[3,64,512]{2,1,0:T(8,128)(2,1)S(1)}, u32[]{:S(2)}, u32[]{:S(2)}) collective-permute-start(bf16[3,64,512]{2,1,0:T(8,128)(2,1)S(1)} %pad_maximum_fusion.here_ref), channel_id=1, source_target_pairs={{0,8},{8,0},{16,24},{24,16},{32,40},{40,32},{48,56},{56,48},{64,72... | collective-permute-start | bytes 589832 | tf_op jit(solution)/shard_map/ppermute | solution.py:265
  26.0 0.7 copy-start.2
  26.7 0.9 copy-start.3
  30.0 0.8 copy-start.6
  37.1 4.2 %collective-permute-start.4 = (bf16[8,128,512]{2,1,0:T(8,128)(2,1)S(1)}, bf16[8,128,512]{2,1,0:T(8,128)(2,1)S(1)}, u32[]{:S(2)}, u32[]{:S(2)}) collective-permute-start(bf16[8,128,512]{2,1,0:T(8,128)(2,1)S(1)} %all-to-all-done.mine_ref), channel_id=1, source_target_pairs={{0,8},{8,0},{16,24},{24,16},{32,40},{40,32},{48,56},{56,48},{64,72... | collective-permute-start | bytes 3145736 | tf_op jit(solution)/shard_map/ppermute | solution.py:265
  39.0 13.9 %collective-permute-start.5 = (f32[4,64,512]{2,1,0:T(8,128)}, f32[4,64,512]{2,1,0:T(8,128)}, u32[]{:S(2)}, u32[]{:S(2)}) collective-permute-start(f32[4,64,512]{2,1,0:T(8,128)} %copy-done.6), channel_id=1, source_target_pairs={{0,1},{1,0},{2,3},{3,2},{4,5},{5,4},{6,7},{7,6},{8,9},{9,8},{10,11... | collective-permute-start | bytes 1572872 | tf_op jit(solution)/shard_map/ppermute | solution.py:324
  41.3 0.9 copy-start.4
  45.7 21.3 %all-to-all-start.1 = ((f16[8,224,128]{2,1,0:T(8,128)(2,1)}), f16[8,224,128]{2,1,0:T(8,128)(2,1)S(1)}, u32[]{:S(2)}, u32[]{:S(2)}) async-start(f16[8,224,128]{2,1,0:T(8,128)(2,1)} %convert_element_type.32), calls=%async_computation.1 | async-start | bytes 917504 | tf_op jit(solution)/shard_map/all_to_all | solution.py:321
  54.0 8.4 %collective-permute-start.8 = (f32[64,512]{1,0:T(8,128)S(1)}, f32[64,512]{1,0:T(8,128)S(1)}, u32[]{:S(2)}, u32[]{:S(2)}) collective-permute-start(f32[64,512]{1,0:T(8,128)S(1)} %get-tuple-element.53), channel_id=1, source_target_pairs={{0,6},{1,7},{2,4},{3,5},{4,2},{5,3},{6,0},{7,1},{8,14},{9,15},{10,... | collective-permute-start | bytes 393224 | tf_op jit(solution)/shard_map/ppermute | solution.py:324
  54.6 7.8 %collective-permute-start.7 = (f32[64,512]{1,0:T(8,128)S(1)}, f32[64,512]{1,0:T(8,128)S(1)}, u32[]{:S(2)}, u32[]{:S(2)}) collective-permute-start(f32[64,512]{1,0:T(8,128)S(1)} %get-tuple-element.54), channel_id=1, source_target_pairs={{0,4},{1,5},{2,6},{3,7},{4,0},{5,1},{6,2},{7,3},{8,12},{9,13},{10,... | collective-permute-start | bytes 393224 | tf_op jit(solution)/shard_map/ppermute | solution.py:324
  56.2 6.5 %collective-permute-start.6 = (f32[64,512]{1,0:T(8,128)S(1)}, f32[64,512]{1,0:T(8,128)S(1)}, u32[]{:S(2)}, u32[]{:S(2)}) collective-permute-start(f32[64,512]{1,0:T(8,128)S(1)} %get-tuple-element.55), channel_id=1, source_target_pairs={{0,2},{1,3},{2,0},{3,1},{4,6},{5,7},{6,4},{7,5},{8,10},{9,11},{10,... | collective-permute-start | bytes 393224 | tf_op jit(solution)/shard_map/ppermute | solution.py:324
  68.1 20.0 %all-to-all-start.2 = ((f16[8,224,128]{2,1,0:T(8,128)(2,1)}), f16[8,224,128]{2,1,0:T(8,128)(2,1)S(1)}, u32[]{:S(2)}, u32[]{:S(2)}) async-start(f16[8,224,128]{2,1,0:T(8,128)(2,1)} %broadcast_in_dim.12), calls=%async_computation.2 | async-start | bytes 917504 | tf_op jit(solution)/shard_map/all_to_all | solution.py:273
  72.7 1.5 %copy-start.1 = (bf16[3,3,3,64,512]{4,3,2,1,0:T(8,128)(2,1)S(1)}, bf16[3,3,3,64,512]{4,3,2,1,0:T(8,128)(2,1)}, u32[]{:S(2)}) copy-start(bf16[3,3,3,64,512]{4,3,2,1,0:T(8,128)(2,1)} %param.4) | copy-start | bytes 5308420
  88.1 2.9 %collective-permute-start.9 = (f16[8,224,128]{2,1,0:T(8,128)(2,1)S(1)}, f16[8,224,128]{2,1,0:T(8,128)(2,1)S(1)}, u32[]{:S(2)}, u32[]{:S(2)}) collective-permute-start(f16[8,224,128]{2,1,0:T(8,128)(2,1)S(1)} %all-to-all-done.2), channel_id=1, source_target_pairs={{0,8},{8,0},{16,24},{24,16},{32,40},{40,32},{48,56},{56,48},{64,72... | collective-permute-start | bytes 1376264 | tf_op jit(solution)/shard_map/ppermute | solution.py:265
  89.3 7.3 %collective-permute-start.11 = (f16[4,224,128]{2,1,0:T(8,128)(2,1)S(1)}, f16[4,224,128]{2,1,0:T(8,128)(2,1)S(1)}, u32[]{:S(2)}, u32[]{:S(2)}) collective-permute-start(f16[4,224,128]{2,1,0:T(8,128)(2,1)S(1)} %get-tuple-element.57), channel_id=1, source_target_pairs={{0,224},{8,232},{16,240},{24,248},{32,0},{40,8},{48,16},{56,24},{6... | collective-permute-start | bytes 688136 | tf_op jit(solution)/shard_map/ppermute | solution.py:354
  89.4 8.3 %collective-permute-start.10 = (f16[4,224,128]{2,1,0:T(8,128)(2,1)S(1)}, f16[4,224,128]{2,1,0:T(8,128)(2,1)S(1)}, u32[]{:S(2)}, u32[]{:S(2)}) collective-permute-start(f16[4,224,128]{2,1,0:T(8,128)(2,1)S(1)} %get-tuple-element.58), channel_id=1, source_target_pairs={{0,32},{8,40},{16,48},{24,56},{32,64},{40,72},{48,80},{56,88},{64,... | collective-permute-start | bytes 688136 | tf_op jit(solution)/shard_map/ppermute | solution.py:353
  97.7 2.1 %collective-permute-start.12 = (f16[4,224,128]{2,1,0:T(8,128)(2,1)S(1)}, f16[4,224,128]{2,1,0:T(8,128)(2,1)S(1)}, u32[]{:S(2)}, u32[]{:S(2)}) collective-permute-start(f16[4,224,128]{2,1,0:T(8,128)(2,1)S(1)} %collective-permute-done.10), channel_id=1, source_target_pairs={{0,8},{8,0},{16,24},{24,16},{32,40},{40,32},{48,56},{56,48},{64,72... | collective-permute-start | bytes 688136 | tf_op jit(solution)/shard_map/ppermute | solution.py:265
  98.7 1.5 %collective-permute-start.13 = (f16[4,224,128]{2,1,0:T(8,128)(2,1)S(1)}, f16[4,224,128]{2,1,0:T(8,128)(2,1)S(1)}, u32[]{:S(2)}, u32[]{:S(2)}) collective-permute-start(f16[4,224,128]{2,1,0:T(8,128)(2,1)S(1)} %collective-permute-done.11), channel_id=1, source_target_pairs={{0,8},{8,0},{16,24},{24,16},{32,40},{40,32},{48,56},{56,48},{64,72... | collective-permute-start | bytes 688136 | tf_op jit(solution)/shard_map/ppermute | solution.py:265

commit v5 on v4

--- a/solution.py
+++ b/solution.py
@@ -51,12 +51,18 @@
     return ref[pl.ds(first, count), start : start + local, :].reshape(count * local, cells)
 
 
-def pack_kernel(own_ref, halo_ref, out_ref):
+def pack_kernel(part, in_ref, *refs):
+    out_ref, sems = refs[-2:]
     blocks, both, _ = out_ref.shape
     local = both // 2
-    for block in range(blocks):
-        out_ref[block, :local, :] = own_ref[...]
-        out_ref[block, local:, :] = halo_ref[...]
+    copies = [
+        pltpu.make_async_copy(in_ref, out_ref.at[block, pl.ds(part * local, local), :], sems.at[block])
+        for block in range(blocks)
+    ]
+    for copy in copies:
+        copy.start()
+    for copy in copies:
+        copy.wait()
 
 
 def input_kernel(info_ref, here_ref, there_ref, taps_ref, give_ref, keep_ref, spread_ref, acc_ref):
@@ -275,15 +281,11 @@
     x_halo = lax.ppermute(x_own, "gz", outward)
     c_halo = lax.ppermute(c_own, "gz", outward)
     across = xor(c_own, 2)
-    x_halo, c_halo, across = lax.optimization_barrier((x_halo, c_halo, across))
-    send = call(
-        pack_kernel,
-        jax.ShapeDtypeStruct((cols, 2 * local, cells), bf16),
-        [],
-        0,
-        x_own,
-        x_halo,
-    )
+    shape = jax.ShapeDtypeStruct((cols, 2 * local, cells), bf16)
+    scratch = [pltpu.SemaphoreType.DMA((cols,))]
+    send = call(functools.partial(pack_kernel, 0), shape, scratch, 0, x_own, spaces=ANY)
+    x_halo, c_halo, across, send = lax.optimization_barrier((x_halo, c_halo, across, send))
+    send = call(functools.partial(pack_kernel, 1), shape, scratch, 0, x_halo, into=send, spaces=ANY)
     gathered = lax.all_to_all(send, "col", 0, 0, tiled=True)
     send, here = lax.optimization_barrier((send, jnp.stack([c_own, c_halo, across])))
     there = xor(here, 1)

time: 103 us -> 102 us (level)
    ppermute x1, waiting for transfers between devices: 3.15 us -> 1.43 us  [body(): c_halo = lax.ppermute(c_own, 'gz', outward)]
    pallas_call x7 -> x8, Pallas kernels: 12.7 us -> 13.4 us  [call(): pl.pallas_call(kernel, out_shape=out, in_specs=[SMEM if a.dtype == jnp.in...]
    unnamed x14 -> x16, local copies, waits for them, and re-layouts: 5.64 us -> 5.67 us
  transfers between devices with their start and end apart: 17 -> 17, of which waited for: 13 -> 13; matrix products, arithmetic and copies ran while one was open for 4% -> 3% of each run, Pallas kernels for 9% -> 10%
where the time goes in v5:
time: 102 us; the launch traced here: 101 us
  waiting for transfers between devices  39.7 us (39%)
  starting transfers between devices  37.5 us (37%)
  Pallas kernels  13.4 us (13%)
  local copies, waits for them, and re-layouts  6.67 us (7%)
  other arithmetic  3.01 us (3%)
    pallas_call x8, Pallas kernels, call(): pl.pallas_call(kernel, out_shape=out, in_specs=[SMEM if a.dtype == jnp.in...  13.4 us
    all_to_all x1, waiting for transfers between devices, everywhere(): lax.all_to_all(copies, axis, 0, 0, axis_index_groups=groups, tiled=True)  10.5 us
    ppermute x4, waiting for transfers between devices, exchanged(): return lax.ppermute(value, 'col', [(j, j ^ bits) for j in range(cols)])  7.77 us
    all_to_all x1, waiting for transfers between devices, body(): gathered = lax.all_to_all(send, 'col', 0, 0, tiled=True)  7.1 us
    ppermute x6, starting transfers between devices, xor(): return lax.ppermute(value, 'gz', [(i, i ^ bits) for i in range(devices)])  7.09 us
    ppermute x1, starting transfers between devices, body(): c_halo = lax.ppermute(c_own, 'gz', outward)  6.85 us
    unnamed x16, local copies, waits for them, and re-layouts  5.67 us
    all_to_all x1, starting transfers between devices, body(): lax.all_to_all(grads.astype(f16), 'gz', 0, 0, axis_index_groups=ring, til...  4.79 us
  transfers between devices with their start and end apart: 17, of which 13 were waited for; matrix products, arithmetic and copies ran while one was open for 3% of the time, Pallas kernels for 10%

profile of v5, /device:TPU:1, one launch (start us, length us, event | category | flops | bytes accessed | tf_op | source)
XLA Modules:
  0.0 101.1 jit_solution(3851798756967557656)
XLA Ops:
  0.6 4.4 %collective-permute-start = (bf16[64,512]{1,0:T(8,128)(2,1)}, bf16[64,512]{1,0:T(8,128)(2,1)S(1)}, u32[]{:S(2)}, u32[]{:S(2)}) collective-permute-start(bf16[64,512]{1,0:T(8,128)(2,1)} %bitcast.23), channel_id=1, source_target_pairs={{0,248},{8,16},{16,8},{24,32},{32,24},{40,48},{48,40},{56,64},{64,... | collective-permute-start | bytes 196616 | tf_op jit(solution)/shard_map/ppermute | solution.py:281
  5.0 1.4 %collective-permute-start.2 = (bf16[64,512]{1,0:T(8,128)(2,1)}, bf16[64,512]{1,0:T(8,128)(2,1)S(1)}, u32[]{:S(2)}, u32[]{:S(2)}) collective-permute-start(bf16[64,512]{1,0:T(8,128)(2,1)} %bitcast.28), channel_id=1, source_target_pairs={{0,16},{8,24},{16,0},{24,8},{32,48},{40,56},{48,32},{56,40},{64,80... | collective-permute-start | bytes 196616 | tf_op jit(solution)/shard_map/ppermute | solution.py:271
  6.4 6.9 %collective-permute-start.1 = (bf16[64,512]{1,0:T(8,128)(2,1)}, bf16[64,512]{1,0:T(8,128)(2,1)S(1)}, u32[]{:S(2)}, u32[]{:S(2)}) collective-permute-start(bf16[64,512]{1,0:T(8,128)(2,1)} %bitcast.29), channel_id=1, source_target_pairs={{0,248},{8,16},{16,8},{24,32},{32,24},{40,48},{48,40},{56,64},{64,... | collective-permute-start | bytes 196616 | tf_op jit(solution)/shard_map/ppermute | solution.py:282
  13.3 0.8 copy-done.5
  14.1 0.8 shard_map.58.refs_0_
  15.0 1.4 %collective-permute-done.1 = bf16[64,512]{1,0:T(8,128)(2,1)S(1)} collective-permute-done((bf16[64,512]{1,0:T(8,128)(2,1)}, bf16[64,512]{1,0:T(8,128)(2,1)S(1)}, u32[]{:S(2)}, u32[]{:S(2)}) %collective-permute-start.1) | collective-permute-done | bytes 65568 | tf_op jit(solution)/shard_map/ppermute | solution.py:282
  16.4 0.8 shard_map.59
  17.3 4.1 %all-to-all-start = ((bf16[8,128,512]{2,1,0:T(8,128)(2,1)}), bf16[8,128,512]{2,1,0:T(8,128)(2,1)S(1)}, u32[]{:S(2)}, u32[]{:S(2)}) async-start(bf16[8,128,512]{2,1,0:T(8,128)(2,1)} %shard_map.59), calls=%async_computation | async-start | bytes 2097152 | tf_op jit(solution)/shard_map/all_to_all | solution.py:289
  21.5 1.6 %collective-permute-start.3 = (bf16[3,64,512]{2,1,0:T(8,128)(2,1)S(1)}, bf16[3,64,512]{2,1,0:T(8,128)(2,1)S(1)}, u32[]{:S(2)}, u32[]{:S(2)}) collective-permute-start(bf16[3,64,512]{2,1,0:T(8,128)(2,1)S(1)} %pad_maximum_fusion.here_ref), channel_id=1, source_target_pairs={{0,8},{8,0},{16,24},{24,16},{32,40},{40,32},{48,56},{56,48},{64,72... | collective-permute-start | bytes 589832 | tf_op jit(solution)/shard_map/ppermute | solution.py:271
  23.1 0.1 stack.40.info_ref
  23.2 1.0 collective-permute-done.3.there_ref
  24.2 0.7 copy-done.2
  24.8 0.9 copy-done.3
  25.8 2.4 %shard_map.60 = (f32[4,64,512]{2,1,0:T(8,128)S(1)}, f32[4,64,512]{2,1,0:T(8,128)S(1)}) custom-call(s32[5]{0:T(128)S(1)} %stack.40.info_ref, bf16[3,64,512]{2,1,0:T(8,128)(2,1)S(1)} %pad_maximum_fusion.here_ref, bf16[3,64,512]{2,1,0:T(8,128)(2,1)S(1)} %copy-done.3, bf16[3,576,512]{2,1,0:T(8,128)(2,1)S(1)} %bitcast.21), custom_call_target="tpu_custom_call" | custom-call | flops 905969664 | bytes 2162708 | tf_op jit(solution)/shard_map/pallas_call | solution.py:228
  28.1 0.8 copy-done.6
  28.9 7.1 %all-to-all-done.mine_ref = bf16[8,128,512]{2,1,0:T(8,128)(2,1)S(1)} async-done(((bf16[8,128,512]{2,1,0:T(8,128)(2,1)}), bf16[8,128,512]{2,1,0:T(8,128)(2,1)S(1)}, u32[]{:S(2)}, u32[]{:S(2)}) %all-to-all-start) | async-done | bytes 1048608 | tf_op jit(solution)/shard_map/all_to_all | solution.py:289
  36.0 1.9 %collective-permute-start.4 = (bf16[8,128,512]{2,1,0:T(8,128)(2,1)S(1)}, bf16[8,128,512]{2,1,0:T(8,128)(2,1)S(1)}, u32[]{:S(2)}, u32[]{:S(2)}) collective-permute-start(bf16[8,128,512]{2,1,0:T(8,128)(2,1)S(1)} %all-to-all-done.mine_ref), channel_id=1, source_target_pairs={{0,8},{8,0},{16,24},{24,16},{32,40},{40,32},{48,56},{56,48},{64,72... | collective-permute-start | bytes 3145736 | tf_op jit(solution)/shard_map/ppermute | solution.py:271
  38.0 0.7 collective-permute-start.5
  38.7 1.5 %collective-permute-done.4.other_ref = bf16[8,128,512]{2,1,0:T(8,128)(2,1)S(1)} collective-permute-done((bf16[8,128,512]{2,1,0:T(8,128)(2,1)S(1)}, bf16[8,128,512]{2,1,0:T(8,128)(2,1)S(1)}, u32[]{:S(2)}, u32[]{:S(2)}) %collective-permute-start.4) | collective-permute-done | bytes 1048608 | tf_op jit(solution)/shard_map/ppermute | solution.py:271
  40.3 0.9 copy-done.4
  41.2 2.6 %shard_map.61 = f32[8,224,128]{2,1,0:T(8,128)S(1)} custom-call(s32[5]{0:T(128)S(1)} %stack.40.info_ref, bf16[8,128,512]{2,1,0:T(8,128)(2,1)S(1)} %all-to-all-done.mine_ref, bf16[8,128,512]{2,1,0:T(8,128)(2,1)S(1)} %collective-permute-done.4.other_ref, bf16[3,64,512]{2,1,0:T(8,128)(2,1)S(1)} %pad_maximum_fusion.here_ref, bf16[3,64,512]{2,1,0:T(8,128)(2,1)S(1)} %copy-done.4), custom_call_target="tpu_custom_call" | custom-call | flops 905969664 | bytes 2490388 | tf_op jit(solution)/shard_map/pallas_call | solution.py:228
  43.8 0.8 convert_element_type.32
  44.6 4.8 %all-to-all-start.1 = ((f16[8,224,128]{2,1,0:T(8,128)(2,1)}), f16[8,224,128]{2,1,0:T(8,128)(2,1)S(1)}, u32[]{:S(2)}, u32[]{:S(2)}) async-start(f16[8,224,128]{2,1,0:T(8,128)(2,1)} %convert_element_type.32), calls=%async_computation.1 | async-start | bytes 917504 | tf_op jit(solution)/shard_map/all_to_all | solution.py:323
  49.4 2.4 %collective-permute-done.5 = f32[4,64,512]{2,1,0:T(8,128)} collective-permute-done((f32[4,64,512]{2,1,0:T(8,128)}, f32[4,64,512]{2,1,0:T(8,128)}, u32[]{:S(2)}, u32[]{:S(2)}) %collective-permute-start.5) | collective-permute-done | bytes 524320 | tf_op jit(solution)/shard_map/ppermute | solution.py:326
  51.9 1.2 %fusion = (f32[64,512]{1,0:T(8,128)S(1)}, f32[64,512]{1,0:T(8,128)S(1)}, f32[64,512]{1,0:T(8,128)S(1)}, f32[64,512]{1,0:T(8,128)S(1)}) fusion(f32[4,64,512]{2,1,0:T(8,128)} %collective-permute-done.5, f32[4,64,512]{2,1,0:T(8,128)S(1)} %get-tuple-element.39), kind=kLoop, calls=%fused_computation.2 | loop fusion | flops 131072 | bytes 1572864 | tf_op jit(solution)/shard_map/add | solution.py:329
  53.0 0.5 collective-permute-start.8
  53.6 1.6 %collective-permute-start.7 = (f32[64,512]{1,0:T(8,128)S(1)}, f32[64,512]{1,0:T(8,128)S(1)}, u32[]{:S(2)}, u32[]{:S(2)}) collective-permute-start(f32[64,512]{1,0:T(8,128)S(1)} %get-tuple-element.56), channel_id=1, source_target_pairs={{0,4},{1,5},{2,6},{3,7},{4,0},{5,1},{6,2},{7,3},{8,12},{9,13},{10,... | collective-permute-start | bytes 393224 | tf_op jit(solution)/shard_map/ppermute | solution.py:326
  55.2 1.2 %collective-permute-start.6 = (f32[64,512]{1,0:T(8,128)S(1)}, f32[64,512]{1,0:T(8,128)S(1)}, u32[]{:S(2)}, u32[]{:S(2)}) collective-permute-start(f32[64,512]{1,0:T(8,128)S(1)} %get-tuple-element.57), channel_id=1, source_target_pairs={{0,2},{1,3},{2,0},{3,1},{4,6},{5,7},{6,4},{7,5},{8,10},{9,11},{10,... | collective-permute-start | bytes 393224 | tf_op jit(solution)/shard_map/ppermute | solution.py:326
  56.4 5.0 %collective-permute-done.8 = f32[64,512]{1,0:T(8,128)S(1)} collective-permute-done((f32[64,512]{1,0:T(8,128)S(1)}, f32[64,512]{1,0:T(8,128)S(1)}, u32[]{:S(2)}, u32[]{:S(2)}) %collective-permute-start.8) | collective-permute-done | bytes 131104 | tf_op jit(solution)/shard_map/ppermute | solution.py:326
  61.4 0.3 collective-permute-done.6
  61.7 4.3 %all-to-all-done.1 = f16[8,224,128]{2,1,0:T(8,128)(2,1)S(1)} async-done(((f16[8,224,128]{2,1,0:T(8,128)(2,1)}), f16[8,224,128]{2,1,0:T(8,128)(2,1)S(1)}, u32[]{:S(2)}, u32[]{:S(2)}) %all-to-all-start.1) | async-done | bytes 458784 | tf_op jit(solution)/shard_map/all_to_all | solution.py:323
  66.1 0.2 shard_map.62
  66.3 0.8 broadcast_in_dim.12
  67.1 4.6 %all-to-all-start.2 = ((f16[8,224,128]{2,1,0:T(8,128)(2,1)}), f16[8,224,128]{2,1,0:T(8,128)(2,1)S(1)}, u32[]{:S(2)}, u32[]{:S(2)}) async-start(f16[8,224,128]{2,1,0:T(8,128)(2,1)} %broadcast_in_dim.12), calls=%async_computation.2 | async-start | bytes 917504 | tf_op jit(solution)/shard_map/all_to_all | solution.py:279
  71.7 1.5 %copy-done.1 = bf16[3,3,3,64,512]{4,3,2,1,0:T(8,128)(2,1)S(1)} copy-done((bf16[3,3,3,64,512]{4,3,2,1,0:T(8,128)(2,1)S(1)}, bf16[3,3,3,64,512]{4,3,2,1,0:T(8,128)(2,1)}, u32[]{:S(2)}) %copy-start.1) | copy-done | bytes 1769496
  73.2 2.7 %shard_map.63 = bf16[64,512]{1,0:T(8,128)(2,1)} custom-call(s32[5]{0:T(128)S(1)} %stack.40.info_ref, bf16[8,128,512]{2,1,0:T(8,128)(2,1)S(1)} %all-to-all-done.mine_ref, bf16[8,128,512]{2,1,0:T(8,128)(2,1)S(1)} %collective-permute-done.4.other_ref, bf16[3,576,512]{2,1,0:T(8,128)(2,1)S(1)} %bitcast.22), custom_call_target="tpu_custom_call" | custom-call | flops 905969664 | bytes 3866644 | tf_op jit(solution)/shard_map/pallas_call | solution.py:228
  75.9 0.7 add_convert_fusion
  76.6 10.5 %all-to-all-done.2 = f16[8,224,128]{2,1,0:T(8,128)(2,1)S(1)} async-done(((f16[8,224,128]{2,1,0:T(8,128)(2,1)}), f16[8,224,128]{2,1,0:T(8,128)(2,1)S(1)}, u32[]{:S(2)}, u32[]{:S(2)}) %all-to-all-start.2) | async-done | bytes 458784 | tf_op jit(solution)/shard_map/all_to_all | solution.py:279
  87.1 1.2 %collective-permute-start.9 = (f16[8,224,128]{2,1,0:T(8,128)(2,1)S(1)}, f16[8,224,128]{2,1,0:T(8,128)(2,1)S(1)}, u32[]{:S(2)}, u32[]{:S(2)}) collective-permute-start(f16[8,224,128]{2,1,0:T(8,128)(2,1)S(1)} %all-to-all-done.2), channel_id=1, source_target_pairs={{0,8},{8,0},{16,24},{24,16},{32,40},{40,32},{48,56},{56,48},{64,72... | collective-permute-start | bytes 1376264 | tf_op jit(solution)/shard_map/ppermute | solution.py:271
  88.2 0.1 fusion.4
  88.4 1.5 %collective-permute-start.10 = (f16[4,224,128]{2,1,0:T(8,128)(2,1)S(1)}, f16[4,224,128]{2,1,0:T(8,128)(2,1)S(1)}, u32[]{:S(2)}, u32[]{:S(2)}) collective-permute-start(f16[4,224,128]{2,1,0:T(8,128)(2,1)S(1)} %get-tuple-element.60), channel_id=1, source_target_pairs={{0,32},{8,40},{16,48},{24,56},{32,64},{40,72},{48,80},{56,88},{64,... | collective-permute-start | bytes 688136 | tf_op jit(solution)/shard_map/ppermute | solution.py:355
  90.0 1.9 %shard_map.64.refs_4_ = f32[3,576,512]{2,1,0:T(8,128)} custom-call(s32[5]{0:T(128)S(1)} %stack.40.info_ref, f32[8,224,128]{2,1,0:T(8,128)S(1)} %convert_element_type.36.refs_0_, f32[8,224,128]{2,1,0:T(8,128)S(1)} %convert_element_type.37.refs_1_), custom_call_target="tpu_custom_call" | custom-call | bytes 1835028 | tf_op jit(solution)/shard_map/pallas_call | solution.py:228
  91.9 3.7 %collective-permute-done.11 = f16[4,224,128]{2,1,0:T(8,128)(2,1)S(1)} collective-permute-done((f16[4,224,128]{2,1,0:T(8,128)(2,1)S(1)}, f16[4,224,128]{2,1,0:T(8,128)(2,1)S(1)}, u32[]{:S(2)}, u32[]{:S(2)}) %collective-permute-start.11) | collective-permute-done | bytes 229408 | tf_op jit(solution)/shard_map/ppermute | solution.py:356
  95.6 1.1 %collective-permute-done.10 = f16[4,224,128]{2,1,0:T(8,128)(2,1)S(1)} collective-permute-done((f16[4,224,128]{2,1,0:T(8,128)(2,1)S(1)}, f16[4,224,128]{2,1,0:T(8,128)(2,1)S(1)}, u32[]{:S(2)}, u32[]{:S(2)}) %collective-permute-start.10) | collective-permute-done | bytes 229408 | tf_op jit(solution)/shard_map/ppermute | solution.py:355
  96.7 1.0 collective-permute-start.12
  97.8 1.0 %collective-permute-done.12 = f16[4,224,128]{2,1,0:T(8,128)(2,1)S(1)} collective-permute-done((f16[4,224,128]{2,1,0:T(8,128)(2,1)S(1)}, f16[4,224,128]{2,1,0:T(8,128)(2,1)S(1)}, u32[]{:S(2)}, u32[]{:S(2)}) %collective-permute-start.12) | collective-permute-done | bytes 229408 | tf_op jit(solution)/shard_map/ppermute | solution.py:271
  98.9 0.3 collective-permute-done.13
  99.2 1.9 %shard_map.65 = f32[3,576,512]{2,1,0:T(8,128)} custom-call(s32[5]{0:T(128)S(1)} %stack.40.info_ref, f32[4,224,128]{2,1,0:T(8,128)S(1)} %convert_element_type.38.refs_0_, f32[4,224,128]{2,1,0:T(8,128)S(1)} %convert_element_type.39.refs_1_, f32[4,224,128]{2,1,0:T(8,128)S(1)} %convert_element_type.40.refs_2_, ...), custom_call_target="tpu_custom_call", output_to_operand_aliasing={{}: (5, {})} | custom-call | bytes 1835028 | tf_op jit(solution)/shard_map/pallas_call | solution.py:228
  (25 shorter events, 0.5 us)
Async XLA Ops:
  0.6 24.2 %copy-start = (bf16[3,3,3,64,512]{4,3,2,1,0:T(8,128)(2,1)S(1)}, bf16[3,3,3,64,512]{4,3,2,1,0:T(8,128)(2,1)}, u32[]{:S(2)}) copy-start(bf16[3,3,3,64,512]{4,3,2,1,0:T(8,128)(2,1)} %param.4) | copy-start | bytes 5308420
  0.6 14.4 %collective-permute-start = (bf16[64,512]{1,0:T(8,128)(2,1)}, bf16[64,512]{1,0:T(8,128)(2,1)S(1)}, u32[]{:S(2)}, u32[]{:S(2)}) collective-permute-start(bf16[64,512]{1,0:T(8,128)(2,1)} %bitcast.23), channel_id=1, source_target_pairs={{0,248},{8,16},{16,8},{24,32},{32,24},{40,48},{48,40},{56,64},{64,... | collective-permute-start | bytes 196616 | tf_op jit(solution)/shard_map/ppermute | solution.py:281
  5.0 10.0 %collective-permute-start.2 = (bf16[64,512]{1,0:T(8,128)(2,1)}, bf16[64,512]{1,0:T(8,128)(2,1)S(1)}, u32[]{:S(2)}, u32[]{:S(2)}) collective-permute-start(bf16[64,512]{1,0:T(8,128)(2,1)} %bitcast.28), channel_id=1, source_target_pairs={{0,16},{8,24},{16,0},{24,8},{32,48},{40,56},{48,32},{56,40},{64,80... | collective-permute-start | bytes 196616 | tf_op jit(solution)/shard_map/ppermute | solution.py:271
  6.4 10.0 %collective-permute-start.1 = (bf16[64,512]{1,0:T(8,128)(2,1)}, bf16[64,512]{1,0:T(8,128)(2,1)S(1)}, u32[]{:S(2)}, u32[]{:S(2)}) collective-permute-start(bf16[64,512]{1,0:T(8,128)(2,1)} %bitcast.29), channel_id=1, source_target_pairs={{0,248},{8,16},{16,8},{24,32},{32,24},{40,48},{48,40},{56,64},{64,... | collective-permute-start | bytes 196616 | tf_op jit(solution)/shard_map/ppermute | solution.py:282
  13.3 0.8 copy-start.5
  14.1 7.3 %copy-start.7 = (bf16[1,64,512]{2,1,0:T(8,128)(2,1)S(1)}, bf16[1,64,512]{2,1,0:T(8,128)(2,1)}, u32[]{:S(2)}) copy-start(bf16[1,64,512]{2,1,0:T(8,128)(2,1)} %param.5) | copy-start | bytes 196612
  17.3 18.7 %all-to-all-start = ((bf16[8,128,512]{2,1,0:T(8,128)(2,1)}), bf16[8,128,512]{2,1,0:T(8,128)(2,1)S(1)}, u32[]{:S(2)}, u32[]{:S(2)}) async-start(bf16[8,128,512]{2,1,0:T(8,128)(2,1)} %shard_map.59), calls=%async_computation | async-start | bytes 2097152 | tf_op jit(solution)/shard_map/all_to_all | solution.py:289
  21.5 2.7 %collective-permute-start.3 = (bf16[3,64,512]{2,1,0:T(8,128)(2,1)S(1)}, bf16[3,64,512]{2,1,0:T(8,128)(2,1)S(1)}, u32[]{:S(2)}, u32[]{:S(2)}) collective-permute-start(bf16[3,64,512]{2,1,0:T(8,128)(2,1)S(1)} %pad_maximum_fusion.here_ref), channel_id=1, source_target_pairs={{0,8},{8,0},{16,24},{24,16},{32,40},{40,32},{48,56},{56,48},{64,72... | collective-permute-start | bytes 589832 | tf_op jit(solution)/shard_map/ppermute | solution.py:271
  24.2 0.7 copy-start.2
  24.8 0.9 copy-start.3
  28.1 0.8 copy-start.6
  36.0 4.2 %collective-permute-start.4 = (bf16[8,128,512]{2,1,0:T(8,128)(2,1)S(1)}, bf16[8,128,512]{2,1,0:T(8,128)(2,1)S(1)}, u32[]{:S(2)}, u32[]{:S(2)}) collective-permute-start(bf16[8,128,512]{2,1,0:T(8,128)(2,1)S(1)} %all-to-all-done.mine_ref), channel_id=1, source_target_pairs={{0,8},{8,0},{16,24},{24,16},{32,40},{40,32},{48,56},{56,48},{64,72... | collective-permute-start | bytes 3145736 | tf_op jit(solution)/shard_map/ppermute | solution.py:271
  38.0 13.9 %collective-permute-start.5 = (f32[4,64,512]{2,1,0:T(8,128)}, f32[4,64,512]{2,1,0:T(8,128)}, u32[]{:S(2)}, u32[]{:S(2)}) collective-permute-start(f32[4,64,512]{2,1,0:T(8,128)} %copy-done.6), channel_id=1, source_target_pairs={{0,1},{1,0},{2,3},{3,2},{4,5},{5,4},{6,7},{7,6},{8,9},{9,8},{10,11... | collective-permute-start | bytes 1572872 | tf_op jit(solution)/shard_map/ppermute | solution.py:326
  40.3 0.9 copy-start.4
  44.6 21.3 %all-to-all-start.1 = ((f16[8,224,128]{2,1,0:T(8,128)(2,1)}), f16[8,224,128]{2,1,0:T(8,128)(2,1)S(1)}, u32[]{:S(2)}, u32[]{:S(2)}) async-start(f16[8,224,128]{2,1,0:T(8,128)(2,1)} %convert_element_type.32), calls=%async_computation.1 | async-start | bytes 917504 | tf_op jit(solution)/shard_map/all_to_all | solution.py:323
  53.0 8.4 %collective-permute-start.8 = (f32[64,512]{1,0:T(8,128)S(1)}, f32[64,512]{1,0:T(8,128)S(1)}, u32[]{:S(2)}, u32[]{:S(2)}) collective-permute-start(f32[64,512]{1,0:T(8,128)S(1)} %get-tuple-element.55), channel_id=1, source_target_pairs={{0,6},{1,7},{2,4},{3,5},{4,2},{5,3},{6,0},{7,1},{8,14},{9,15},{10,... | collective-permute-start | bytes 393224 | tf_op jit(solution)/shard_map/ppermute | solution.py:326
  53.6 7.8 %collective-permute-start.7 = (f32[64,512]{1,0:T(8,128)S(1)}, f32[64,512]{1,0:T(8,128)S(1)}, u32[]{:S(2)}, u32[]{:S(2)}) collective-permute-start(f32[64,512]{1,0:T(8,128)S(1)} %get-tuple-element.56), channel_id=1, source_target_pairs={{0,4},{1,5},{2,6},{3,7},{4,0},{5,1},{6,2},{7,3},{8,12},{9,13},{10,... | collective-permute-start | bytes 393224 | tf_op jit(solution)/shard_map/ppermute | solution.py:326
  55.2 6.5 %collective-permute-start.6 = (f32[64,512]{1,0:T(8,128)S(1)}, f32[64,512]{1,0:T(8,128)S(1)}, u32[]{:S(2)}, u32[]{:S(2)}) collective-permute-start(f32[64,512]{1,0:T(8,128)S(1)} %get-tuple-element.57), channel_id=1, source_target_pairs={{0,2},{1,3},{2,0},{3,1},{4,6},{5,7},{6,4},{7,5},{8,10},{9,11},{10,... | collective-permute-start | bytes 393224 | tf_op jit(solution)/shard_map/ppermute | solution.py:326
  67.1 20.0 %all-to-all-start.2 = ((f16[8,224,128]{2,1,0:T(8,128)(2,1)}), f16[8,224,128]{2,1,0:T(8,128)(2,1)S(1)}, u32[]{:S(2)}, u32[]{:S(2)}) async-start(f16[8,224,128]{2,1,0:T(8,128)(2,1)} %broadcast_in_dim.12), calls=%async_computation.2 | async-start | bytes 917504 | tf_op jit(solution)/shard_map/all_to_all | solution.py:279
  71.7 1.5 %copy-start.1 = (bf16[3,3,3,64,512]{4,3,2,1,0:T(8,128)(2,1)S(1)}, bf16[3,3,3,64,512]{4,3,2,1,0:T(8,128)(2,1)}, u32[]{:S(2)}) copy-start(bf16[3,3,3,64,512]{4,3,2,1,0:T(8,128)(2,1)} %param.4) | copy-start | bytes 5308420
  87.1 2.9 %collective-permute-start.9 = (f16[8,224,128]{2,1,0:T(8,128)(2,1)S(1)}, f16[8,224,128]{2,1,0:T(8,128)(2,1)S(1)}, u32[]{:S(2)}, u32[]{:S(2)}) collective-permute-start(f16[8,224,128]{2,1,0:T(8,128)(2,1)S(1)} %all-to-all-done.2), channel_id=1, source_target_pairs={{0,8},{8,0},{16,24},{24,16},{32,40},{40,32},{48,56},{56,48},{64,72... | collective-permute-start | bytes 1376264 | tf_op jit(solution)/shard_map/ppermute | solution.py:271
  88.3 7.3 %collective-permute-start.11 = (f16[4,224,128]{2,1,0:T(8,128)(2,1)S(1)}, f16[4,224,128]{2,1,0:T(8,128)(2,1)S(1)}, u32[]{:S(2)}, u32[]{:S(2)}) collective-permute-start(f16[4,224,128]{2,1,0:T(8,128)(2,1)S(1)} %get-tuple-element.59), channel_id=1, source_target_pairs={{0,224},{8,232},{16,240},{24,248},{32,0},{40,8},{48,16},{56,24},{6... | collective-permute-start | bytes 688136 | tf_op jit(solution)/shard_map/ppermute | solution.py:356
  88.4 8.3 %collective-permute-start.10 = (f16[4,224,128]{2,1,0:T(8,128)(2,1)S(1)}, f16[4,224,128]{2,1,0:T(8,128)(2,1)S(1)}, u32[]{:S(2)}, u32[]{:S(2)}) collective-permute-start(f16[4,224,128]{2,1,0:T(8,128)(2,1)S(1)} %get-tuple-element.60), channel_id=1, source_target_pairs={{0,32},{8,40},{16,48},{24,56},{32,64},{40,72},{48,80},{56,88},{64,... | collective-permute-start | bytes 688136 | tf_op jit(solution)/shard_map/ppermute | solution.py:355
  96.7 2.1 %collective-permute-start.12 = (f16[4,224,128]{2,1,0:T(8,128)(2,1)S(1)}, f16[4,224,128]{2,1,0:T(8,128)(2,1)S(1)}, u32[]{:S(2)}, u32[]{:S(2)}) collective-permute-start(f16[4,224,128]{2,1,0:T(8,128)(2,1)S(1)} %collective-permute-done.10), channel_id=1, source_target_pairs={{0,8},{8,0},{16,24},{24,16},{32,40},{40,32},{48,56},{56,48},{64,72... | collective-permute-start | bytes 688136 | tf_op jit(solution)/shard_map/ppermute | solution.py:271
  97.7 1.5 %collective-permute-start.13 = (f16[4,224,128]{2,1,0:T(8,128)(2,1)S(1)}, f16[4,224,128]{2,1,0:T(8,128)(2,1)S(1)}, u32[]{:S(2)}, u32[]{:S(2)}) collective-permute-start(f16[4,224,128]{2,1,0:T(8,128)(2,1)S(1)} %collective-permute-done.11), channel_id=1, source_target_pairs={{0,8},{8,0},{16,24},{24,16},{32,40},{40,32},{48,56},{56,48},{64,72... | collective-permute-start | bytes 688136 | tf_op jit(solution)/shard_map/ppermute | solution.py:271

commit v6 on v5

--- a/solution.py
+++ b/solution.py
@@ -280,7 +280,8 @@
 
     x_halo = lax.ppermute(x_own, "gz", outward)
     c_halo = lax.ppermute(c_own, "gz", outward)
-    across = xor(c_own, 2)
+    inward = [(4 * g + 3 * r, 4 * g + 2 - r) for g in range(quads) for r in range(2)]
+    across = lax.ppermute(c_own, "gz", inward)
     shape = jax.ShapeDtypeStruct((cols, 2 * local, cells), bf16)
     scratch = [pltpu.SemaphoreType.DMA((cols,))]
     send = call(functools.partial(pack_kernel, 0), shape, scratch, 0, x_own, spaces=ANY)

time: 102 us -> 102 us (level)
  starting transfers between devices: 37.5 us -> 40.9 us
  waiting for transfers between devices: 39.7 us -> 36.7 us
    all_to_all x1, waiting for transfers between devices: 7.1 us -> 0.01 us  [body(): gathered = lax.all_to_all(send, 'col', 0, 0, tiled=True)]
    ppermute x6 -> x5, starting transfers between devices: 7.09 us -> 13.9 us  [xor(): return lax.ppermute(value, 'gz', [(i, i ^ bits) for i in range(devices)])]
    ppermute x1, starting transfers between devices: 6.85 us -> 0.24 us  [body(): c_halo = lax.ppermute(c_own, 'gz', outward)]
    ppermute x0 -> x1, waiting for transfers between devices: none -> 4.76 us  [body(): across = lax.ppermute(c_own, 'gz', inward)]
    ppermute x1, starting transfers between devices: 0.08 us -> 2.47 us  [body(): lax.ppermute(second, 'gz', [(i, (i - 4) % devices) for i in range(devices)])]
    ppermute x1, waiting for transfers between devices: 1.1 us -> 3.09 us  [body(): lax.ppermute(first, 'gz', [(i, (i + 4) % devices) for i in range(devices)])]
    all_to_all x1, starting transfers between devices: 4.79 us -> 6.45 us  [body(): lax.all_to_all(grads.astype(f16), 'gz', 0, 0, axis_index_groups=ring, til...]
    all_to_all x1, waiting for transfers between devices: 4.26 us -> 5.91 us  [body(): lax.all_to_all(grads.astype(f16), 'gz', 0, 0, axis_index_groups=ring, til...]
  transfers between devices with their start and end apart: 17 -> 17, of which waited for: 13 -> 12; matrix products, arithmetic and copies ran while one was open for 3% -> 3% of each run, Pallas kernels for 10% -> 10%
where the time goes in v6:
time: 102 us
  starting transfers between devices  40.9 us (40%)
  waiting for transfers between devices  36.7 us (36%)
  Pallas kernels  13.4 us (13%)
  local copies, waits for them, and re-layouts  6.67 us (7%)
  other arithmetic  3.01 us (3%)
    ppermute x5, starting transfers between devices, xor(): return lax.ppermute(value, 'gz', [(i, i ^ bits) for i in range(devices)])  13.9 us
    pallas_call x8, Pallas kernels, call(): pl.pallas_call(kernel, out_shape=out, in_specs=[SMEM if a.dtype == jnp.in...  13.4 us
    all_to_all x1, waiting for transfers between devices, everywhere(): lax.all_to_all(copies, axis, 0, 0, axis_index_groups=groups, tiled=True)  10.4 us
    all_to_all x1, starting transfers between devices, body(): lax.all_to_all(grads.astype(f16), 'gz', 0, 0, axis_index_groups=ring, til...  6.45 us
    ppermute x4, waiting for transfers between devices, exchanged(): return lax.ppermute(value, 'col', [(j, j ^ bits) for j in range(cols)])  6.12 us
    all_to_all x1, waiting for transfers between devices, body(): lax.all_to_all(grads.astype(f16), 'gz', 0, 0, axis_index_groups=ring, til...  5.91 us
    unnamed x16, local copies, waits for them, and re-layouts  5.67 us
    ppermute x1, waiting for transfers between devices, body(): across = lax.ppermute(c_own, 'gz', inward)  4.76 us
  transfers between devices with their start and end apart: 17, of which 12 were waited for; matrix products, arithmetic and copies ran while one was open for 3% of the time, Pallas kernels for 10%

profile of v6, /device:TPU:1, one launch (start us, length us, event | category | flops | bytes accessed | tf_op | source)
XLA Modules:
  0.0 101.6 jit_solution(8322220293873315038)
XLA Ops:
  0.6 4.4 %collective-permute-start = (bf16[64,512]{1,0:T(8,128)(2,1)}, bf16[64,512]{1,0:T(8,128)(2,1)S(1)}, u32[]{:S(2)}, u32[]{:S(2)}) collective-permute-start(bf16[64,512]{1,0:T(8,128)(2,1)} %bitcast.23), channel_id=1, source_target_pairs={{0,248},{8,16},{16,8},{24,32},{32,24},{40,48},{48,40},{56,64},{64,... | collective-permute-start | bytes 196616 | tf_op jit(solution)/shard_map/ppermute | solution.py:281
  5.0 1.3 %collective-permute-start.2 = (bf16[64,512]{1,0:T(8,128)(2,1)}, bf16[64,512]{1,0:T(8,128)(2,1)S(1)}, u32[]{:S(2)}, u32[]{:S(2)}) collective-permute-start(bf16[64,512]{1,0:T(8,128)(2,1)} %bitcast.28), channel_id=1, source_target_pairs={{0,16},{24,8},{32,48},{56,40},{64,80},{88,72},{96,112},{120,104},{... | collective-permute-start | bytes 196616 | tf_op jit(solution)/shard_map/ppermute | solution.py:284
  6.3 0.2 collective-permute-start.1
  6.6 0.8 copy-done.5
  7.4 0.8 shard_map.58.refs_0_
  8.3 4.8 %collective-permute-done.2 = bf16[64,512]{1,0:T(8,128)(2,1)S(1)} collective-permute-done((bf16[64,512]{1,0:T(8,128)(2,1)}, bf16[64,512]{1,0:T(8,128)(2,1)S(1)}, u32[]{:S(2)}, u32[]{:S(2)}) %collective-permute-start.2) | collective-permute-done | bytes 65568 | tf_op jit(solution)/shard_map/ppermute | solution.py:284
  13.0 0.8 shard_map.59
  13.9 4.1 %all-to-all-start = ((bf16[8,128,512]{2,1,0:T(8,128)(2,1)}), bf16[8,128,512]{2,1,0:T(8,128)(2,1)S(1)}, u32[]{:S(2)}, u32[]{:S(2)}) async-start(bf16[8,128,512]{2,1,0:T(8,128)(2,1)} %shard_map.59), calls=%async_computation | async-start | bytes 2097152 | tf_op jit(solution)/shard_map/all_to_all | solution.py:290
  18.1 6.4 %collective-permute-start.3 = (bf16[3,64,512]{2,1,0:T(8,128)(2,1)S(1)}, bf16[3,64,512]{2,1,0:T(8,128)(2,1)S(1)}, u32[]{:S(2)}, u32[]{:S(2)}) collective-permute-start(bf16[3,64,512]{2,1,0:T(8,128)(2,1)S(1)} %pad_maximum_fusion.here_ref), channel_id=1, source_target_pairs={{0,8},{8,0},{16,24},{24,16},{32,40},{40,32},{48,56},{56,48},{64,72... | collective-permute-start | bytes 589832 | tf_op jit(solution)/shard_map/ppermute | solution.py:271
  24.5 0.1 stack.40.info_ref
  24.5 1.0 collective-permute-done.3.there_ref
  25.5 0.7 copy-done.2
  26.2 0.9 copy-done.3
  27.1 2.4 %shard_map.60 = (f32[4,64,512]{2,1,0:T(8,128)S(1)}, f32[4,64,512]{2,1,0:T(8,128)S(1)}) custom-call(s32[5]{0:T(128)S(1)} %stack.40.info_ref, bf16[3,64,512]{2,1,0:T(8,128)(2,1)S(1)} %pad_maximum_fusion.here_ref, bf16[3,64,512]{2,1,0:T(8,128)(2,1)S(1)} %copy-done.3, bf16[3,576,512]{2,1,0:T(8,128)(2,1)S(1)} %bitcast.21), custom_call_target="tpu_custom_call" | custom-call | flops 905969664 | bytes 2162708 | tf_op jit(solution)/shard_map/pallas_call | solution.py:228
  29.5 0.8 copy-done.6
  30.3 5.4 %collective-permute-start.4 = (bf16[8,128,512]{2,1,0:T(8,128)(2,1)S(1)}, bf16[8,128,512]{2,1,0:T(8,128)(2,1)S(1)}, u32[]{:S(2)}, u32[]{:S(2)}) collective-permute-start(bf16[8,128,512]{2,1,0:T(8,128)(2,1)S(1)} %all-to-all-done.mine_ref), channel_id=1, source_target_pairs={{0,8},{8,0},{16,24},{24,16},{32,40},{40,32},{48,56},{56,48},{64,72... | collective-permute-start | bytes 3145736 | tf_op jit(solution)/shard_map/ppermute | solution.py:271
  35.7 1.1 %collective-permute-start.5 = (f32[4,64,512]{2,1,0:T(8,128)}, f32[4,64,512]{2,1,0:T(8,128)}, u32[]{:S(2)}, u32[]{:S(2)}) collective-permute-start(f32[4,64,512]{2,1,0:T(8,128)} %copy-done.6), channel_id=1, source_target_pairs={{0,1},{1,0},{2,3},{3,2},{4,5},{5,4},{6,7},{7,6},{8,9},{9,8},{10,11... | collective-permute-start | bytes 1572872 | tf_op jit(solution)/shard_map/ppermute | solution.py:327
  36.8 1.2 %collective-permute-done.4.other_ref = bf16[8,128,512]{2,1,0:T(8,128)(2,1)S(1)} collective-permute-done((bf16[8,128,512]{2,1,0:T(8,128)(2,1)S(1)}, bf16[8,128,512]{2,1,0:T(8,128)(2,1)S(1)}, u32[]{:S(2)}, u32[]{:S(2)}) %collective-permute-start.4) | collective-permute-done | bytes 1048608 | tf_op jit(solution)/shard_map/ppermute | solution.py:271
  38.0 0.9 copy-done.4
  38.9 2.6 %shard_map.61 = f32[8,224,128]{2,1,0:T(8,128)S(1)} custom-call(s32[5]{0:T(128)S(1)} %stack.40.info_ref, bf16[8,128,512]{2,1,0:T(8,128)(2,1)S(1)} %all-to-all-done.mine_ref, bf16[8,128,512]{2,1,0:T(8,128)(2,1)S(1)} %collective-permute-done.4.other_ref, bf16[3,64,512]{2,1,0:T(8,128)(2,1)S(1)} %pad_maximum_fusion.here_ref, bf16[3,64,512]{2,1,0:T(8,128)(2,1)S(1)} %copy-done.4), custom_call_target="tpu_custom_call" | custom-call | flops 905969664 | bytes 2490388 | tf_op jit(solution)/shard_map/pallas_call | solution.py:228
  41.5 0.8 convert_element_type.32
  42.4 6.4 %all-to-all-start.1 = ((f16[8,224,128]{2,1,0:T(8,128)(2,1)}), f16[8,224,128]{2,1,0:T(8,128)(2,1)S(1)}, u32[]{:S(2)}, u32[]{:S(2)}) async-start(f16[8,224,128]{2,1,0:T(8,128)(2,1)} %convert_element_type.32), calls=%async_computation.1 | async-start | bytes 917504 | tf_op jit(solution)/shard_map/all_to_all | solution.py:324
  48.8 0.8 collective-permute-done.5
  49.6 1.2 %fusion = (f32[64,512]{1,0:T(8,128)S(1)}, f32[64,512]{1,0:T(8,128)S(1)}, f32[64,512]{1,0:T(8,128)S(1)}, f32[64,512]{1,0:T(8,128)S(1)}) fusion(f32[4,64,512]{2,1,0:T(8,128)} %collective-permute-done.5, f32[4,64,512]{2,1,0:T(8,128)S(1)} %get-tuple-element.39), kind=kLoop, calls=%fused_computation.2 | loop fusion | flops 131072 | bytes 1572864 | tf_op jit(solution)/shard_map/add | solution.py:330
  50.8 0.5 collective-permute-start.8
  51.3 1.6 %collective-permute-start.7 = (f32[64,512]{1,0:T(8,128)S(1)}, f32[64,512]{1,0:T(8,128)S(1)}, u32[]{:S(2)}, u32[]{:S(2)}) collective-permute-start(f32[64,512]{1,0:T(8,128)S(1)} %get-tuple-element.56), channel_id=1, source_target_pairs={{0,4},{1,5},{2,6},{3,7},{4,0},{5,1},{6,2},{7,3},{8,12},{9,13},{10,... | collective-permute-start | bytes 393224 | tf_op jit(solution)/shard_map/ppermute | solution.py:327
  52.9 1.2 %collective-permute-start.6 = (f32[64,512]{1,0:T(8,128)S(1)}, f32[64,512]{1,0:T(8,128)S(1)}, u32[]{:S(2)}, u32[]{:S(2)}) collective-permute-start(f32[64,512]{1,0:T(8,128)S(1)} %get-tuple-element.57), channel_id=1, source_target_pairs={{0,2},{1,3},{2,0},{3,1},{4,6},{5,7},{6,4},{7,5},{8,10},{9,11},{10,... | collective-permute-start | bytes 393224 | tf_op jit(solution)/shard_map/ppermute | solution.py:327
  54.1 5.0 %collective-permute-done.8 = f32[64,512]{1,0:T(8,128)S(1)} collective-permute-done((f32[64,512]{1,0:T(8,128)S(1)}, f32[64,512]{1,0:T(8,128)S(1)}, u32[]{:S(2)}, u32[]{:S(2)}) %collective-permute-start.8) | collective-permute-done | bytes 131104 | tf_op jit(solution)/shard_map/ppermute | solution.py:327
  59.1 0.3 collective-permute-done.6
  59.5 5.9 %all-to-all-done.1 = f16[8,224,128]{2,1,0:T(8,128)(2,1)S(1)} async-done(((f16[8,224,128]{2,1,0:T(8,128)(2,1)}), f16[8,224,128]{2,1,0:T(8,128)(2,1)S(1)}, u32[]{:S(2)}, u32[]{:S(2)}) %all-to-all-start.1) | async-done | bytes 458784 | tf_op jit(solution)/shard_map/all_to_all | solution.py:324
  65.4 0.2 shard_map.62
  65.6 0.8 broadcast_in_dim.12
  66.5 3.6 %all-to-all-start.2 = ((f16[8,224,128]{2,1,0:T(8,128)(2,1)}), f16[8,224,128]{2,1,0:T(8,128)(2,1)S(1)}, u32[]{:S(2)}, u32[]{:S(2)}) async-start(f16[8,224,128]{2,1,0:T(8,128)(2,1)} %broadcast_in_dim.12), calls=%async_computation.2 | async-start | bytes 917504 | tf_op jit(solution)/shard_map/all_to_all | solution.py:279
  70.0 1.5 %copy-done.1 = bf16[3,3,3,64,512]{4,3,2,1,0:T(8,128)(2,1)S(1)} copy-done((bf16[3,3,3,64,512]{4,3,2,1,0:T(8,128)(2,1)S(1)}, bf16[3,3,3,64,512]{4,3,2,1,0:T(8,128)(2,1)}, u32[]{:S(2)}) %copy-start.1) | copy-done | bytes 1769496
  71.5 2.7 %shard_map.63 = bf16[64,512]{1,0:T(8,128)(2,1)} custom-call(s32[5]{0:T(128)S(1)} %stack.40.info_ref, bf16[8,128,512]{2,1,0:T(8,128)(2,1)S(1)} %all-to-all-done.mine_ref, bf16[8,128,512]{2,1,0:T(8,128)(2,1)S(1)} %collective-permute-done.4.other_ref, bf16[3,576,512]{2,1,0:T(8,128)(2,1)S(1)} %bitcast.22), custom_call_target="tpu_custom_call" | custom-call | flops 905969664 | bytes 3866644 | tf_op jit(solution)/shard_map/pallas_call | solution.py:228
  74.2 0.7 add_convert_fusion
  74.9 10.4 %all-to-all-done.2 = f16[8,224,128]{2,1,0:T(8,128)(2,1)S(1)} async-done(((f16[8,224,128]{2,1,0:T(8,128)(2,1)}), f16[8,224,128]{2,1,0:T(8,128)(2,1)S(1)}, u32[]{:S(2)}, u32[]{:S(2)}) %all-to-all-start.2) | async-done | bytes 458784 | tf_op jit(solution)/shard_map/all_to_all | solution.py:279
  85.3 1.1 %collective-permute-start.9 = (f16[8,224,128]{2,1,0:T(8,128)(2,1)S(1)}, f16[8,224,128]{2,1,0:T(8,128)(2,1)S(1)}, u32[]{:S(2)}, u32[]{:S(2)}) collective-permute-start(f16[8,224,128]{2,1,0:T(8,128)(2,1)S(1)} %all-to-all-done.2), channel_id=1, source_target_pairs={{0,8},{8,0},{16,24},{24,16},{32,40},{40,32},{48,56},{56,48},{64,72... | collective-permute-start | bytes 1376264 | tf_op jit(solution)/shard_map/ppermute | solution.py:271
  86.3 0.1 fusion.4
  86.4 2.5 %collective-permute-start.11 = (f16[4,224,128]{2,1,0:T(8,128)(2,1)S(1)}, f16[4,224,128]{2,1,0:T(8,128)(2,1)S(1)}, u32[]{:S(2)}, u32[]{:S(2)}) collective-permute-start(f16[4,224,128]{2,1,0:T(8,128)(2,1)S(1)} %get-tuple-element.59), channel_id=1, source_target_pairs={{0,224},{8,232},{16,240},{24,248},{32,0},{40,8},{48,16},{56,24},{6... | collective-permute-start | bytes 688136 | tf_op jit(solution)/shard_map/ppermute | solution.py:357
  89.0 0.1 convert_element_type.37.refs_1_
  89.0 1.9 %shard_map.64.refs_4_ = f32[3,576,512]{2,1,0:T(8,128)} custom-call(s32[5]{0:T(128)S(1)} %stack.40.info_ref, f32[8,224,128]{2,1,0:T(8,128)S(1)} %convert_element_type.36.refs_0_, f32[8,224,128]{2,1,0:T(8,128)S(1)} %convert_element_type.37.refs_1_), custom_call_target="tpu_custom_call" | custom-call | bytes 1835028 | tf_op jit(solution)/shard_map/pallas_call | solution.py:228
  91.0 3.0 %collective-permute-done.11 = f16[4,224,128]{2,1,0:T(8,128)(2,1)S(1)} collective-permute-done((f16[4,224,128]{2,1,0:T(8,128)(2,1)S(1)}, f16[4,224,128]{2,1,0:T(8,128)(2,1)S(1)}, u32[]{:S(2)}, u32[]{:S(2)}) %collective-permute-start.11) | collective-permute-done | bytes 229408 | tf_op jit(solution)/shard_map/ppermute | solution.py:357
  93.9 3.1 %collective-permute-done.10 = f16[4,224,128]{2,1,0:T(8,128)(2,1)S(1)} collective-permute-done((f16[4,224,128]{2,1,0:T(8,128)(2,1)S(1)}, f16[4,224,128]{2,1,0:T(8,128)(2,1)S(1)}, u32[]{:S(2)}, u32[]{:S(2)}) %collective-permute-start.10) | collective-permute-done | bytes 229408 | tf_op jit(solution)/shard_map/ppermute | solution.py:356
  97.0 1.1 %collective-permute-start.12 = (f16[4,224,128]{2,1,0:T(8,128)(2,1)S(1)}, f16[4,224,128]{2,1,0:T(8,128)(2,1)S(1)}, u32[]{:S(2)}, u32[]{:S(2)}) collective-permute-start(f16[4,224,128]{2,1,0:T(8,128)(2,1)S(1)} %collective-permute-done.10), channel_id=1, source_target_pairs={{0,8},{8,0},{16,24},{24,16},{32,40},{40,32},{48,56},{56,48},{64,72... | collective-permute-start | bytes 688136 | tf_op jit(solution)/shard_map/ppermute | solution.py:271
  98.2 1.0 %collective-permute-done.12 = f16[4,224,128]{2,1,0:T(8,128)(2,1)S(1)} collective-permute-done((f16[4,224,128]{2,1,0:T(8,128)(2,1)S(1)}, f16[4,224,128]{2,1,0:T(8,128)(2,1)S(1)}, u32[]{:S(2)}, u32[]{:S(2)}) %collective-permute-start.12) | collective-permute-done | bytes 229408 | tf_op jit(solution)/shard_map/ppermute | solution.py:271
  99.3 0.3 collective-permute-done.13
  99.6 1.9 %shard_map.65 = f32[3,576,512]{2,1,0:T(8,128)} custom-call(s32[5]{0:T(128)S(1)} %stack.40.info_ref, f32[4,224,128]{2,1,0:T(8,128)S(1)} %convert_element_type.38.refs_0_, f32[4,224,128]{2,1,0:T(8,128)S(1)} %convert_element_type.39.refs_1_, f32[4,224,128]{2,1,0:T(8,128)S(1)} %convert_element_type.40.refs_2_, ...), custom_call_target="tpu_custom_call", output_to_operand_aliasing={{}: (5, {})} | custom-call | bytes 1835028 | tf_op jit(solution)/shard_map/pallas_call | solution.py:228
  (25 shorter events, 0.3 us)
Async XLA Ops:
  0.6 25.6 %copy-start = (bf16[3,3,3,64,512]{4,3,2,1,0:T(8,128)(2,1)S(1)}, bf16[3,3,3,64,512]{4,3,2,1,0:T(8,128)(2,1)}, u32[]{:S(2)}) copy-start(bf16[3,3,3,64,512]{4,3,2,1,0:T(8,128)(2,1)} %param.4) | copy-start | bytes 5308420
  0.6 7.6 %collective-permute-start = (bf16[64,512]{1,0:T(8,128)(2,1)}, bf16[64,512]{1,0:T(8,128)(2,1)S(1)}, u32[]{:S(2)}, u32[]{:S(2)}) collective-permute-start(bf16[64,512]{1,0:T(8,128)(2,1)} %bitcast.23), channel_id=1, source_target_pairs={{0,248},{8,16},{16,8},{24,32},{32,24},{40,48},{48,40},{56,64},{64,... | collective-permute-start | bytes 196616 | tf_op jit(solution)/shard_map/ppermute | solution.py:281
  5.0 8.0 %collective-permute-start.2 = (bf16[64,512]{1,0:T(8,128)(2,1)}, bf16[64,512]{1,0:T(8,128)(2,1)S(1)}, u32[]{:S(2)}, u32[]{:S(2)}) collective-permute-start(bf16[64,512]{1,0:T(8,128)(2,1)} %bitcast.28), channel_id=1, source_target_pairs={{0,16},{24,8},{32,48},{56,40},{64,80},{88,72},{96,112},{120,104},{... | collective-permute-start | bytes 196616 | tf_op jit(solution)/shard_map/ppermute | solution.py:284
  6.3 6.7 %collective-permute-start.1 = (bf16[64,512]{1,0:T(8,128)(2,1)}, bf16[64,512]{1,0:T(8,128)(2,1)S(1)}, u32[]{:S(2)}, u32[]{:S(2)}) collective-permute-start(bf16[64,512]{1,0:T(8,128)(2,1)} %bitcast.29), channel_id=1, source_target_pairs={{0,248},{8,16},{16,8},{24,32},{32,24},{40,48},{48,40},{56,64},{64,... | collective-permute-start | bytes 196616 | tf_op jit(solution)/shard_map/ppermute | solution.py:282
  6.6 0.8 copy-start.5
  7.4 10.6 %copy-start.7 = (bf16[1,64,512]{2,1,0:T(8,128)(2,1)S(1)}, bf16[1,64,512]{2,1,0:T(8,128)(2,1)}, u32[]{:S(2)}) copy-start(bf16[1,64,512]{2,1,0:T(8,128)(2,1)} %param.5) | copy-start | bytes 196612
  13.9 16.4 %all-to-all-start = ((bf16[8,128,512]{2,1,0:T(8,128)(2,1)}), bf16[8,128,512]{2,1,0:T(8,128)(2,1)S(1)}, u32[]{:S(2)}, u32[]{:S(2)}) async-start(bf16[8,128,512]{2,1,0:T(8,128)(2,1)} %shard_map.59), calls=%async_computation | async-start | bytes 2097152 | tf_op jit(solution)/shard_map/all_to_all | solution.py:290
  18.1 7.5 %collective-permute-start.3 = (bf16[3,64,512]{2,1,0:T(8,128)(2,1)S(1)}, bf16[3,64,512]{2,1,0:T(8,128)(2,1)S(1)}, u32[]{:S(2)}, u32[]{:S(2)}) collective-permute-start(bf16[3,64,512]{2,1,0:T(8,128)(2,1)S(1)} %pad_maximum_fusion.here_ref), channel_id=1, source_target_pairs={{0,8},{8,0},{16,24},{24,16},{32,40},{40,32},{48,56},{56,48},{64,72... | collective-permute-start | bytes 589832 | tf_op jit(solution)/shard_map/ppermute | solution.py:271
  25.5 0.7 copy-start.2
  26.2 0.9 copy-start.3
  29.5 0.8 copy-start.6
  30.3 7.7 %collective-permute-start.4 = (bf16[8,128,512]{2,1,0:T(8,128)(2,1)S(1)}, bf16[8,128,512]{2,1,0:T(8,128)(2,1)S(1)}, u32[]{:S(2)}, u32[]{:S(2)}) collective-permute-start(bf16[8,128,512]{2,1,0:T(8,128)(2,1)S(1)} %all-to-all-done.mine_ref), channel_id=1, source_target_pairs={{0,8},{8,0},{16,24},{24,16},{32,40},{40,32},{48,56},{56,48},{64,72... | collective-permute-start | bytes 3145736 | tf_op jit(solution)/shard_map/ppermute | solution.py:271
  35.7 13.9 %collective-permute-start.5 = (f32[4,64,512]{2,1,0:T(8,128)}, f32[4,64,512]{2,1,0:T(8,128)}, u32[]{:S(2)}, u32[]{:S(2)}) collective-permute-start(f32[4,64,512]{2,1,0:T(8,128)} %copy-done.6), channel_id=1, source_target_pairs={{0,1},{1,0},{2,3},{3,2},{4,5},{5,4},{6,7},{7,6},{8,9},{9,8},{10,11... | collective-permute-start | bytes 1572872 | tf_op jit(solution)/shard_map/ppermute | solution.py:327
  38.0 0.9 copy-start.4
  42.4 23.0 %all-to-all-start.1 = ((f16[8,224,128]{2,1,0:T(8,128)(2,1)}), f16[8,224,128]{2,1,0:T(8,128)(2,1)S(1)}, u32[]{:S(2)}, u32[]{:S(2)}) async-start(f16[8,224,128]{2,1,0:T(8,128)(2,1)} %convert_element_type.32), calls=%async_computation.1 | async-start | bytes 917504 | tf_op jit(solution)/shard_map/all_to_all | solution.py:324
  50.8 8.4 %collective-permute-start.8 = (f32[64,512]{1,0:T(8,128)S(1)}, f32[64,512]{1,0:T(8,128)S(1)}, u32[]{:S(2)}, u32[]{:S(2)}) collective-permute-start(f32[64,512]{1,0:T(8,128)S(1)} %get-tuple-element.55), channel_id=1, source_target_pairs={{0,6},{1,7},{2,4},{3,5},{4,2},{5,3},{6,0},{7,1},{8,14},{9,15},{10,... | collective-permute-start | bytes 393224 | tf_op jit(solution)/shard_map/ppermute | solution.py:327
  51.3 7.8 %collective-permute-start.7 = (f32[64,512]{1,0:T(8,128)S(1)}, f32[64,512]{1,0:T(8,128)S(1)}, u32[]{:S(2)}, u32[]{:S(2)}) collective-permute-start(f32[64,512]{1,0:T(8,128)S(1)} %get-tuple-element.56), channel_id=1, source_target_pairs={{0,4},{1,5},{2,6},{3,7},{4,0},{5,1},{6,2},{7,3},{8,12},{9,13},{10,... | collective-permute-start | bytes 393224 | tf_op jit(solution)/shard_map/ppermute | solution.py:327
  52.9 6.5 %collective-permute-start.6 = (f32[64,512]{1,0:T(8,128)S(1)}, f32[64,512]{1,0:T(8,128)S(1)}, u32[]{:S(2)}, u32[]{:S(2)}) collective-permute-start(f32[64,512]{1,0:T(8,128)S(1)} %get-tuple-element.57), channel_id=1, source_target_pairs={{0,2},{1,3},{2,0},{3,1},{4,6},{5,7},{6,4},{7,5},{8,10},{9,11},{10,... | collective-permute-start | bytes 393224 | tf_op jit(solution)/shard_map/ppermute | solution.py:327
  66.5 18.8 %all-to-all-start.2 = ((f16[8,224,128]{2,1,0:T(8,128)(2,1)}), f16[8,224,128]{2,1,0:T(8,128)(2,1)S(1)}, u32[]{:S(2)}, u32[]{:S(2)}) async-start(f16[8,224,128]{2,1,0:T(8,128)(2,1)} %broadcast_in_dim.12), calls=%async_computation.2 | async-start | bytes 917504 | tf_op jit(solution)/shard_map/all_to_all | solution.py:279
  70.0 1.5 %copy-start.1 = (bf16[3,3,3,64,512]{4,3,2,1,0:T(8,128)(2,1)S(1)}, bf16[3,3,3,64,512]{4,3,2,1,0:T(8,128)(2,1)}, u32[]{:S(2)}) copy-start(bf16[3,3,3,64,512]{4,3,2,1,0:T(8,128)(2,1)} %param.4) | copy-start | bytes 5308420
  85.3 3.7 %collective-permute-start.9 = (f16[8,224,128]{2,1,0:T(8,128)(2,1)S(1)}, f16[8,224,128]{2,1,0:T(8,128)(2,1)S(1)}, u32[]{:S(2)}, u32[]{:S(2)}) collective-permute-start(f16[8,224,128]{2,1,0:T(8,128)(2,1)S(1)} %all-to-all-done.2), channel_id=1, source_target_pairs={{0,8},{8,0},{16,24},{24,16},{32,40},{40,32},{48,56},{56,48},{64,72... | collective-permute-start | bytes 1376264 | tf_op jit(solution)/shard_map/ppermute | solution.py:271
  86.4 7.5 %collective-permute-start.11 = (f16[4,224,128]{2,1,0:T(8,128)(2,1)S(1)}, f16[4,224,128]{2,1,0:T(8,128)(2,1)S(1)}, u32[]{:S(2)}, u32[]{:S(2)}) collective-permute-start(f16[4,224,128]{2,1,0:T(8,128)(2,1)S(1)} %get-tuple-element.59), channel_id=1, source_target_pairs={{0,224},{8,232},{16,240},{24,248},{32,0},{40,8},{48,16},{56,24},{6... | collective-permute-start | bytes 688136 | tf_op jit(solution)/shard_map/ppermute | solution.py:357
  88.9 8.1 %collective-permute-start.10 = (f16[4,224,128]{2,1,0:T(8,128)(2,1)S(1)}, f16[4,224,128]{2,1,0:T(8,128)(2,1)S(1)}, u32[]{:S(2)}, u32[]{:S(2)}) collective-permute-start(f16[4,224,128]{2,1,0:T(8,128)(2,1)S(1)} %get-tuple-element.60), channel_id=1, source_target_pairs={{0,32},{8,40},{16,48},{24,56},{32,64},{40,72},{48,80},{56,88},{64,... | collective-permute-start | bytes 688136 | tf_op jit(solution)/shard_map/ppermute | solution.py:356
  97.0 2.2 %collective-permute-start.12 = (f16[4,224,128]{2,1,0:T(8,128)(2,1)S(1)}, f16[4,224,128]{2,1,0:T(8,128)(2,1)S(1)}, u32[]{:S(2)}, u32[]{:S(2)}) collective-permute-start(f16[4,224,128]{2,1,0:T(8,128)(2,1)S(1)} %collective-permute-done.10), channel_id=1, source_target_pairs={{0,8},{8,0},{16,24},{24,16},{32,40},{40,32},{48,56},{56,48},{64,72... | collective-permute-start | bytes 688136 | tf_op jit(solution)/shard_map/ppermute | solution.py:271
  98.1 1.5 %collective-permute-start.13 = (f16[4,224,128]{2,1,0:T(8,128)(2,1)S(1)}, f16[4,224,128]{2,1,0:T(8,128)(2,1)S(1)}, u32[]{:S(2)}, u32[]{:S(2)}) collective-permute-start(f16[4,224,128]{2,1,0:T(8,128)(2,1)S(1)} %collective-permute-done.11), channel_id=1, source_target_pairs={{0,8},{8,0},{16,24},{24,16},{32,40},{40,32},{48,56},{56,48},{64,72... | collective-permute-start | bytes 688136 | tf_op jit(solution)/shard_map/ppermute | solution.py:271

commit v7 on v5

--- a/solution.py
+++ b/solution.py
@@ -329,7 +329,9 @@
     pairs = [keep[i] + given[i] for i in range(cols // 2)]
     pieces = pairs[:1] + [exchanged(2 * i, pairs[i]) for i in range(1, cols // 2)]
     other, _ = lax.optimization_barrier((other, given))
-    narrow, pieces, other = lax.optimization_barrier((narrow, pieces, other))
+    near = [pieces[0]] + pieces[1::2]
+    narrow, near, far, other = lax.optimization_barrier((narrow, near, pairs[2], other))
+    pieces = near + [exchanged(4, far)]
     input_grad = sum(pieces[1:], pieces[0]).astype(bf16)
     output = call(
         output_kernel,

time: 102 us -> 102 us (level)
  starting transfers between devices: 37.5 us -> 34.3 us
  waiting for transfers between devices: 39.7 us -> 42.5 us
    all_to_all x1, waiting for transfers between devices: 4.26 us -> 7.42 us  [body(): lax.all_to_all(grads.astype(f16), 'gz', 0, 0, axis_index_groups=ring, til...]
    ppermute x4, starting transfers between devices: 4.08 us -> 1.28 us  [exchanged(): return lax.ppermute(value, 'col', [(j, j ^ bits) for j in range(cols)])]
    all_to_all x1, waiting for transfers between devices: 10.5 us -> 8.67 us  [everywhere(): lax.all_to_all(copies, axis, 0, 0, axis_index_groups=groups, tiled=True)]
    ppermute x4, waiting for transfers between devices: 7.77 us -> 8.95 us  [exchanged(): return lax.ppermute(value, 'col', [(j, j ^ bits) for j in range(cols)])]
where the time goes in v7:
time: 102 us; the launch traced here: 101 us
  waiting for transfers between devices  42.5 us (42%)
  starting transfers between devices  34.3 us (34%)
  Pallas kernels  13.4 us (13%)
  local copies, waits for them, and re-layouts  6.67 us (7%)
  other arithmetic  3.02 us (3%)
    pallas_call x8, Pallas kernels, call(): pl.pallas_call(kernel, out_shape=out, in_specs=[SMEM if a.dtype == jnp.in...  13.4 us
    ppermute x4, waiting for transfers between devices, exchanged(): return lax.ppermute(value, 'col', [(j, j ^ bits) for j in range(cols)])  8.95 us
    all_to_all x1, waiting for transfers between devices, everywhere(): lax.all_to_all(copies, axis, 0, 0, axis_index_groups=groups, tiled=True)  8.67 us
    all_to_all x1, waiting for transfers between devices, body(): lax.all_to_all(grads.astype(f16), 'gz', 0, 0, axis_index_groups=ring, til...  7.42 us
    all_to_all x1, waiting for transfers between devices, body(): gathered = lax.all_to_all(send, 'col', 0, 0, tiled=True)  7.1 us
    ppermute x1, starting transfers between devices, body(): c_halo = lax.ppermute(c_own, 'gz', outward)  6.85 us
    ppermute x6, starting transfers between devices, xor(): return lax.ppermute(value, 'gz', [(i, i ^ bits) for i in range(devices)])  6.63 us
    unnamed x16, local copies, waits for them, and re-layouts  5.66 us
  transfers between devices with their start and end apart: 17, of which 13 were waited for; matrix products, arithmetic and copies ran while one was open for 3% of the time, Pallas kernels for 10%

profile of v7, /device:TPU:1, one launch (start us, length us, event | category | flops | bytes accessed | tf_op | source)
XLA Modules:
  0.0 100.6 jit_solution(13332517680122216159)
XLA Ops:
  0.6 4.4 %collective-permute-start = (bf16[64,512]{1,0:T(8,128)(2,1)}, bf16[64,512]{1,0:T(8,128)(2,1)S(1)}, u32[]{:S(2)}, u32[]{:S(2)}) collective-permute-start(bf16[64,512]{1,0:T(8,128)(2,1)} %bitcast.23), channel_id=1, source_target_pairs={{0,248},{8,16},{16,8},{24,32},{32,24},{40,48},{48,40},{56,64},{64,... | collective-permute-start | bytes 196616 | tf_op jit(solution)/shard_map/ppermute | solution.py:281
  5.0 1.4 %collective-permute-start.2 = (bf16[64,512]{1,0:T(8,128)(2,1)}, bf16[64,512]{1,0:T(8,128)(2,1)S(1)}, u32[]{:S(2)}, u32[]{:S(2)}) collective-permute-start(bf16[64,512]{1,0:T(8,128)(2,1)} %bitcast.28), channel_id=1, source_target_pairs={{0,16},{8,24},{16,0},{24,8},{32,48},{40,56},{48,32},{56,40},{64,80... | collective-permute-start | bytes 196616 | tf_op jit(solution)/shard_map/ppermute | solution.py:271
  6.4 6.9 %collective-permute-start.1 = (bf16[64,512]{1,0:T(8,128)(2,1)}, bf16[64,512]{1,0:T(8,128)(2,1)S(1)}, u32[]{:S(2)}, u32[]{:S(2)}) collective-permute-start(bf16[64,512]{1,0:T(8,128)(2,1)} %bitcast.29), channel_id=1, source_target_pairs={{0,248},{8,16},{16,8},{24,32},{32,24},{40,48},{48,40},{56,64},{64,... | collective-permute-start | bytes 196616 | tf_op jit(solution)/shard_map/ppermute | solution.py:282
  13.3 0.8 copy-done.5
  14.1 0.8 shard_map.58.refs_0_
  15.0 1.4 %collective-permute-done.1 = bf16[64,512]{1,0:T(8,128)(2,1)S(1)} collective-permute-done((bf16[64,512]{1,0:T(8,128)(2,1)}, bf16[64,512]{1,0:T(8,128)(2,1)S(1)}, u32[]{:S(2)}, u32[]{:S(2)}) %collective-permute-start.1) | collective-permute-done | bytes 65568 | tf_op jit(solution)/shard_map/ppermute | solution.py:282
  16.4 0.8 shard_map.59
  17.3 4.1 %all-to-all-start = ((bf16[8,128,512]{2,1,0:T(8,128)(2,1)}), bf16[8,128,512]{2,1,0:T(8,128)(2,1)S(1)}, u32[]{:S(2)}, u32[]{:S(2)}) async-start(bf16[8,128,512]{2,1,0:T(8,128)(2,1)} %shard_map.59), calls=%async_computation | async-start | bytes 2097152 | tf_op jit(solution)/shard_map/all_to_all | solution.py:289
  21.5 1.6 %collective-permute-start.3 = (bf16[3,64,512]{2,1,0:T(8,128)(2,1)S(1)}, bf16[3,64,512]{2,1,0:T(8,128)(2,1)S(1)}, u32[]{:S(2)}, u32[]{:S(2)}) collective-permute-start(bf16[3,64,512]{2,1,0:T(8,128)(2,1)S(1)} %pad_maximum_fusion.here_ref), channel_id=1, source_target_pairs={{0,8},{8,0},{16,24},{24,16},{32,40},{40,32},{48,56},{56,48},{64,72... | collective-permute-start | bytes 589832 | tf_op jit(solution)/shard_map/ppermute | solution.py:271
  23.1 0.1 stack.40.info_ref
  23.2 1.0 collective-permute-done.3.there_ref
  24.2 0.7 copy-done.2
  24.8 0.9 copy-done.3
  25.8 2.4 %shard_map.60 = (f32[4,64,512]{2,1,0:T(8,128)S(1)}, f32[4,64,512]{2,1,0:T(8,128)S(1)}) custom-call(s32[5]{0:T(128)S(1)} %stack.40.info_ref, bf16[3,64,512]{2,1,0:T(8,128)(2,1)S(1)} %pad_maximum_fusion.here_ref, bf16[3,64,512]{2,1,0:T(8,128)(2,1)S(1)} %copy-done.3, bf16[3,576,512]{2,1,0:T(8,128)(2,1)S(1)} %bitcast.21), custom_call_target="tpu_custom_call" | custom-call | flops 905969664 | bytes 2162708 | tf_op jit(solution)/shard_map/pallas_call | solution.py:228
  28.1 0.8 copy-done.6
  28.9 7.1 %all-to-all-done.mine_ref = bf16[8,128,512]{2,1,0:T(8,128)(2,1)S(1)} async-done(((bf16[8,128,512]{2,1,0:T(8,128)(2,1)}), bf16[8,128,512]{2,1,0:T(8,128)(2,1)S(1)}, u32[]{:S(2)}, u32[]{:S(2)}) %all-to-all-start) | async-done | bytes 1048608 | tf_op jit(solution)/shard_map/all_to_all | solution.py:289
  36.0 1.9 %collective-permute-start.4 = (bf16[8,128,512]{2,1,0:T(8,128)(2,1)S(1)}, bf16[8,128,512]{2,1,0:T(8,128)(2,1)S(1)}, u32[]{:S(2)}, u32[]{:S(2)}) collective-permute-start(bf16[8,128,512]{2,1,0:T(8,128)(2,1)S(1)} %all-to-all-done.mine_ref), channel_id=1, source_target_pairs={{0,8},{8,0},{16,24},{24,16},{32,40},{40,32},{48,56},{56,48},{64,72... | collective-permute-start | bytes 3145736 | tf_op jit(solution)/shard_map/ppermute | solution.py:271
  38.0 0.7 collective-permute-start.5
  38.7 1.5 %collective-permute-done.4.other_ref = bf16[8,128,512]{2,1,0:T(8,128)(2,1)S(1)} collective-permute-done((bf16[8,128,512]{2,1,0:T(8,128)(2,1)S(1)}, bf16[8,128,512]{2,1,0:T(8,128)(2,1)S(1)}, u32[]{:S(2)}, u32[]{:S(2)}) %collective-permute-start.4) | collective-permute-done | bytes 1048608 | tf_op jit(solution)/shard_map/ppermute | solution.py:271
  40.3 0.9 copy-done.4
  41.2 2.6 %shard_map.61 = f32[8,224,128]{2,1,0:T(8,128)S(1)} custom-call(s32[5]{0:T(128)S(1)} %stack.40.info_ref, bf16[8,128,512]{2,1,0:T(8,128)(2,1)S(1)} %all-to-all-done.mine_ref, bf16[8,128,512]{2,1,0:T(8,128)(2,1)S(1)} %collective-permute-done.4.other_ref, bf16[3,64,512]{2,1,0:T(8,128)(2,1)S(1)} %pad_maximum_fusion.here_ref, bf16[3,64,512]{2,1,0:T(8,128)(2,1)S(1)} %copy-done.4), custom_call_target="tpu_custom_call" | custom-call | flops 905969664 | bytes 2490388 | tf_op jit(solution)/shard_map/pallas_call | solution.py:228
  43.8 0.8 convert_element_type.32
  44.6 4.8 %all-to-all-start.1 = ((f16[8,224,128]{2,1,0:T(8,128)(2,1)}), f16[8,224,128]{2,1,0:T(8,128)(2,1)S(1)}, u32[]{:S(2)}, u32[]{:S(2)}) async-start(f16[8,224,128]{2,1,0:T(8,128)(2,1)} %convert_element_type.32), calls=%async_computation.1 | async-start | bytes 917504 | tf_op jit(solution)/shard_map/all_to_all | solution.py:323
  49.4 2.4 %collective-permute-done.5 = f32[4,64,512]{2,1,0:T(8,128)} collective-permute-done((f32[4,64,512]{2,1,0:T(8,128)}, f32[4,64,512]{2,1,0:T(8,128)}, u32[]{:S(2)}, u32[]{:S(2)}) %collective-permute-start.5) | collective-permute-done | bytes 524320 | tf_op jit(solution)/shard_map/ppermute | solution.py:326
  51.9 1.2 %fusion = (f32[64,512]{1,0:T(8,128)S(1)}, f32[64,512]{1,0:T(8,128)S(1)}, f32[64,512]{1,0:T(8,128)S(1)}, f32[64,512]{1,0:T(8,128)S(1)}) fusion(f32[4,64,512]{2,1,0:T(8,128)} %collective-permute-done.5, f32[4,64,512]{2,1,0:T(8,128)S(1)} %get-tuple-element.39), kind=kLoop, calls=%fused_computation.2 | loop fusion | flops 131072 | bytes 1572864 | tf_op jit(solution)/shard_map/add | solution.py:329
  53.0 0.5 collective-permute-start.7
  53.6 5.0 %collective-permute-done.7 = f32[64,512]{1,0:T(8,128)S(1)} collective-permute-done((f32[64,512]{1,0:T(8,128)S(1)}, f32[64,512]{1,0:T(8,128)S(1)}, u32[]{:S(2)}, u32[]{:S(2)}) %collective-permute-start.7) | collective-permute-done | bytes 131104 | tf_op jit(solution)/shard_map/ppermute | solution.py:326
  58.6 7.4 %all-to-all-done.1 = f16[8,224,128]{2,1,0:T(8,128)(2,1)S(1)} async-done(((f16[8,224,128]{2,1,0:T(8,128)(2,1)}), f16[8,224,128]{2,1,0:T(8,128)(2,1)S(1)}, u32[]{:S(2)}, u32[]{:S(2)}) %all-to-all-start.1) | async-done | bytes 458784 | tf_op jit(solution)/shard_map/all_to_all | solution.py:323
  66.1 0.2 shard_map.62
  66.3 0.8 broadcast_in_dim.12
  67.1 4.6 %all-to-all-start.2 = ((f16[8,224,128]{2,1,0:T(8,128)(2,1)}), f16[8,224,128]{2,1,0:T(8,128)(2,1)S(1)}, u32[]{:S(2)}, u32[]{:S(2)}) async-start(f16[8,224,128]{2,1,0:T(8,128)(2,1)} %broadcast_in_dim.12), calls=%async_computation.2 | async-start | bytes 917504 | tf_op jit(solution)/shard_map/all_to_all | solution.py:279
  71.7 1.5 %copy-done.1 = bf16[3,3,3,64,512]{4,3,2,1,0:T(8,128)(2,1)S(1)} copy-done((bf16[3,3,3,64,512]{4,3,2,1,0:T(8,128)(2,1)S(1)}, bf16[3,3,3,64,512]{4,3,2,1,0:T(8,128)(2,1)}, u32[]{:S(2)}) %copy-start.1) | copy-done | bytes 1769496
  73.2 2.7 %shard_map.63 = bf16[64,512]{1,0:T(8,128)(2,1)} custom-call(s32[5]{0:T(128)S(1)} %stack.40.info_ref, bf16[8,128,512]{2,1,0:T(8,128)(2,1)S(1)} %all-to-all-done.mine_ref, bf16[8,128,512]{2,1,0:T(8,128)(2,1)S(1)} %collective-permute-done.4.other_ref, bf16[3,576,512]{2,1,0:T(8,128)(2,1)S(1)} %bitcast.22), custom_call_target="tpu_custom_call" | custom-call | flops 905969664 | bytes 3866644 | tf_op jit(solution)/shard_map/pallas_call | solution.py:228
  75.9 1.5 %collective-permute-done.8 = f32[64,512]{1,0:T(8,128)S(1)} collective-permute-done((f32[64,512]{1,0:T(8,128)S(1)}, f32[64,512]{1,0:T(8,128)S(1)}, u32[]{:S(2)}, u32[]{:S(2)}) %collective-permute-start.8) | collective-permute-done | bytes 131104 | tf_op jit(solution)/shard_map/ppermute | solution.py:326
  77.5 0.7 add_convert_fusion
  78.1 8.7 %all-to-all-done.2 = f16[8,224,128]{2,1,0:T(8,128)(2,1)S(1)} async-done(((f16[8,224,128]{2,1,0:T(8,128)(2,1)}), f16[8,224,128]{2,1,0:T(8,128)(2,1)S(1)}, u32[]{:S(2)}, u32[]{:S(2)}) %all-to-all-start.2) | async-done | bytes 458784 | tf_op jit(solution)/shard_map/all_to_all | solution.py:279
  86.8 0.9 collective-permute-start.9
  87.7 0.1 fusion.4
  87.8 0.1 collective-permute-start.11
  87.9 1.5 %collective-permute-start.10 = (f16[4,224,128]{2,1,0:T(8,128)(2,1)S(1)}, f16[4,224,128]{2,1,0:T(8,128)(2,1)S(1)}, u32[]{:S(2)}, u32[]{:S(2)}) collective-permute-start(f16[4,224,128]{2,1,0:T(8,128)(2,1)S(1)} %get-tuple-element.60), channel_id=1, source_target_pairs={{0,32},{8,40},{16,48},{24,56},{32,64},{40,72},{48,80},{56,88},{64,... | collective-permute-start | bytes 688136 | tf_op jit(solution)/shard_map/ppermute | solution.py:357
  89.4 0.1 convert_element_type.37.refs_1_
  89.5 1.9 %shard_map.64.refs_4_ = f32[3,576,512]{2,1,0:T(8,128)} custom-call(s32[5]{0:T(128)S(1)} %stack.40.info_ref, f32[8,224,128]{2,1,0:T(8,128)S(1)} %convert_element_type.36.refs_0_, f32[8,224,128]{2,1,0:T(8,128)S(1)} %convert_element_type.37.refs_1_), custom_call_target="tpu_custom_call" | custom-call | bytes 1835028 | tf_op jit(solution)/shard_map/pallas_call | solution.py:228
  91.4 3.7 %collective-permute-done.11 = f16[4,224,128]{2,1,0:T(8,128)(2,1)S(1)} collective-permute-done((f16[4,224,128]{2,1,0:T(8,128)(2,1)S(1)}, f16[4,224,128]{2,1,0:T(8,128)(2,1)S(1)}, u32[]{:S(2)}, u32[]{:S(2)}) %collective-permute-start.11) | collective-permute-done | bytes 229408 | tf_op jit(solution)/shard_map/ppermute | solution.py:358
  95.1 1.3 %collective-permute-done.10 = f16[4,224,128]{2,1,0:T(8,128)(2,1)S(1)} collective-permute-done((f16[4,224,128]{2,1,0:T(8,128)(2,1)S(1)}, f16[4,224,128]{2,1,0:T(8,128)(2,1)S(1)}, u32[]{:S(2)}, u32[]{:S(2)}) %collective-permute-start.10) | collective-permute-done | bytes 229408 | tf_op jit(solution)/shard_map/ppermute | solution.py:357
  96.4 0.8 collective-permute-start.12
  97.3 1.0 %collective-permute-done.12 = f16[4,224,128]{2,1,0:T(8,128)(2,1)S(1)} collective-permute-done((f16[4,224,128]{2,1,0:T(8,128)(2,1)S(1)}, f16[4,224,128]{2,1,0:T(8,128)(2,1)S(1)}, u32[]{:S(2)}, u32[]{:S(2)}) %collective-permute-start.12) | collective-permute-done | bytes 229408 | tf_op jit(solution)/shard_map/ppermute | solution.py:271
  98.4 0.3 collective-permute-done.13
  98.7 1.9 %shard_map.65 = f32[3,576,512]{2,1,0:T(8,128)} custom-call(s32[5]{0:T(128)S(1)} %stack.40.info_ref, f32[4,224,128]{2,1,0:T(8,128)S(1)} %convert_element_type.38.refs_0_, f32[4,224,128]{2,1,0:T(8,128)S(1)} %convert_element_type.39.refs_1_, f32[4,224,128]{2,1,0:T(8,128)S(1)} %convert_element_type.40.refs_2_, ...), custom_call_target="tpu_custom_call", output_to_operand_aliasing={{}: (5, {})} | custom-call | bytes 1835028 | tf_op jit(solution)/shard_map/pallas_call | solution.py:228
  (25 shorter events, 0.3 us)
Async XLA Ops:
  0.6 24.2 %copy-start = (bf16[3,3,3,64,512]{4,3,2,1,0:T(8,128)(2,1)S(1)}, bf16[3,3,3,64,512]{4,3,2,1,0:T(8,128)(2,1)}, u32[]{:S(2)}) copy-start(bf16[3,3,3,64,512]{4,3,2,1,0:T(8,128)(2,1)} %param.4) | copy-start | bytes 5308420
  0.6 14.4 %collective-permute-start = (bf16[64,512]{1,0:T(8,128)(2,1)}, bf16[64,512]{1,0:T(8,128)(2,1)S(1)}, u32[]{:S(2)}, u32[]{:S(2)}) collective-permute-start(bf16[64,512]{1,0:T(8,128)(2,1)} %bitcast.23), channel_id=1, source_target_pairs={{0,248},{8,16},{16,8},{24,32},{32,24},{40,48},{48,40},{56,64},{64,... | collective-permute-start | bytes 196616 | tf_op jit(solution)/shard_map/ppermute | solution.py:281
  5.0 10.0 %collective-permute-start.2 = (bf16[64,512]{1,0:T(8,128)(2,1)}, bf16[64,512]{1,0:T(8,128)(2,1)S(1)}, u32[]{:S(2)}, u32[]{:S(2)}) collective-permute-start(bf16[64,512]{1,0:T(8,128)(2,1)} %bitcast.28), channel_id=1, source_target_pairs={{0,16},{8,24},{16,0},{24,8},{32,48},{40,56},{48,32},{56,40},{64,80... | collective-permute-start | bytes 196616 | tf_op jit(solution)/shard_map/ppermute | solution.py:271
  6.4 10.0 %collective-permute-start.1 = (bf16[64,512]{1,0:T(8,128)(2,1)}, bf16[64,512]{1,0:T(8,128)(2,1)S(1)}, u32[]{:S(2)}, u32[]{:S(2)}) collective-permute-start(bf16[64,512]{1,0:T(8,128)(2,1)} %bitcast.29), channel_id=1, source_target_pairs={{0,248},{8,16},{16,8},{24,32},{32,24},{40,48},{48,40},{56,64},{64,... | collective-permute-start | bytes 196616 | tf_op jit(solution)/shard_map/ppermute | solution.py:282
  13.3 0.8 copy-start.5
  14.1 7.3 %copy-start.7 = (bf16[1,64,512]{2,1,0:T(8,128)(2,1)S(1)}, bf16[1,64,512]{2,1,0:T(8,128)(2,1)}, u32[]{:S(2)}) copy-start(bf16[1,64,512]{2,1,0:T(8,128)(2,1)} %param.5) | copy-start | bytes 196612
  17.3 18.7 %all-to-all-start = ((bf16[8,128,512]{2,1,0:T(8,128)(2,1)}), bf16[8,128,512]{2,1,0:T(8,128)(2,1)S(1)}, u32[]{:S(2)}, u32[]{:S(2)}) async-start(bf16[8,128,512]{2,1,0:T(8,128)(2,1)} %shard_map.59), calls=%async_computation | async-start | bytes 2097152 | tf_op jit(solution)/shard_map/all_to_all | solution.py:289
  21.5 2.7 %collective-permute-start.3 = (bf16[3,64,512]{2,1,0:T(8,128)(2,1)S(1)}, bf16[3,64,512]{2,1,0:T(8,128)(2,1)S(1)}, u32[]{:S(2)}, u32[]{:S(2)}) collective-permute-start(bf16[3,64,512]{2,1,0:T(8,128)(2,1)S(1)} %pad_maximum_fusion.here_ref), channel_id=1, source_target_pairs={{0,8},{8,0},{16,24},{24,16},{32,40},{40,32},{48,56},{56,48},{64,72... | collective-permute-start | bytes 589832 | tf_op jit(solution)/shard_map/ppermute | solution.py:271
  24.2 0.7 copy-start.2
  24.8 0.9 copy-start.3
  28.1 0.8 copy-start.6
  36.0 4.2 %collective-permute-start.4 = (bf16[8,128,512]{2,1,0:T(8,128)(2,1)S(1)}, bf16[8,128,512]{2,1,0:T(8,128)(2,1)S(1)}, u32[]{:S(2)}, u32[]{:S(2)}) collective-permute-start(bf16[8,128,512]{2,1,0:T(8,128)(2,1)S(1)} %all-to-all-done.mine_ref), channel_id=1, source_target_pairs={{0,8},{8,0},{16,24},{24,16},{32,40},{40,32},{48,56},{56,48},{64,72... | collective-permute-start | bytes 3145736 | tf_op jit(solution)/shard_map/ppermute | solution.py:271
  38.0 13.9 %collective-permute-start.5 = (f32[4,64,512]{2,1,0:T(8,128)}, f32[4,64,512]{2,1,0:T(8,128)}, u32[]{:S(2)}, u32[]{:S(2)}) collective-permute-start(f32[4,64,512]{2,1,0:T(8,128)} %copy-done.6), channel_id=1, source_target_pairs={{0,1},{1,0},{2,3},{3,2},{4,5},{5,4},{6,7},{7,6},{8,9},{9,8},{10,11... | collective-permute-start | bytes 1572872 | tf_op jit(solution)/shard_map/ppermute | solution.py:326
  40.3 0.9 copy-start.4
  44.6 21.3 %all-to-all-start.1 = ((f16[8,224,128]{2,1,0:T(8,128)(2,1)}), f16[8,224,128]{2,1,0:T(8,128)(2,1)S(1)}, u32[]{:S(2)}, u32[]{:S(2)}) async-start(f16[8,224,128]{2,1,0:T(8,128)(2,1)} %convert_element_type.32), calls=%async_computation.1 | async-start | bytes 917504 | tf_op jit(solution)/shard_map/all_to_all | solution.py:323
  53.0 5.5 %collective-permute-start.7 = (f32[64,512]{1,0:T(8,128)S(1)}, f32[64,512]{1,0:T(8,128)S(1)}, u32[]{:S(2)}, u32[]{:S(2)}) collective-permute-start(f32[64,512]{1,0:T(8,128)S(1)} %get-tuple-element.56), channel_id=1, source_target_pairs={{0,6},{1,7},{2,4},{3,5},{4,2},{5,3},{6,0},{7,1},{8,14},{9,15},{10,... | collective-permute-start | bytes 393224 | tf_op jit(solution)/shard_map/ppermute | solution.py:326
  53.6 5.0 %collective-permute-start.6 = (f32[64,512]{1,0:T(8,128)S(1)}, f32[64,512]{1,0:T(8,128)S(1)}, u32[]{:S(2)}, u32[]{:S(2)}) collective-permute-start(f32[64,512]{1,0:T(8,128)S(1)} %get-tuple-element.57), channel_id=1, source_target_pairs={{0,2},{1,3},{2,0},{3,1},{4,6},{5,7},{6,4},{7,5},{8,10},{9,11},{10,... | collective-permute-start | bytes 393224 | tf_op jit(solution)/shard_map/ppermute | solution.py:326
  67.1 19.7 %all-to-all-start.2 = ((f16[8,224,128]{2,1,0:T(8,128)(2,1)}), f16[8,224,128]{2,1,0:T(8,128)(2,1)S(1)}, u32[]{:S(2)}, u32[]{:S(2)}) async-start(f16[8,224,128]{2,1,0:T(8,128)(2,1)} %broadcast_in_dim.12), calls=%async_computation.2 | async-start | bytes 917504 | tf_op jit(solution)/shard_map/all_to_all | solution.py:279
  71.7 5.8 %collective-permute-start.8 = (f32[64,512]{1,0:T(8,128)S(1)}, f32[64,512]{1,0:T(8,128)S(1)}, u32[]{:S(2)}, u32[]{:S(2)}) collective-permute-start(f32[64,512]{1,0:T(8,128)S(1)} %get-tuple-element.48), channel_id=1, source_target_pairs={{0,4},{1,5},{2,6},{3,7},{4,0},{5,1},{6,2},{7,3},{8,12},{9,13},{10,... | collective-permute-start | bytes 393224 | tf_op jit(solution)/shard_map/ppermute | solution.py:326
  71.7 1.5 %copy-start.1 = (bf16[3,3,3,64,512]{4,3,2,1,0:T(8,128)(2,1)S(1)}, bf16[3,3,3,64,512]{4,3,2,1,0:T(8,128)(2,1)}, u32[]{:S(2)}) copy-start(bf16[3,3,3,64,512]{4,3,2,1,0:T(8,128)(2,1)} %param.4) | copy-start | bytes 5308420
  86.8 2.6 %collective-permute-start.9 = (f16[8,224,128]{2,1,0:T(8,128)(2,1)S(1)}, f16[8,224,128]{2,1,0:T(8,128)(2,1)S(1)}, u32[]{:S(2)}, u32[]{:S(2)}) collective-permute-start(f16[8,224,128]{2,1,0:T(8,128)(2,1)S(1)} %all-to-all-done.2), channel_id=1, source_target_pairs={{0,8},{8,0},{16,24},{24,16},{32,40},{40,32},{48,56},{56,48},{64,72... | collective-permute-start | bytes 1376264 | tf_op jit(solution)/shard_map/ppermute | solution.py:271
  87.8 7.3 %collective-permute-start.11 = (f16[4,224,128]{2,1,0:T(8,128)(2,1)S(1)}, f16[4,224,128]{2,1,0:T(8,128)(2,1)S(1)}, u32[]{:S(2)}, u32[]{:S(2)}) collective-permute-start(f16[4,224,128]{2,1,0:T(8,128)(2,1)S(1)} %get-tuple-element.59), channel_id=1, source_target_pairs={{0,224},{8,232},{16,240},{24,248},{32,0},{40,8},{48,16},{56,24},{6... | collective-permute-start | bytes 688136 | tf_op jit(solution)/shard_map/ppermute | solution.py:358
  87.9 8.5 %collective-permute-start.10 = (f16[4,224,128]{2,1,0:T(8,128)(2,1)S(1)}, f16[4,224,128]{2,1,0:T(8,128)(2,1)S(1)}, u32[]{:S(2)}, u32[]{:S(2)}) collective-permute-start(f16[4,224,128]{2,1,0:T(8,128)(2,1)S(1)} %get-tuple-element.60), channel_id=1, source_target_pairs={{0,32},{8,40},{16,48},{24,56},{32,64},{40,72},{48,80},{56,88},{64,... | collective-permute-start | bytes 688136 | tf_op jit(solution)/shard_map/ppermute | solution.py:357
  96.4 1.9 %collective-permute-start.12 = (f16[4,224,128]{2,1,0:T(8,128)(2,1)S(1)}, f16[4,224,128]{2,1,0:T(8,128)(2,1)S(1)}, u32[]{:S(2)}, u32[]{:S(2)}) collective-permute-start(f16[4,224,128]{2,1,0:T(8,128)(2,1)S(1)} %collective-permute-done.10), channel_id=1, source_target_pairs={{0,8},{8,0},{16,24},{24,16},{32,40},{40,32},{48,56},{56,48},{64,72... | collective-permute-start | bytes 688136 | tf_op jit(solution)/shard_map/ppermute | solution.py:271
  97.2 1.5 %collective-permute-start.13 = (f16[4,224,128]{2,1,0:T(8,128)(2,1)S(1)}, f16[4,224,128]{2,1,0:T(8,128)(2,1)S(1)}, u32[]{:S(2)}, u32[]{:S(2)}) collective-permute-start(f16[4,224,128]{2,1,0:T(8,128)(2,1)S(1)} %collective-permute-done.11), channel_id=1, source_target_pairs={{0,8},{8,0},{16,24},{24,16},{32,40},{40,32},{48,56},{56,48},{64,72... | collective-permute-start | bytes 688136 | tf_op jit(solution)/shard_map/ppermute | solution.py:271
